TPU v7x, 32 devices: a whole 2x2x4 slice. The times are simulated.
32 devices in a mesh: front: 4 (over y, core), row: 4 (over z), col: 2 (over x).
Axes of the slice: x: 2, y: 2, z: 4, core: 2. Of those that a mesh axis runs over, the one named last changes fastest.
Arguments:
- pivot_block: bfloat16 [4, 1024, 1024], P('front'), may hold values from -6 to 6
- border: bfloat16 [4, 8192, 1024], P('front', 'row'), may hold values from -6 to 6
- contrib: bfloat16 [4, 8192, 8192], P('front', 'row', 'col'), may hold values from -6 to 6
- inverses: bfloat16 [4, 4, 256, 256], P('front'), may hold values from -0.0625 to 0.0625
- row_tiles: int32 [4, 64], replicated, may hold values from 0 to 79, as said below
- col_tiles: int32 [4, 64], replicated, may hold values from 0 to 79, as said below
- owner: int32 [80], replicated, may hold values from 0 to 79, as said below
- schur_init: bfloat16 [10240, 10240], P(('front', 'row'), 'col'), may hold values from -6 to 6
- block: bfloat16 [10240, 512], P('col'), may hold values from -0.0625 to 0.0625
Outputs:
- schur: float32 [10240, 10240], P(('front', 'row'), 'col')
- product: float32 [10240, 512], P(('front', 'row', 'col'))
Inputs may be any that keep to these rules, and one draw needn't show every extreme that they name: owner is a permutation of 0 .. 79. For each front the 64 entries are distinct. With s = owner[row_tiles[f, i]], each front has exactly 4 entries in each group s // 5; among the 16 entries of one aligned block of a front at most 2 fall in one group, and that many in some block of every draw. For each front the 64 entries are distinct. With s = owner[col_tiles[f, j]], each front has exactly 32 entries in each group s // 40; among the 32 entries of one aligned block of a front at most 32 fall in one group, and that many in some block of every draw.
All inputs are finite; a program needn't handle non-finite values.
Results may differ from a plain program's by a relative error of at most 0.008.
Values may be sent and summed in bfloat16 or wider, within the bound.
No kernel may reach another device: no remote copies, remote signals or barrier semaphores. Data moves between devices by JAX's collectives and lax.ppermute only.
A program may use at most 256 MiB of HBM per device.

v0:
```python
import jax
import jax.numpy as jnp
from jax import lax
from jax.sharding import PartitionSpec as P

TILE = 128


def eliminate(pivot, rows, inverse_set):
    panels = inverse_set.shape[0]
    width = inverse_set.shape[1]
    pivot_now = pivot.astype(jnp.float32)
    rows_now = rows.astype(jnp.float32)
    leaves = []
    for panel_index in range(panels):
        start = panel_index * width
        left = pivot_now[:, start : start + width].astype(jnp.bfloat16)
        below = jnp.arange(pivot.shape[0])[:, None] >= start + width
        lower = jnp.where(
            below, jnp.dot(left, inverse_set[panel_index], preferred_element_type=jnp.float32), 0.0
        ).astype(jnp.bfloat16)
        side = jnp.dot(
            rows_now[:, start : start + width].astype(jnp.bfloat16),
            inverse_set[panel_index],
            preferred_element_type=jnp.float32,
        ).astype(jnp.bfloat16)
        pivot_now = pivot_now - lax.dot_general(
            lower, lower, (((1,), (1,)), ((), ())), preferred_element_type=jnp.float32
        )
        rows_now = rows_now - lax.dot_general(
            side, lower, (((1,), (1,)), ((), ())), preferred_element_type=jnp.float32
        )
        leaves.append(side)
    return jnp.concatenate(leaves, axis=1)


def route_tables(slots, per_group):
    group = slots // per_group
    within = slots % per_group
    count = slots.shape[-1]
    same = group[..., :, None] == group[..., None, :]
    earlier = jnp.arange(count)[None, :] < jnp.arange(count)[:, None]
    rank = jnp.sum((same & earlier).astype(jnp.int32), axis=-1)
    return (group, rank, within)


def pick_sources(group, rank, n_groups, capacity):
    count = group.shape[-1]
    match = (group[None, None, :] == jnp.arange(n_groups)[:, None, None]) & (
        rank[None, None, :] == jnp.arange(capacity)[None, :, None]
    )
    return jnp.sum(match.astype(jnp.int32) * jnp.arange(count)[None, None, :], axis=-1)


def shards(pivot_block, border, contrib, inverses, row_tiles, col_tiles, owner, schur_init, block):
    n_front = lax.axis_size("front")
    n_row = lax.axis_size("row")
    n_col = lax.axis_size("col")
    front_index = lax.axis_index("front")
    row_index = lax.axis_index("row")
    col_index = lax.axis_index("col")
    groups = n_front * n_row
    tiles_all = row_tiles.shape[1]
    slots_all = owner.shape[0]
    row_span = border.shape[1]
    col_span = contrib.shape[2]
    tile_rows = row_span // TILE
    tile_cols = col_span // TILE
    rows_per_group = slots_all // groups
    cols_per_group = slots_all // n_col
    cap_rows = 2 * tiles_all // (n_row * groups)
    cap_cols = 2 * tiles_all // (n_col * n_col)
    share = row_span // n_col
    own_rows = lax.dynamic_slice_in_dim(border[0], col_index * share, share, 0)
    leaves = eliminate(pivot_block[0], own_rows, inverses[0])
    factor = lax.all_gather(leaves, ("row", "col"), axis=0, tiled=True)
    mine = lax.dynamic_slice_in_dim(factor, row_index * row_span, row_span, 0)
    theirs = lax.dynamic_slice_in_dim(factor, col_index * col_span, col_span, 0)
    update = (
        contrib[0].astype(jnp.float32)
        - lax.dot_general(
            mine, theirs, (((1,), (1,)), ((), ())), preferred_element_type=jnp.float32
        )
    ).astype(jnp.bfloat16)
    tiles = update.reshape(tile_rows, TILE, tile_cols, TILE)
    slot_rows = owner[row_tiles].reshape(n_front, n_row, tile_rows)
    slot_cols = owner[col_tiles].reshape(n_front, n_col, tile_cols)
    group_rows, rank_rows, within_rows = route_tables(slot_rows, rows_per_group)
    group_cols, rank_cols, within_cols = route_tables(slot_cols, cols_per_group)
    send_rows = pick_sources(
        group_rows[front_index, row_index], rank_rows[front_index, row_index], groups, cap_rows
    )
    my_group = front_index * n_row + row_index
    flat_group = group_rows.reshape(groups, tile_rows)
    flat_rank = rank_rows.reshape(groups, tile_rows)
    flat_within = within_rows.reshape(groups, tile_rows)
    hit_rows = (flat_group == my_group)[:, None, :] & (
        flat_rank[:, None, :] == jnp.arange(cap_rows)[None, :, None]
    )
    place_rows = jnp.sum(
        (
            hit_rows[None]
            & (flat_within[None, :, None, :] == jnp.arange(rows_per_group)[:, None, None, None])
        ).astype(jnp.int32),
        axis=-1,
    ).astype(jnp.bfloat16)
    hit_cols = (group_cols == col_index)[:, :, None, :] & (
        rank_cols[:, :, None, :] == jnp.arange(cap_cols)[None, None, :, None]
    )
    place_cols = jnp.sum(
        (
            hit_cols[None]
            & (
                within_cols[None, :, :, None, :]
                == jnp.arange(cols_per_group)[:, None, None, None, None]
            )
        ).astype(jnp.int32),
        axis=-1,
    ).astype(jnp.bfloat16)
    place_cols = jnp.repeat(place_cols, n_row, axis=1)
    send_cols = pick_sources(
        group_cols[front_index, col_index], rank_cols[front_index, col_index], n_col, cap_cols
    )
    by_rows = jnp.take(tiles, send_rows.reshape(-1), axis=0)
    by_both = jnp.take(by_rows, send_cols.reshape(-1), axis=2)
    outgoing = by_both.reshape(groups, cap_rows, TILE, n_col, cap_cols, TILE).transpose(
        0, 3, 1, 4, 2, 5
    )
    outgoing = outgoing.reshape(groups * n_col, cap_rows, cap_cols, TILE, TILE)
    received = lax.all_to_all(
        outgoing, ("front", "row", "col"), split_axis=0, concat_axis=0, tiled=True
    )
    received = received.reshape(groups, n_col, cap_rows, cap_cols, TILE, TILE)
    gathered = jnp.einsum(
        "bgcm,gckmxy->bgkxy", place_cols, received, preferred_element_type=jnp.float32
    ).astype(jnp.bfloat16)
    summed = jnp.einsum("agk,bgkxy->abxy", place_rows, gathered, preferred_element_type=jnp.float32)
    schur = schur_init.astype(jnp.float32) + summed.transpose(0, 2, 1, 3).reshape(
        rows_per_group * TILE, cols_per_group * TILE
    )
    rounded = schur.astype(jnp.bfloat16)
    product = lax.psum_scatter(
        jnp.dot(rounded, block, preferred_element_type=jnp.float32),
        "col",
        scatter_dimension=0,
        tiled=True,
    )
    return (schur, product)


def solution(mesh):
    in_specs = (
        P("front", None, None),
        P("front", "row", None),
        P("front", "row", "col"),
        P("front", None, None, None),
        P(),
        P(),
        P(),
        P(("front", "row"), "col"),
        P("col", None),
    )
    out_specs = (P(("front", "row"), "col"), P(("front", "row", "col"), None))
    return jax.shard_map(shards, mesh=mesh, in_specs=in_specs, out_specs=out_specs, check_vma=False)
```

profile of v0, /device:TPU:0, one launch (start us, length us, event | category | flops | bytes accessed | tf_op | source)
XLA Modules:
  0.0 2108.5 jit_solution(10007459200147742277)
XLA Ops:
  7.3 1.9 dynamic-slice_bitcast_fusion
  9.2 1.2 convolution_convert_fusion.3
  10.5 0.3 fusion.18
  10.8 0.7 convert_subtract_fusion.1
  11.6 0.8 convert_subtract_fusion.2
  12.3 0.4 convolution_convert_fusion.2
  12.7 0.3 fusion.19
  13.0 0.5 copy-done.3
  13.5 2.8 fusion.59
  16.3 0.8 convolution_subtract_fusion
  17.1 2.0 copy-done.4
  19.0 0.3 convolution_convert_fusion.1
  19.4 4.5 fusion.21
  23.9 1.9 convolution_convert_fusion
  25.9 1.5 pad_maximum_fusion
  27.5 2.2 gather_fusion
  29.7 0.6 broadcast_remainder_fusion.1
  30.4 0.5 compare_and_fusion
  31.0 0.4 convert_reduce_fusion.2
  31.5 0.5 copy-done.9
  32.1 0.1 select_reduce_fusion.1
  32.3 0.1 reshape.422
  32.6 1.9 gather_fusion.1
  34.6 0.1 ne.123
  34.7 0.6 broadcast_compare_fusion.1
  35.3 0.3 convert_reduce_fusion.1
  35.7 0.6 copy-done.11
  36.3 0.1 select_reduce_fusion
  36.6 221.0 %all-gather.2.cloned.1.call-done = bf16[8192,1024]{0,1:T(8,128)(2,1)} async-done(((bf16[1024,1024]{0,1:T(8,128)(2,1)}), bf16[8192,1024]{0,1:T(8,128)(2,1)}) %all-gather.2.cloned.1.call-update) | async-done | bytes 16777232 | tf_op jit(solution)/shard_map/all_gather | solution.py:76
  257.6 25.7 %fusion.12 = bf16[256,8,32,128]{3,1,2,0:T(8,128)(2,1)} fusion(bf16[8192,1024]{0,1:T(8,128)(2,1)} %all-gather.2.cloned.1.call-done, s32[]{:T(128)S(6)} %select_n.154, bf16[1,2048,4096]{2,1,0:T(8,128)(2,1)} %param.11, s32[]{:T(128)S(6)} %select_n.153), kind=kOutput, calls=%fused_computation.17 | convolution fusion | flops 17205035008 | bytes 46137352 | tf_op jit(solution)/shard_map/dot_general | solution.py:81
  283.3 15.1 copy.36
  298.3 18.8 gather_fusion.2
  317.1 22.8 %broadcast_select_fusion = bf16[32,128,32,128]{3,2,1,0:T(8,128)(2,1)} fusion(bf16[32,128,32,128]{3,2,1,0:T(8,128)(2,1)} %gather_fusion.2, pred[32]{0:T(512)(128)(4,1)S(1)} %compare_and_fusion.1), kind=kLoop, calls=%fused_computation.13 | loop fusion | flops 16777216 | bytes 67108896 | tf_op jit(solution)/shard_map/jit(_take)/select_n | solution.py:124
  339.9 23.4 %copy.24 = bf16[32,128,32,128]{3,1,0,2:T(8,128)(2,1)} copy(bf16[32,128,32,128]{3,2,1,0:T(8,128)(2,1)} %broadcast_select_fusion) | data formatting | bytes 67108864 | tf_op jit(solution)/shard_map/jit(_take)/select_n | solution.py:124
  363.3 35.9 %gather_fusion.3 = bf16[64,32,128,128]{3,2,1,0:T(8,128)(2,1)} fusion(bf16[32,128,32,128]{3,1,0,2:T(8,128)(2,1)} %copy.24, s32[1024]{0:T(1024)S(1)} %pad_clamp_fusion), kind=kCustom, calls=%fused_computation.3 | custom fusion | bytes 134217984 | tf_op jit(solution)/shard_map/jit(_take)/gather | solution.py:125
  399.2 44.4 %copy_select_fusion = bf16[16,2,128,2,32,128]{5,2,4,1,3,0:T(8,128)(2,1)} fusion(bf16[16,2,128,2,32,128]{5,2,1,0,4,3:T(8,128)(2,1)} %bitcast.16, pred[2,32]{1,0:T(4,128)(4,1)S(1)} %compare_and_fusion.2), kind=kLoop, calls=%fused_computation.7 | loop fusion | flops 33554432 | bytes 134217792 | tf_op jit(solution)/shard_map/jit(_take)/select_n | solution.py:125
  443.7 5.1 all-to-all-start
  448.9 0.1 iota_compare_fusion
  449.1 2.0 convert_reduce_fusion
  451.4 0.3 convert_reduce_fusion.3
  451.6 1442.9 %all-to-all-done = bf16[32,2,32,128,128]{4,3,2,1,0:T(8,128)(2,1)} async-done(((bf16[32,2,32,128,128]{4,3,2,1,0:T(8,128)(2,1)}), bf16[32,2,32,128,128]{4,3,2,1,0:T(8,128)(2,1)}, u32[]{:S(2)}, u32[]{:S(2)}) %all-to-all-start) | async-done | bytes 67108896 | tf_op jit(solution)/shard_map/all_to_all | solution.py:130
  1894.6 66.8 %fusion.2 = bf16[40,16,2,128,128]{4,0,3,2,1:T(8,128)(2,1)} fusion(bf16[40,16,2,32,1,1]{0,3,2,5,4,1:T(8,128)(2,1)S(1)} %bitcast.89, bf16[16,2,2,32,128,128]{5,4,3,2,1,0:T(8,128)(2,1)} %bitcast.19), kind=kOutput, calls=%fused_computation.8 | convolution fusion | flops 2705326080 | bytes 109133824 | tf_op jit(solution)/shard_map/bgcm,gckmxy->bgkxy/dot_general | solution.py:134
  1961.4 34.2 %fusion.8 = f32[5,128,40,128]{3,0,1,2:T(8,128)} fusion(bf16[40,16,2,128,128]{4,0,3,2,1:T(8,128)(2,1)} %fusion.2, bf16[5,16,2,1,1]{1,2,0,4,3:T(2,128)(2,1)S(1)} %convert_bitcast_fusion), kind=kOutput, calls=%fused_computation.15 | convolution fusion | flops 209715200 | bytes 55050560 | tf_op jit(solution)/shard_map/agk,bgkxy->abxy/dot_general | solution.py:137
  1995.6 9.8 copy.29
  2005.5 6.0 bitcast_add_fusion
  2011.4 4.9 copy-done.2
  2016.4 4.6 fusion.15
  2021.0 80.4 %reduce-scatter.2.cloned.1.call-done = f32[320,512]{1,0:T(8,128)} async-done(((f32[640,512]{1,0:T(8,128)}), f32[320,512]{1,0:T(8,128)}) %reduce-scatter.2.cloned.1.call-update) | async-done | bytes 655376 | tf_op jit(solution)/shard_map/reduce_scatter | solution.py:142
  (90 shorter events, 1.5 us)
Async XLA Ops:
  7.2 20.4 copy-start
  7.2 3.3 copy-start.6
  7.2 3.3 copy-start.5
  7.2 250.4 %all-gather.2.cloned.1.call-start = ((), (), s32[]{:S(2)}) async-start(), calls=%async_computation.2 | async-start | bytes 18874368 | tf_op jit(solution)/shard_map/all_gather | solution.py:76
  11.6 2.0 copy-start.3
  17.1 2.0 copy-start.4
  23.9 3.5 copy-start.18
  23.9 3.5 copy-start.19
  30.3 253.0 %copy-start.13 = (s32[256]{0:T(256)}, s32[256]{0:T(256)S(1)}, u32[]{:S(2)}) copy-start(s32[256]{0:T(256)S(1)} %get-tuple-element.7) | copy-start | bytes 3076
  31.5 0.6 copy-start.9
  34.5 248.7 %copy-start.7 = (s32[4,2,32]{2,1,0:T(2,128)}, s32[4,2,32]{2,1,0:T(2,128)S(1)}, u32[]{:S(2)}) copy-start(s32[4,2,32]{2,1,0:T(2,128)S(1)} %rem.73) | copy-start | bytes 3076
  35.7 0.6 copy-start.11
  443.6 5.2 copy-start.14
  443.6 5.3 copy-start.8
  443.6 5.4 copy-start.12
  443.6 5.4 copy-start.15
  443.6 7.5 copy-start.16
  443.7 7.6 copy-start.17
  443.7 7.7 copy-start.10
  443.7 1450.9 %all-to-all-start = ((bf16[32,2,32,128,128]{4,3,2,1,0:T(8,128)(2,1)}), bf16[32,2,32,128,128]{4,3,2,1,0:T(8,128)(2,1)}, u32[]{:S(2)}, u32[]{:S(2)}) async-start(bf16[32,2,32,128,128]{4,3,2,1,0:T(8,128)(2,1)} %bitcast.18), calls=%async_computation | async-start | bytes 134217728 | tf_op jit(solution)/shard_map/all_to_all | solution.py:130
  448.8 1652.7 %reduce-scatter.2.cloned.1.call-start = ((), (), s32[]{:S(2)}) async-start(), calls=%async_computation.3 | async-start | bytes 1966080 | tf_op jit(solution)/shard_map/reduce_scatter | solution.py:142
  1961.4 55.0 %slice-start = ((s8[5242880]{0:T(1024)(128)(4,1)}), s8[1048576]{0:T(1024)(128)(4,1)S(1)}, s32[]{:S(2)}) async-start(s8[5242880]{0:T(1024)(128)(4,1)} %bitcast.91), calls=%async_computation.4 | async-start | bytes 2097152
  1995.6 20.7 slice-start.1
  2011.4 5.0 copy-start.2
  2016.4 85.1 %copy-start.1 = (s32[80]{0:T(128)S(1)}, s32[80]{0:T(128)}, u32[]{:S(2)}) copy-start(s32[80]{0:T(128)} %param.15) | copy-start | bytes 964
Sparse Core Ops, SparseCore 0:
  27.5 230.0 all-gather.1
  2021.1 80.2 reduce-scatter.1
where the time goes:
time: 2110 us
  waiting for transfers between devices  1740 us (82%)
  matrix products  145 us (7%)
  local copies, waits for them, and re-layouts  119 us (6%)
  other arithmetic  80 us (4%)
    all_to_all x1, waiting for transfers between devices, shards(): lax.all_to_all(outgoing, ('front', 'row', 'col'), split_axis=0, concat_ax...  1440 us
    all_gather x1, waiting for transfers between devices, shards(): factor = lax.all_gather(leaves, ('row', 'col'), axis=0, tiled=True)  221 us
    reduce_scatter x1, waiting for transfers between devices, shards(): lax.psum_scatter(jnp.dot(rounded, block, preferred_element_type=jnp.float...  80.4 us
    dot_general x1, matrix products, shards(): jnp.einsum('bgcm,gckmxy->bgkxy', place_cols, received, preferred_element_...  66.8 us
    select_n x2, other arithmetic, shards(): by_both = jnp.take(by_rows, send_cols.reshape(-1), axis=2)  44.4 us
  transfers between devices with their start and end apart: 3, of which 3 were waited for; matrix products, arithmetic and copies ran while one was open for 0% of the time, Pallas kernels for 0%

commit v1 on v0

v1 whole, which is shorter than its diff:
```python
import jax
import jax.numpy as jnp
from jax import lax
from jax.experimental import pallas as pl
from jax.experimental.pallas import tpu as pltpu
from jax.sharding import PartitionSpec as P

TILE = 128
CHUNKS = 4
ADJACENT = 8
FR = ("front", "row")


def eliminate(pivot, rows, inverse_set):
    panels = inverse_set.shape[0]
    width = inverse_set.shape[1]
    pivot_now = pivot.astype(jnp.float32)
    rows_now = rows.astype(jnp.float32)
    leaves = []
    for panel_index in range(panels):
        start = panel_index * width
        left = pivot_now[:, start : start + width].astype(jnp.bfloat16)
        below = jnp.arange(pivot.shape[0])[:, None] >= start + width
        lower = jnp.where(
            below, jnp.dot(left, inverse_set[panel_index], preferred_element_type=jnp.float32), 0.0
        ).astype(jnp.bfloat16)
        side = jnp.dot(
            rows_now[:, start : start + width].astype(jnp.bfloat16),
            inverse_set[panel_index],
            preferred_element_type=jnp.float32,
        ).astype(jnp.bfloat16)
        pivot_now = pivot_now - lax.dot_general(
            lower, lower, (((1,), (1,)), ((), ())), preferred_element_type=jnp.float32
        )
        rows_now = rows_now - lax.dot_general(
            side, lower, (((1,), (1,)), ((), ())), preferred_element_type=jnp.float32
        )
        leaves.append(side)
    return jnp.concatenate(leaves, axis=1)


def count(mask, axis=-1):
    return jnp.sum(mask.astype(jnp.int32), axis=axis)


def earlier(n):
    return jnp.arange(n)[None, :] < jnp.arange(n)[:, None]


def row_plan(slot_rows, per_group, groups, adjacent):
    sources, tile_rows = slot_rows.shape
    target = slot_rows // per_group
    within = slot_rows % per_group
    same = target[:, :, None] == target[:, None, :]
    rank = count(same & earlier(tile_rows)[None])
    extra = rank > 0
    key = target * tile_rows + rank
    extra_order = count(extra[:, None, :] & (key[:, None, :] < key[:, :, None]))
    empty = count(target[:, None, :] == jnp.arange(groups)[None, :, None]) == 0
    empty_order = count(empty[:, None, :] & earlier(groups)[None])
    lands = jnp.where(
        extra[:, None, :],
        empty[:, :, None] & (empty_order[:, :, None] == extra_order[:, None, :]),
        target[:, None, :] == jnp.arange(groups)[None, :, None],
    ).astype(jnp.int32)
    source_row = jnp.sum(lands * jnp.arange(tile_rows), axis=-1)
    to_group = jnp.sum(lands * target[:, None, :], axis=-1)
    to_within = jnp.sum(lands * within[:, None, :], axis=-1)
    here = jnp.arange(groups)[None, :]
    astray = to_group != here
    order = count(
        (to_group[:, None, :] == to_group[None, :, :])
        & astray[None]
        & earlier(sources)[:, :, None],
        axis=1,
    )
    near = astray & (to_group == (here ^ 1)) & (order < adjacent)
    far = astray & ~near
    far_round = jnp.where(to_group == (here ^ 1), order - adjacent, order)
    rounds = jnp.max(jnp.where(far, far_round + 1, 0))
    flat_group = to_group.T.reshape(-1)
    flat_far = far.T.reshape(-1)
    total = flat_group.shape[0]
    far_place = count(
        (flat_group[None, :] == flat_group[:, None]) & flat_far[None, :] & earlier(total)
    ).reshape(groups, sources).T
    return dict(
        source_row=source_row,
        to_group=to_group,
        to_within=to_within,
        order=order,
        near=near,
        far=far,
        far_round=far_round,
        far_place=far_place,
        astray=astray,
        rounds=rounds,
    )


def unwritten(shape, dtype):
    return pl.pallas_call(
        lambda out: None,
        out_shape=jax.ShapeDtypeStruct(shape, dtype),
        out_specs=pl.BlockSpec(memory_space=pl.ANY),
    )()


def update_kernel(parts, scalars, *refs):
    left = refs[:parts]
    right = refs[parts]
    old = refs[parts + 1 : 2 * parts + 1]
    out = refs[2 * parts + 1]
    lhs = jnp.concatenate([part[0] for part in left], axis=0)
    change = lax.dot_general(
        lhs, right[...], (((1,), (1,)), ((), ())), preferred_element_type=jnp.float32
    )
    for part in range(parts):
        new = old[part][...].astype(jnp.float32) - change[part * TILE : (part + 1) * TILE]
        out[part] = new.astype(out.dtype)


def update_chunk(factor, contrib, scalars, chunk, width, groups):
    parts = 4 if groups % 4 == 0 else 1
    depth = factor.shape[1]
    block = min(width, 1024)
    steps = width // block
    tiles = factor.reshape(-1, TILE, depth)
    left_specs = [
        pl.BlockSpec(
            (1, TILE, depth),
            lambda n, m, s, part=part: (s[groups] + s[m * parts + part], 0, 0),
        )
        for part in range(parts)
    ]
    right_spec = pl.BlockSpec(
        (block, depth), lambda n, m, s: (s[groups + 1] + chunk * steps + n, 0)
    )
    old_specs = [
        pl.BlockSpec(
            (TILE, block), lambda n, m, s, part=part: (s[m * parts + part], chunk * steps + n)
        )
        for part in range(parts)
    ]
    return pl.pallas_call(
        lambda *refs: update_kernel(parts, *refs),
        out_shape=jax.ShapeDtypeStruct((groups, TILE, width), contrib.dtype),
        grid_spec=pltpu.PrefetchScalarGridSpec(
            num_scalar_prefetch=1,
            grid=(steps, groups // parts),
            in_specs=left_specs + [right_spec] + old_specs,
            out_specs=pl.BlockSpec((parts, TILE, block), lambda n, m, s: (m, 0, n)),
        ),
        name="update",
    )(scalars, *([tiles] * parts), factor, *([contrib] * parts))


def assemble(row_code, col_code, has_cross, recv, near, far, cross_recv, cross_near, init, block):
    fronts, per_rows = row_code.shape
    per_cols = col_code.shape[1]
    chunks = len(recv)
    width = recv[0].shape[2]
    span = chunks * width
    cross_span = cross_recv.shape[2]
    vectors = block.shape[1]
    cap = recv[0].shape[0]
    scalars = jnp.concatenate(
        [row_code.reshape(-1), col_code.reshape(-1), has_cross.astype(jnp.int32).reshape(1)]
    )
    col_base = fronts * per_rows
    flag = col_base + fronts * per_cols

    def kernel(s, *refs):
        recv_refs = refs[:chunks]
        near_refs = refs[chunks : 2 * chunks]
        far_ref, cross_recv_ref, cross_near_ref, init_ref, block_ref = refs[
            2 * chunks : 2 * chunks + 5
        ]
        schur_ref, product_ref = refs[2 * chunks + 5 : 2 * chunks + 7]
        held, rounded, sems = refs[2 * chunks + 7 :]
        step = pl.program_id(0)

        def moves(b, act):
            slot = b % 2
            for f in range(fronts):
                code = s[f * per_rows + b]
                index = code % cap

                def go(source, place, lanes, which):
                    act(
                        pltpu.make_async_copy(
                            source.at[index],
                            held.at[slot, f, :, pl.ds(place, lanes)],
                            sems.at[slot, f, which],
                        )
                    )

                @pl.when((code >= 0) & (code < cap))
                def _():
                    for chunk in range(chunks):
                        go(recv_refs[chunk], chunk * width, width, chunk)

                    @pl.when(s[flag] > 0)
                    def _():
                        go(cross_recv_ref, span, cross_span, chunks)

                @pl.when((code >= cap) & (code < 2 * cap))
                def _():
                    for chunk in range(chunks):
                        go(near_refs[chunk], chunk * width, width, chunk)

                    @pl.when(s[flag] > 0)
                    def _():
                        go(cross_near_ref, span, cross_span, chunks)

                @pl.when(code >= 2 * cap)
                def _():
                    go(far_ref, 0, span + cross_span, chunks)

        @pl.when(step == 0)
        def _():
            moves(step, lambda copy: copy.start())

        @pl.when(step + 1 < per_rows)
        def _():
            moves(step + 1, lambda copy: copy.start())

        moves(step, lambda copy: copy.wait())
        slot = step % 2

        def column(c, carry):
            lanes = pl.ds(pl.multiple_of(c * TILE, TILE), TILE)
            total = init_ref[:, lanes].astype(jnp.float32)
            for f in range(fronts):
                code = s[col_base + f * per_cols + c]
                used = (code >= 0) & (s[f * per_rows + step] >= 0)
                place = pl.multiple_of(jnp.maximum(code, 0) * TILE, TILE)
                piece = held[slot, f, :, pl.ds(place, TILE)].astype(jnp.float32)
                total = total + jnp.where(used, piece, 0.0)
            schur_ref[:, lanes] = total
            rounded[:, lanes] = total.astype(jnp.bfloat16)
            return carry

        lax.fori_loop(0, per_cols, column, 0, unroll=4 if per_cols % 4 == 0 else 1)
        product_ref[...] = jnp.dot(
            rounded[...], block_ref[...], preferred_element_type=jnp.float32
        )

    anywhere = pl.BlockSpec(memory_space=pl.ANY)
    wide = per_cols * TILE
    return pl.pallas_call(
        kernel,
        out_shape=(
            jax.ShapeDtypeStruct((per_rows * TILE, wide), jnp.float32),
            jax.ShapeDtypeStruct((per_rows * TILE, vectors), jnp.float32),
        ),
        grid_spec=pltpu.PrefetchScalarGridSpec(
            num_scalar_prefetch=1,
            grid=(per_rows,),
            in_specs=[anywhere] * (2 * chunks + 3)
            + [
                pl.BlockSpec((TILE, wide), lambda b, s: (b, 0)),
                pl.BlockSpec((wide, vectors), lambda b, s: (0, 0)),
            ],
            out_specs=[
                pl.BlockSpec((TILE, wide), lambda b, s: (b, 0)),
                pl.BlockSpec((TILE, vectors), lambda b, s: (b, 0)),
            ],
            scratch_shapes=[
                pltpu.VMEM((2, fronts, TILE, span + cross_span), jnp.bfloat16),
                pltpu.VMEM((TILE, wide), jnp.bfloat16),
                pltpu.SemaphoreType.DMA((2, fronts, chunks + 1)),
            ],
        ),
        name="assemble",
    )(scalars, *recv, *near, far, cross_recv, cross_near, init, block)


def shards(pivot_block, border, contrib, inverses, row_tiles, col_tiles, owner, schur_init, block):
    n_front = lax.axis_size("front")
    n_row = lax.axis_size("row")
    n_col = lax.axis_size("col")
    front_index = lax.axis_index("front")
    row_index = lax.axis_index("row")
    col_index = lax.axis_index("col")
    groups = n_front * n_row
    tiles_all = row_tiles.shape[1]
    slots_all = owner.shape[0]
    row_span = border.shape[1]
    col_span = contrib.shape[2]
    tile_rows = row_span // TILE
    tile_cols = col_span // TILE
    rows_per_group = slots_all // groups
    cols_per_group = slots_all // n_col
    share = row_span // n_col
    chunks = CHUNKS if tile_cols % CHUNKS == 0 else 1
    width = col_span // chunks
    me = front_index * n_row + row_index

    own_rows = lax.dynamic_slice_in_dim(border[0], col_index * share, share, 0)
    leaves = eliminate(pivot_block[0], own_rows, inverses[0])
    factor = lax.all_gather(leaves, ("row", "col"), axis=0, tiled=True)

    slot_rows = owner[row_tiles].reshape(groups, tile_rows)
    plan = row_plan(slot_rows, rows_per_group, groups, ADJACENT)
    held = lambda table: lax.dynamic_index_in_dim(table, me, 1, keepdims=False)
    my_group = held(plan["to_group"])
    my_order = held(plan["order"])
    near_index = jnp.sum(
        (held(plan["near"])[None, :] & (my_order[None, :] == jnp.arange(ADJACENT)[:, None])).astype(
            jnp.int32
        )
        * jnp.arange(groups),
        axis=-1,
    )
    for_me = plan["to_group"] == me
    code = jnp.where(
        ~plan["astray"],
        jnp.arange(groups)[:, None],
        jnp.where(plan["near"], groups + plan["order"], 2 * groups + plan["far_place"]),
    )
    hit = for_me[:, :, None] & (plan["to_within"][:, :, None] == jnp.arange(rows_per_group))
    row_code = (
        jnp.sum(
            jnp.where(hit, code[:, :, None] + 1, 0).reshape(
                n_front, n_row * groups, rows_per_group
            ),
            axis=1,
        )
        - 1
    )

    slot_cols = owner[col_tiles].reshape(n_front, n_col, tile_cols)
    to_col = slot_cols // cols_per_group
    within_col = slot_cols % cols_per_group
    crossing = to_col != jnp.arange(n_col)[None, :, None]
    cross_order = count(
        (to_col[..., :, None] == to_col[..., None, :]) & earlier(tile_cols)[None, None]
    )
    cross_rounds = jnp.max(jnp.where(crossing, cross_order + 1, 0))
    flat_to = to_col.reshape(n_front, -1)
    flat_cross = crossing.reshape(n_front, -1)
    cross_place = count(
        (flat_to[:, :, None] == flat_to[:, None, :])
        & flat_cross[:, None, :]
        & earlier(n_col * tile_cols)[None]
    ).reshape(n_front, n_col, tile_cols)
    col_place = jnp.where(crossing, tile_cols + cross_place, jnp.arange(tile_cols))
    col_hit = (to_col == col_index)[..., None] & (
        within_col[..., None] == jnp.arange(cols_per_group)
    )
    col_code = jnp.sum(jnp.where(col_hit, col_place[..., None] + 1, 0), axis=(1, 2)) - 1
    my_to = to_col[front_index]
    my_cross_order = cross_order[front_index]
    my_cross_place = cross_place[front_index]

    scalars = jnp.concatenate(
        [
            lax.dynamic_index_in_dim(plan["source_row"], me, 0, keepdims=False),
            jnp.stack([row_index * tile_rows, col_index * (col_span // min(width, 1024))]),
        ]
    ).astype(jnp.int32)
    neighbours = [(g, g ^ 1) for g in range(groups)]

    def settle(received):
        picked = jnp.take(received, near_index, axis=0)
        return lax.ppermute(picked, FR, neighbours)

    sent, recv, near = [], [], []
    for chunk in range(chunks):
        piece = update_chunk(factor, contrib[0], scalars, chunk, width, groups)
        sent.append(piece)
        recv.append(lax.all_to_all(piece, FR, split_axis=0, concat_axis=0, tiled=True))
    for chunk in range(chunks):
        near.append(settle(recv[chunk]))

    cross_span = (tile_cols + 1) * TILE

    def cross_round(state):
        turn, buffer = state
        picks = []
        for other in range(n_col):
            chosen = (my_to[col_index] == other) & (my_cross_order[col_index] == turn)
            column = jnp.sum(chosen.astype(jnp.int32) * jnp.arange(tile_cols))
            pick = None
            for chunk in range(chunks):
                local = column - chunk * (width // TILE)
                inside = (local >= 0) & (local < width // TILE)
                part = lax.dynamic_slice_in_dim(
                    sent[chunk], jnp.clip(local, 0, width // TILE - 1) * TILE, TILE, 2
                )
                pick = part if pick is None else jnp.where(inside, part, pick)
            picks.append(pick)
        arrived = lax.all_to_all(jnp.stack(picks), "col", split_axis=0, concat_axis=0, tiled=True)
        for other in range(n_col):
            chosen = (
                (my_to[other] == col_index) & (my_cross_order[other] == turn) & (other != col_index)
            )
            place = jnp.where(
                jnp.any(chosen),
                jnp.sum(jnp.where(chosen, my_cross_place[other], 0)),
                tile_cols,
            )
            buffer = lax.dynamic_update_slice_in_dim(buffer, arrived[other], place * TILE, 2)
        return (turn + 1, buffer)

    crossed = unwritten((groups, TILE, cross_span), contrib.dtype)
    _, crossed = lax.while_loop(
        lambda state: state[0] < cross_rounds, cross_round, (jnp.int32(0), crossed)
    )

    def cross_exchange(state):
        received = lax.all_to_all(crossed, FR, split_axis=0, concat_axis=0, tiled=True)
        return (state[0] + 1, received, settle(received))

    _, cross_recv, cross_near = lax.while_loop(
        lambda state: state[0] < jnp.minimum(cross_rounds, 1),
        cross_exchange,
        (
            jnp.int32(0),
            unwritten((groups, TILE, cross_span), contrib.dtype),
            unwritten((ADJACENT, TILE, cross_span), contrib.dtype),
        ),
    )

    my_far = held(plan["far"])
    my_far_round = held(plan["far_round"])

    def far_exchange(state):
        turn, buffer = state
        chosen = (
            my_far[None, :]
            & (my_far_round[None, :] == turn)
            & (my_group[None, :] == jnp.arange(groups)[:, None])
        )
        index = jnp.sum(chosen.astype(jnp.int32) * jnp.arange(groups), axis=-1)
        rows = jnp.concatenate(
            [jnp.take(part, index, axis=0) for part in recv + [cross_recv]], axis=2
        )
        arrived = lax.all_to_all(rows, FR, split_axis=0, concat_axis=0, tiled=True)
        coming = plan["far"] & for_me & (plan["far_round"] == turn)
        place = jnp.where(
            jnp.any(coming, axis=0),
            jnp.sum(jnp.where(coming, plan["far_place"], 0), axis=0),
            groups,
        )
        for holder in range(groups):
            buffer = lax.dynamic_update_slice_in_dim(
                buffer, arrived[holder : holder + 1], place[holder], 0
            )
        return (turn + 1, buffer)

    far = unwritten((groups + 1, TILE, col_span + cross_span), contrib.dtype)
    _, far = lax.while_loop(
        lambda state: state[0] < plan["rounds"], far_exchange, (jnp.int32(0), far)
    )

    schur, partial = assemble(
        row_code,
        col_code,
        cross_rounds > 0,
        recv,
        near,
        far,
        cross_recv,
        cross_near,
        schur_init,
        block,
    )
    if n_col == 2:
        part = partial.shape[0] // n_col
        keep = lax.dynamic_slice_in_dim(partial, col_index * part, part, 0)
        give = lax.dynamic_slice_in_dim(partial, (1 - col_index) * part, part, 0)
        product = keep + lax.ppermute(give, "col", [(0, 1), (1, 0)])
    else:
        product = lax.psum_scatter(partial, "col", scatter_dimension=0, tiled=True)
    return (schur, product)


def solution(mesh):
    in_specs = (
        P("front", None, None),
        P("front", "row", None),
        P("front", "row", "col"),
        P("front", None, None, None),
        P(),
        P(),
        P(),
        P(("front", "row"), "col"),
        P("col", None),
    )
    out_specs = (P(("front", "row"), "col"), P(("front", "row", "col"), None))
    return jax.shard_map(shards, mesh=mesh, in_specs=in_specs, out_specs=out_specs, check_vma=False)
```

time: 2110 us -> 1210 us (0.57)
  waiting for transfers between devices: 1740 us -> 651 us
  blocking collectives: 0 us -> 393 us
  matrix products: 145 us -> 13 us
  local copies, waits for them, and re-layouts: 119 us -> 42 us
  Pallas kernels: 0 us -> 62.1 us
  other arithmetic: 80 us -> 18.3 us
    all_to_all x1, waiting for transfers between devices: 1440 us -> 344 us  [cross_exchange(): lax.all_to_all(crossed, FR, split_axis=0, concat_axis=0, tiled=True)]
    all_to_all x0 -> x4, blocking collectives: none -> 393 us  [shards(): lax.all_to_all(piece, FR, split_axis=0, concat_axis=0, tiled=True)]
    dot_general x4 -> x0, matrix products: 131 us -> none  [the longest x1 66.8 us: shards(): jnp.einsum('bgcm,gckmxy->bgkxy', place_cols, received, preferred_element_...]
    ppermute x0 -> x5, waiting for transfers between devices: none -> 90.4 us  [the longest x4 74.7 us: settle(): return lax.ppermute(picked, FR, neighbours)]
    reduce_scatter x1 -> x0, waiting for transfers between devices: 80.4 us -> none  [shards(): lax.psum_scatter(jnp.dot(rounded, block, preferred_element_type=jnp.float...]
    pallas_call x0 -> x9, Pallas kernels: none -> 62.1 us  [the longest x4 41 us: update_chunk(): pl.pallas_call(lambda *refs: update_kernel(parts, *refs), out_shape=jax.S...]
    select_n x7 -> x5, other arithmetic: 67.2 us -> 6.41 us  [the longest x3 6.39 us: settle(): picked = jnp.take(received, near_index, axis=0)]
    gather x3 -> x6, local copies, waits for them, and re-layouts: 56.8 us -> 28.3 us  [the longest x5 26.4 us: settle(): picked = jnp.take(received, near_index, axis=0)]
  transfers between devices with their start and end apart: 3 -> 7, of which waited for: 3 -> 5; matrix products, arithmetic and copies ran while one was open for 0% -> 4% of each run, Pallas kernels for 0% -> 0%
where the time goes in v1:
time: 1210 us
  waiting for transfers between devices  651 us (54%)
  blocking collectives  393 us (32%)
  Pallas kernels  62.1 us (5%)
  local copies, waits for them, and re-layouts  42 us (3%)
  other arithmetic  18.3 us (2%)
  between operations  15.2 us (1%)
  matrix products  13 us (1%)
    all_to_all x4, blocking collectives, shards(): lax.all_to_all(piece, FR, split_axis=0, concat_axis=0, tiled=True)  393 us
    all_to_all x1, waiting for transfers between devices, cross_exchange(): lax.all_to_all(crossed, FR, split_axis=0, concat_axis=0, tiled=True)  344 us
    all_gather x1, waiting for transfers between devices, shards(): factor = lax.all_gather(leaves, ('row', 'col'), axis=0, tiled=True)  216 us
    ppermute x4, waiting for transfers between devices, settle(): return lax.ppermute(picked, FR, neighbours)  74.7 us
    pallas_call x4, Pallas kernels, update_chunk(): pl.pallas_call(lambda *refs: update_kernel(parts, *refs), out_shape=jax.S...  41 us
    gather x5, local copies, waits for them, and re-layouts, settle(): picked = jnp.take(received, near_index, axis=0)  26.4 us
  transfers between devices with their start and end apart: 7, of which 5 were waited for; matrix products, arithmetic and copies ran while one was open for 4% of the time, Pallas kernels for 0%

profile of v1, /device:TPU:0, one launch (start us, length us, event | category | flops | bytes accessed | tf_op | source)
XLA Modules:
  0.0 1206.3 jit_solution(7114994224470894518)
XLA Ops:
  7.3 1.9 dynamic-slice_bitcast_fusion
  9.9 0.7 convert_subtract_fusion
  10.7 0.8 convert_subtract_fusion.1
  11.7 0.8 copy-done.8
  12.9 2.8 fusion.53
  15.6 0.8 convolution_subtract_fusion
  16.5 2.0 copy-done.9
  18.8 4.5 fusion.9
  23.3 1.9 convolution_convert_fusion
  25.1 1.6 pad_maximum_fusion.1
  26.9 2.0 gather_fusion.6
  29.2 1.9 gather_fusion.5
  32.7 0.6 fusion.47
  34.1 0.7 convert_reduce_fusion.6
  35.6 1.6 select_reduce_fusion.4
  37.2 0.6 pad_add_fusion.1.refs_0_
  38.9 0.6 fusion.44
  39.5 1.2 select_add_fusion.1
  40.7 216.3 %all-gather.2.cloned.1.call-done.refs_5_ = bf16[8192,1024]{1,0:T(8,128)(2,1)} async-done(((bf16[1024,1024]{1,0:T(8,128)(2,1)}), bf16[8192,1024]{1,0:T(8,128)(2,1)}) %all-gather.2.cloned.1.call-update) | async-done | bytes 16777232 | tf_op jit(solution)/shard_map/all_gather | solution.py:302
  256.9 10.2 update.7
  267.2 10.2 update.6
  277.4 10.3 update.5
  287.7 10.2 update.4
  298.0 0.6 while.40
  298.6 99.2 %all_to_all.45.refs_3_ = bf16[16,128,1024]{2,1,0:T(8,128)(2,1)} all-to-all(bf16[16,128,1024]{2,1,0:T(8,128)(2,1)} %get-tuple-element.1103), channel_id=1, replica_groups=mesh['front'=4,'row'=4,'col'=2] {'front','row'}, dimensions={0} | all-to-all | bytes 8388608 | tf_op jit(solution)/shard_map/all_to_all | solution.py:373
  397.8 98.0 %all_to_all.46.refs_2_ = bf16[16,128,1024]{2,1,0:T(8,128)(2,1)} all-to-all(bf16[16,128,1024]{2,1,0:T(8,128)(2,1)S(1)} %copy-done.7), channel_id=1, replica_groups=mesh['front'=4,'row'=4,'col'=2] {'front','row'}, dimensions={0} | all-to-all | bytes 8388608 | tf_op jit(solution)/shard_map/all_to_all | solution.py:373
  495.8 98.0 %all_to_all.47.refs_1_ = bf16[16,128,1024]{2,1,0:T(8,128)(2,1)} all-to-all(bf16[16,128,1024]{2,1,0:T(8,128)(2,1)S(1)} %copy-done.6), channel_id=1, replica_groups=mesh['front'=4,'row'=4,'col'=2] {'front','row'}, dimensions={0} | all-to-all | bytes 8388608 | tf_op jit(solution)/shard_map/all_to_all | solution.py:373
  593.8 97.7 %all_to_all.48.refs_0_ = bf16[16,128,1024]{2,1,0:T(8,128)(2,1)} all-to-all(bf16[16,128,1024]{2,1,0:T(8,128)(2,1)S(1)} %copy-done.5), channel_id=1, replica_groups=mesh['front'=4,'row'=4,'col'=2] {'front','row'}, dimensions={0} | all-to-all | bytes 8388608 | tf_op jit(solution)/shard_map/all_to_all | solution.py:373
  691.5 5.5 all-to-all-start.6
  697.7 2.9 gather_fusion.11
  700.6 4.2 gather_fusion.10
  704.8 4.2 gather_fusion.9
  708.9 4.2 gather_fusion.8
  713.2 6.4 broadcast_select_fusion.2
  719.6 1.5 collective-permute-start.1
  721.6 1.5 collective-permute-start.3
  724.9 0.7 select_reduce_fusion.9
  727.0 0.6 pad_add_fusion.s
  727.7 344.3 %all-to-all-done.6 = bf16[16,128,4224]{2,1,0:T(8,128)(2,1)} async-done(((bf16[16,128,4224]{2,1,0:T(8,128)(2,1)}), bf16[16,128,4224]{2,1,0:T(8,128)(2,1)}, u32[]{:S(2)}, u32[]{:S(2)}) %all-to-all-start.6) | async-done | bytes 17301536 | tf_op jit(solution)/shard_map/while/body/all_to_all | solution.py:413
  1072.0 10.9 gather_fusion.7
  1083.0 30.3 %collective-permute-done.3.refs_6_ = bf16[8,128,1024]{2,1,0:T(8,128)(2,1)} collective-permute-done((bf16[8,128,1024]{2,1,0:T(8,128)(2,1)}, bf16[8,128,1024]{2,1,0:T(8,128)(2,1)}, u32[]{:S(2)}, u32[]{:S(2)}) %collective-permute-start.3) | collective-permute-done | bytes 2097184 | tf_op jit(solution)/shard_map/ppermute | solution.py:367
  1113.3 44.4 %collective-permute-done.4.refs_7_ = bf16[8,128,1024]{2,1,0:T(8,128)(2,1)} collective-permute-done((bf16[8,128,1024]{2,1,0:T(8,128)(2,1)}, bf16[8,128,1024]{2,1,0:T(8,128)(2,1)}, u32[]{:S(2)}, u32[]{:S(2)}) %collective-permute-start.4) | collective-permute-done | bytes 2097184 | tf_op jit(solution)/shard_map/ppermute | solution.py:367
  1157.7 0.6 while.41
  1158.2 0.6 while.42
  1158.9 21.1 %assemble.1 = (f32[640,5120]{1,0:T(8,128)}, f32[640,512]{1,0:T(8,128)}) custom-call(s32[181]{0:T(256)} %pad_add_fusion.s, bf16[16,128,1024]{2,1,0:T(8,128)(2,1)} %get-tuple-element.1095, bf16[16,128,1024]{2,1,0:T(8,128)(2,1)} %get-tuple-element.1094, bf16[16,128,1024]{2,1,0:T(8,128)(2,1)} %get-tuple-element.1093, ...), custom_call_target="tpu_custom_call" | custom-call | tf_op jit(solution)/shard_map/assemble/pallas_call | solution.py:251
  1180.0 1.1 constant_dynamic-slice_fusion
  1181.7 15.7 %collective-permute-done.5 = f32[320,512]{1,0:T(8,128)S(1)} collective-permute-done((f32[320,512]{1,0:T(8,128)S(1)}, f32[320,512]{1,0:T(8,128)S(1)}, u32[]{:S(2)}, u32[]{:S(2)}) %collective-permute-start.5) | collective-permute-done | bytes 655392 | tf_op jit(solution)/shard_map/ppermute | solution.py:474
  1197.4 2.1 dynamic-slice_add_fusion
  (138 shorter events, 10.7 us)
Async XLA Ops:
  7.2 19.7 %copy-start = (s32[80]{0:T(128)S(1)}, s32[80]{0:T(128)}, u32[]{:S(2)}) copy-start(s32[80]{0:T(128)} %param.25) | copy-start | bytes 964
  7.2 2.0 copy-start.12
  7.2 2.4 copy-start.10
  7.2 249.7 %all-gather.2.cloned.1.call-start = ((), (), s32[]{:S(2)}) async-start(), calls=%async_computation.7 | async-start | bytes 18874368 | tf_op jit(solution)/shard_map/all_gather | solution.py:302
  10.6 1.9 copy-start.8
  16.5 2.0 copy-start.9
  23.2 3.5 copy-start.26
  23.3 3.5 copy-start.27
  31.5 235.7 %copy-start.14 = (s32[4,2,32]{2,1,0:T(2,128)}, s32[4,2,32]{2,1,0:T(2,128)S(1)}, u32[]{:S(2)}) copy-start(s32[4,2,32]{2,1,0:T(2,128)S(1)} %rem.89) | copy-start | bytes 3076
  34.1 1.1 copy-start.19
  287.7 10.3 copy-start.16
  287.7 10.3 copy-start.17
  287.7 10.3 copy-start.18
  287.7 10.3 copy-start.22
  287.7 10.3 copy-start.23
  298.6 99.2 %copy-start.7 = (bf16[16,128,1024]{2,1,0:T(8,128)(2,1)S(1)}, bf16[16,128,1024]{2,1,0:T(8,128)(2,1)}, u32[]{:S(2)}) copy-start(bf16[16,128,1024]{2,1,0:T(8,128)(2,1)} %get-tuple-element.1102) | copy-start | bytes 12582916
  397.8 98.0 %copy-start.6 = (bf16[16,128,1024]{2,1,0:T(8,128)(2,1)S(1)}, bf16[16,128,1024]{2,1,0:T(8,128)(2,1)}, u32[]{:S(2)}) copy-start(bf16[16,128,1024]{2,1,0:T(8,128)(2,1)} %get-tuple-element.1101) | copy-start | bytes 12582916
  495.8 98.0 %copy-start.5 = (bf16[16,128,1024]{2,1,0:T(8,128)(2,1)S(1)}, bf16[16,128,1024]{2,1,0:T(8,128)(2,1)}, u32[]{:S(2)}) copy-start(bf16[16,128,1024]{2,1,0:T(8,128)(2,1)} %get-tuple-element.1100) | copy-start | bytes 12582916
  691.5 5.5 copy-start.13
  691.5 5.5 copy-start.20
  691.5 380.6 %all-to-all-start.6 = ((bf16[16,128,4224]{2,1,0:T(8,128)(2,1)}), bf16[16,128,4224]{2,1,0:T(8,128)(2,1)}, u32[]{:S(2)}, u32[]{:S(2)}) async-start(bf16[16,128,4224]{2,1,0:T(8,128)(2,1)} %get-tuple-element.497), calls=%async_computation.6 | async-start | bytes 34603008 | tf_op jit(solution)/shard_map/while/body/all_to_all | solution.py:413
  719.6 363.4 %collective-permute-start.1 = (bf16[8,128,1024]{2,1,0:T(8,128)(2,1)}, bf16[8,128,1024]{2,1,0:T(8,128)(2,1)S(1)}, u32[]{:S(2)}, u32[]{:S(2)}) collective-permute-start(bf16[8,128,1024]{2,1,0:T(8,128)(2,1)} %get-tuple-element.649), channel_id=1, source_target_pairs={{0,2},{2,0},{4,6},{6,4},{8,10},{10,8},{12,14},{14,12},{16,18},{18,... | collective-permute-start | bytes 6291464 | tf_op jit(solution)/shard_map/ppermute | solution.py:367
  721.1 361.9 %collective-permute-start.2 = (bf16[8,128,1024]{2,1,0:T(8,128)(2,1)}, bf16[8,128,1024]{2,1,0:T(8,128)(2,1)}, u32[]{:S(2)}, u32[]{:S(2)}) collective-permute-start(bf16[8,128,1024]{2,1,0:T(8,128)(2,1)} %get-tuple-element.647), channel_id=1, source_target_pairs={{0,2},{2,0},{4,6},{6,4},{8,10},{10,8},{12,14},{14,12},{16,18},{18,... | collective-permute-start | bytes 6291464 | tf_op jit(solution)/shard_map/ppermute | solution.py:367
  721.6 391.7 %collective-permute-start.3 = (bf16[8,128,1024]{2,1,0:T(8,128)(2,1)}, bf16[8,128,1024]{2,1,0:T(8,128)(2,1)}, u32[]{:S(2)}, u32[]{:S(2)}) collective-permute-start(bf16[8,128,1024]{2,1,0:T(8,128)(2,1)} %get-tuple-element.648), channel_id=1, source_target_pairs={{0,2},{2,0},{4,6},{6,4},{8,10},{10,8},{12,14},{14,12},{16,18},{18,... | collective-permute-start | bytes 6291464 | tf_op jit(solution)/shard_map/ppermute | solution.py:367
  723.1 434.5 %collective-permute-start.4 = (bf16[8,128,1024]{2,1,0:T(8,128)(2,1)}, bf16[8,128,1024]{2,1,0:T(8,128)(2,1)}, u32[]{:S(2)}, u32[]{:S(2)}) collective-permute-start(bf16[8,128,1024]{2,1,0:T(8,128)(2,1)} %get-tuple-element.646), channel_id=1, source_target_pairs={{0,2},{2,0},{4,6},{6,4},{8,10},{10,8},{12,14},{14,12},{16,18},{18,... | collective-permute-start | bytes 6291464 | tf_op jit(solution)/shard_map/ppermute | solution.py:367
  723.6 2.1 copy-start.21
  723.6 2.6 copy-start.15
  723.6 2.6 copy-start.24
  723.6 2.6 copy-start.25
  1083.0 74.7 %copy-start.11 = (bf16[8,128,1024]{2,1,0:T(8,128)(2,1)}, bf16[8,128,1024]{2,1,0:T(8,128)(2,1)S(1)}, u32[]{:S(2)}) copy-start(bf16[8,128,1024]{2,1,0:T(8,128)(2,1)S(1)} %collective-permute-done.1.refs_4_) | copy-start | bytes 6291460
  1158.9 40.6 %copy-start.1 = (s32[80]{0:T(128)S(1)}, s32[80]{0:T(128)}, u32[]{:S(2)}) copy-start(s32[80]{0:T(128)} %param.25) | copy-start | bytes 964
  1181.1 16.3 %collective-permute-start.5 = (f32[320,512]{1,0:T(8,128)S(1)}, f32[320,512]{1,0:T(8,128)S(1)}, u32[]{:S(2)}, u32[]{:S(2)}) collective-permute-start(f32[320,512]{1,0:T(8,128)S(1)} %constant_dynamic-slice_fusion), channel_id=1, source_target_pairs={{0,1},{1,0},{2,3},{3,2},{4,5},{5,4},{6,7},{7,6},{8,9},{9,8},{10,11... | collective-permute-start | bytes 1966088 | tf_op jit(solution)/shard_map/ppermute | solution.py:474
Sparse Core Ops, SparseCore 0:
  26.9 230.0 all-gather.1

commit v2 on v1

--- a/solution.py
+++ b/solution.py
@@ -5,38 +5,113 @@
 from jax.experimental.pallas import tpu as pltpu
 from jax.sharding import PartitionSpec as P
 
+
 TILE = 128
 CHUNKS = 4
 ADJACENT = 8
 FR = ("front", "row")
 
 
-def eliminate(pivot, rows, inverse_set):
-    panels = inverse_set.shape[0]
-    width = inverse_set.shape[1]
-    pivot_now = pivot.astype(jnp.float32)
-    rows_now = rows.astype(jnp.float32)
-    leaves = []
-    for panel_index in range(panels):
-        start = panel_index * width
-        left = pivot_now[:, start : start + width].astype(jnp.bfloat16)
-        below = jnp.arange(pivot.shape[0])[:, None] >= start + width
-        lower = jnp.where(
-            below, jnp.dot(left, inverse_set[panel_index], preferred_element_type=jnp.float32), 0.0
+def pivot_kernel(pivot, inverse_set, out):
+    panels, width, _ = inverse_set.shape
+    now = {
+        (i, j): pivot[i * width : (i + 1) * width, j * width : (j + 1) * width].astype(jnp.float32)
+        for i in range(panels)
+        for j in range(i + 1)
+    }
+    out[...] = jnp.zeros_like(out)
+    for k in range(panels - 1):
+        lower = {}
+        for i in range(k + 1, panels):
+            lower[i] = jnp.dot(
+                now[i, k].astype(jnp.bfloat16), inverse_set[k], preferred_element_type=jnp.float32
+            ).astype(jnp.bfloat16)
+            out[k, i * width : (i + 1) * width, :] = lower[i]
+        for i in range(k + 1, panels):
+            for j in range(k + 1, i + 1):
+                now[i, j] = now[i, j] - lax.dot_general(
+                    lower[i], lower[j], (((1,), (1,)), ((), ())), preferred_element_type=jnp.float32
+                )
+
+
+def pivot_panels(pivot, inverse_set):
+    panels, width, _ = inverse_set.shape
+    return pl.pallas_call(
+        pivot_kernel,
+        out_shape=jax.ShapeDtypeStruct((panels, pivot.shape[0], width), jnp.bfloat16),
+        name="pivot",
+    )(pivot, inverse_set)
+
+
+def rows_kernel(rows, inverse_set, lower, out):
+    panels, width, _ = inverse_set.shape
+    now = [rows[:, j * width : (j + 1) * width].astype(jnp.float32) for j in range(panels)]
+    for k in range(panels):
+        side = jnp.dot(
+            now[k].astype(jnp.bfloat16), inverse_set[k], preferred_element_type=jnp.float32
         ).astype(jnp.bfloat16)
-        side = jnp.dot(
-            rows_now[:, start : start + width].astype(jnp.bfloat16),
-            inverse_set[panel_index],
-            preferred_element_type=jnp.float32,
-        ).astype(jnp.bfloat16)
-        pivot_now = pivot_now - lax.dot_general(
-            lower, lower, (((1,), (1,)), ((), ())), preferred_element_type=jnp.float32
-        )
-        rows_now = rows_now - lax.dot_general(
-            side, lower, (((1,), (1,)), ((), ())), preferred_element_type=jnp.float32
-        )
-        leaves.append(side)
-    return jnp.concatenate(leaves, axis=1)
+        out[:, k * width : (k + 1) * width] = side
+        for j in range(k + 1, panels):
+            now[j] = now[j] - lax.dot_general(
+                side,
+                lower[k, j * width : (j + 1) * width, :],
+                (((1,), (1,)), ((), ())),
+                preferred_element_type=jnp.float32,
+            )
+
+
+def eliminate(rows, inverse_set, lower):
+    size, depth = rows.shape
+    step = min(size, 512)
+    return pl.pallas_call(
+        rows_kernel,
+        out_shape=jax.ShapeDtypeStruct(rows.shape, jnp.bfloat16),
+        grid=(size // step,),
+        in_specs=[
+            pl.BlockSpec((step, depth), lambda i: (i, 0)),
+            pl.BlockSpec(inverse_set.shape, lambda i: (0, 0, 0)),
+            pl.BlockSpec(lower.shape, lambda i: (0, 0, 0)),
+        ],
+        out_specs=pl.BlockSpec((step, depth), lambda i: (i, 0)),
+        name="eliminate",
+    )(rows, inverse_set, lower)
+
+
+def collect_border(own, row_index, col_index):
+    n_row = 4
+    half = own.shape[0] // 2
+    up = [(z, z + 1) for z in range(n_row - 1)]
+    down = [(z + 1, z) for z in range(n_row - 1)]
+    piece = lax.dynamic_slice_in_dim(own, col_index * half, half, 0)
+    rest = lax.dynamic_slice_in_dim(own, (1 - col_index) * half, half, 0)
+    below, above = [piece], [piece]
+
+    def by_row(options):
+        chosen = options[0]
+        for z in range(1, n_row):
+            chosen = jnp.where(row_index == z, options[z], chosen)
+        return chosen
+
+    for _ in range(n_row - 1):
+        below.append(lax.ppermute(below[-1], "row", up))
+        above.append(lax.ppermute(above[-1], "row", down))
+    held = (row_index // 2) == col_index
+    near = by_row([above[2], above[1], below[1], below[2]])
+    near_other = lax.ppermute(near, ("row", "col"), [(0, 1), (2, 3), (5, 4), (7, 6)])
+    first = jnp.where(held, piece, near)
+
+    def second(done):
+        _, arrived = lax.optimization_barrier((done, near_other))
+        return jnp.where(held, rest, arrived)
+
+    def others(done):
+        _, up_moved, down_moved = lax.optimization_barrier((done, below, above))
+        low = by_row([down_moved[1], up_moved[1], up_moved[2], up_moved[3]])
+        high = by_row([down_moved[3], down_moved[2], down_moved[1], up_moved[1]])
+        other = lax.ppermute(jnp.where(col_index == 0, high, low), "col", [(0, 1), (1, 0)])
+        return jnp.where(col_index == 0, low, high), other
+
+    return first, second, others
 
 
 def count(mask, axis=-1):
@@ -120,25 +195,21 @@
         out[part] = new.astype(out.dtype)
 
 
-def update_chunk(factor, contrib, scalars, chunk, width, groups):
+def update_chunk(mine, theirs, first, contrib, scalars, chunk, width, groups):
     parts = 4 if groups % 4 == 0 else 1
-    depth = factor.shape[1]
+    depth = mine.shape[1]
     block = min(width, 1024)
     steps = width // block
-    tiles = factor.reshape(-1, TILE, depth)
+    tiles = mine.reshape(-1, TILE, depth)
     left_specs = [
-        pl.BlockSpec(
-            (1, TILE, depth),
-            lambda n, m, s, part=part: (s[groups] + s[m * parts + part], 0, 0),
-        )
+        pl.BlockSpec((1, TILE, depth), lambda n, m, s, part=part: (s[m * parts + part], 0, 0))
         for part in range(parts)
     ]
-    right_spec = pl.BlockSpec(
-        (block, depth), lambda n, m, s: (s[groups + 1] + chunk * steps + n, 0)
-    )
+    right_spec = pl.BlockSpec((block, depth), lambda n, m, s: (first // block + n, 0))
     old_specs = [
         pl.BlockSpec(
-            (TILE, block), lambda n, m, s, part=part: (s[m * parts + part], chunk * steps + n)
+            (TILE, block),
+            lambda n, m, s, part=part: (s[m * parts + part], s[groups + chunk] // block + n),
         )
         for part in range(parts)
     ]
@@ -152,10 +223,10 @@
             out_specs=pl.BlockSpec((parts, TILE, block), lambda n, m, s: (m, 0, n)),
         ),
         name="update",
-    )(scalars, *([tiles] * parts), factor, *([contrib] * parts))
-
-
-def assemble(row_code, col_code, has_cross, recv, near, far, cross_recv, cross_near, init, block):
+    )(scalars, *([tiles] * parts), theirs, *([contrib] * parts))
+
+
+def assemble(row_code, row_from, starts, col_code, has_cross, recv, near, far, cross_recv, cross_near, init, block):
     fronts, per_rows = row_code.shape
     per_cols = col_code.shape[1]
     chunks = len(recv)
@@ -165,10 +236,18 @@
     vectors = block.shape[1]
     cap = recv[0].shape[0]
     scalars = jnp.concatenate(
-        [row_code.reshape(-1), col_code.reshape(-1), has_cross.astype(jnp.int32).reshape(1)]
-    )
+        [
+            row_code.reshape(-1),
+            col_code.reshape(-1),
+            has_cross.astype(jnp.int32).reshape(1),
+            row_from.reshape(-1),
+            starts.reshape(-1),
+        ]
+    ).astype(jnp.int32)
     col_base = fronts * per_rows
     flag = col_base + fronts * per_cols
+    from_base = flag + 1
+    start_base = from_base + fronts * per_rows
 
     def kernel(s, *refs):
         recv_refs = refs[:chunks]
@@ -185,11 +264,18 @@
             for f in range(fronts):
                 code = s[f * per_rows + b]
                 index = code % cap
-
-                def go(source, place, lanes, which):
+                source_row = s[from_base + f * per_rows + b]
+                places = [
+                    pl.multiple_of(s[start_base + source_row * chunks + chunk], TILE)
+                    for chunk in range(chunks)
+                ]
+
+                def go(source, place, lanes, which, offset=None):
                     act(
                         pltpu.make_async_copy(
-                            source.at[index],
+                            source.at[index]
+                            if offset is None
+                            else source.at[index, :, pl.ds(offset, lanes)],
                             held.at[slot, f, :, pl.ds(place, lanes)],
                             sems.at[slot, f, which],
                         )
@@ -198,7 +284,7 @@
                 @pl.when((code >= 0) & (code < cap))
                 def _():
                     for chunk in range(chunks):
-                        go(recv_refs[chunk], chunk * width, width, chunk)
+                        go(recv_refs[chunk], places[chunk], width, chunk)
 
                     @pl.when(s[flag] > 0)
                     def _():
@@ -207,7 +293,7 @@
                 @pl.when((code >= cap) & (code < 2 * cap))
                 def _():
                     for chunk in range(chunks):
-                        go(near_refs[chunk], chunk * width, width, chunk)
+                        go(near_refs[chunk], places[chunk], width, chunk)
 
                     @pl.when(s[flag] > 0)
                     def _():
@@ -215,7 +301,12 @@
 
                 @pl.when(code >= 2 * cap)
                 def _():
-                    go(far_ref, 0, span + cross_span, chunks)
+                    for chunk in range(chunks):
+                        go(far_ref, places[chunk], width, chunk, chunk * width)
+
+                    @pl.when(s[flag] > 0)
+                    def _():
+                        go(far_ref, span, cross_span, chunks, span)
 
         @pl.when(step == 0)
         def _():
@@ -241,7 +332,7 @@
             rounded[:, lanes] = total.astype(jnp.bfloat16)
             return carry
 
-        lax.fori_loop(0, per_cols, column, 0, unroll=4 if per_cols % 4 == 0 else 1)
+        lax.fori_loop(0, per_cols, column, 0, unroll=2)
         product_ref[...] = jnp.dot(
             rounded[...], block_ref[...], preferred_element_type=jnp.float32
         )
@@ -284,7 +375,6 @@
     row_index = lax.axis_index("row")
     col_index = lax.axis_index("col")
     groups = n_front * n_row
-    tiles_all = row_tiles.shape[1]
     slots_all = owner.shape[0]
     row_span = border.shape[1]
     col_span = contrib.shape[2]
@@ -292,14 +382,34 @@
     tile_cols = col_span // TILE
     rows_per_group = slots_all // groups
     cols_per_group = slots_all // n_col
-    share = row_span // n_col
     chunks = CHUNKS if tile_cols % CHUNKS == 0 else 1
     width = col_span // chunks
     me = front_index * n_row + row_index
 
-    own_rows = lax.dynamic_slice_in_dim(border[0], col_index * share, share, 0)
-    leaves = eliminate(pivot_block[0], own_rows, inverses[0])
-    factor = lax.all_gather(leaves, ("row", "col"), axis=0, tiled=True)
+    lower = pivot_panels(pivot_block[0], inverses[0])
+    mine = eliminate(border[0], inverses[0], lower)
+    if n_row == 4 and n_col == 2 and col_span == 2 * row_span and chunks == 4:
+        first, second, others = collect_border(border[0], row_index, col_index)
+        theirs = [eliminate(first, inverses[0], lower)]
+        lines = jnp.arange(n_row)
+        turned = jnp.where(col_index == 0, lines > 0, lines == n_row - 1).astype(jnp.int32)
+        starts = width * jnp.stack(
+            [
+                2 * turned + col_index,
+                2 * turned + 1 - col_index,
+                2 - 2 * turned + col_index,
+                3 - 2 * turned - col_index,
+            ],
+            axis=1,
+        )
+    else:
+        share = row_span // n_col
+        own_rows = lax.dynamic_slice_in_dim(mine, col_index * share, share, 0)
+        factor = lax.all_gather(own_rows, ("row", "col"), axis=0, tiled=True)
+        theirs = [lax.dynamic_slice_in_dim(factor, col_index * col_span, col_span, 0)]
+        second = None
+        starts = jnp.broadcast_to(jnp.arange(chunks) * width, (n_row, chunks))
+    my_starts = lax.dynamic_index_in_dim(starts, row_index, 0, keepdims=False)
 
     slot_rows = owner[row_tiles].reshape(groups, tile_rows)
     plan = row_plan(slot_rows, rows_per_group, groups, ADJACENT)
@@ -328,6 +438,13 @@
             axis=1,
         )
         - 1
+    )
+
+    row_from = jnp.sum(
+        jnp.where(hit, (jnp.arange(groups) % n_row)[:, None, None], 0).reshape(
+            n_front, n_row * groups, rows_per_group
+        ),
+        axis=1,
     )
 
     slot_cols = owner[col_tiles].reshape(n_front, n_col, tile_cols)
@@ -357,22 +474,38 @@
     scalars = jnp.concatenate(
         [
             lax.dynamic_index_in_dim(plan["source_row"], me, 0, keepdims=False),
-            jnp.stack([row_index * tile_rows, col_index * (col_span // min(width, 1024))]),
+            my_starts,
         ]
     ).astype(jnp.int32)
     neighbours = [(g, g ^ 1) for g in range(groups)]
 
     def settle(received):
-        picked = jnp.take(received, near_index, axis=0)
-        return lax.ppermute(picked, FR, neighbours)
-
-    sent, recv, near = [], [], []
+        picked = jnp.take(received, near_index, axis=0, mode="clip")
+        return picked, lax.ppermute(picked, FR, neighbours)
+
+    sent, recv, near, picks = [], [], [], []
     for chunk in range(chunks):
-        piece = update_chunk(factor, contrib[0], scalars, chunk, width, groups)
+        per_part = chunks if second is None else 1
+        piece = update_chunk(
+            mine,
+            theirs[chunk // per_part],
+            (chunk % per_part) * width,
+            contrib[0],
+            scalars,
+            chunk,
+            width,
+            groups,
+        )
+        if chunk == 0 and second is not None:
+            theirs.append(eliminate(second(piece), inverses[0], lower))
+            theirs += [eliminate(part, inverses[0], lower) for part in others(theirs[1])]
+        if chunk >= 2:
+            piece, picks[chunk - 2] = lax.optimization_barrier((piece, picks[chunk - 2]))
         sent.append(piece)
         recv.append(lax.all_to_all(piece, FR, split_axis=0, concat_axis=0, tiled=True))
-    for chunk in range(chunks):
-        near.append(settle(recv[chunk]))
+        picked, moved = settle(recv[chunk])
+        picks.append(picked)
+        near.append(moved)
 
     cross_span = (tile_cols + 1) * TILE
 
@@ -384,7 +517,7 @@
             column = jnp.sum(chosen.astype(jnp.int32) * jnp.arange(tile_cols))
             pick = None
             for chunk in range(chunks):
-                local = column - chunk * (width // TILE)
+                local = column - my_starts[chunk] // TILE
                 inside = (local >= 0) & (local < width // TILE)
                 part = lax.dynamic_slice_in_dim(
                     sent[chunk], jnp.clip(local, 0, width // TILE - 1) * TILE, TILE, 2
@@ -404,20 +537,25 @@
             buffer = lax.dynamic_update_slice_in_dim(buffer, arrived[other], place * TILE, 2)
         return (turn + 1, buffer)
 
+    cross_rounds, _ = lax.optimization_barrier((cross_rounds, recv[-1]))
+    far_rounds, _ = lax.optimization_barrier((plan["rounds"], recv[-1]))
     crossed = unwritten((groups, TILE, cross_span), contrib.dtype)
     _, crossed = lax.while_loop(
         lambda state: state[0] < cross_rounds, cross_round, (jnp.int32(0), crossed)
     )
 
     def cross_exchange(state):
-        received = lax.all_to_all(crossed, FR, split_axis=0, concat_axis=0, tiled=True)
-        return (state[0] + 1, received, settle(received))
-
-    _, cross_recv, cross_near = lax.while_loop(
-        lambda state: state[0] < jnp.minimum(cross_rounds, 1),
+        mark = jnp.full((1, 1, TILE), state[0], contrib.dtype)
+        outgoing = lax.dynamic_update_slice(state[1], mark, (0, 0, tile_cols * TILE))
+        received = lax.all_to_all(outgoing, FR, split_axis=0, concat_axis=0, tiled=True)
+        return (cross_rounds, outgoing, received, settle(received)[1])
+
+    _, _, cross_recv, cross_near = lax.while_loop(
+        lambda state: state[0] < cross_rounds,
         cross_exchange,
         (
             jnp.int32(0),
+            crossed,
             unwritten((groups, TILE, cross_span), contrib.dtype),
             unwritten((ADJACENT, TILE, cross_span), contrib.dtype),
         ),
@@ -435,7 +573,7 @@
         )
         index = jnp.sum(chosen.astype(jnp.int32) * jnp.arange(groups), axis=-1)
         rows = jnp.concatenate(
-            [jnp.take(part, index, axis=0) for part in recv + [cross_recv]], axis=2
+            [jnp.take(part, index, axis=0, mode="clip") for part in recv + [cross_recv]], axis=2
         )
         arrived = lax.all_to_all(rows, FR, split_axis=0, concat_axis=0, tiled=True)
         coming = plan["far"] & for_me & (plan["far_round"] == turn)
@@ -452,11 +590,13 @@
 
     far = unwritten((groups + 1, TILE, col_span + cross_span), contrib.dtype)
     _, far = lax.while_loop(
-        lambda state: state[0] < plan["rounds"], far_exchange, (jnp.int32(0), far)
+        lambda state: state[0] < far_rounds, far_exchange, (jnp.int32(0), far)
     )
 
     schur, partial = assemble(
         row_code,
+        row_from,
+        starts,
         col_code,
         cross_rounds > 0,
         recv,
@@ -490,4 +630,5 @@
         P("col", None),
     )
     out_specs = (P(("front", "row"), "col"), P(("front", "row", "col"), None))
+
     return jax.shard_map(shards, mesh=mesh, in_specs=in_specs, out_specs=out_specs, check_vma=False)

time: 1210 us -> 791 us (0.65)
  blocking collectives: 393 us -> 0 us
  waiting for transfers between devices: 651 us -> 555 us
  starting transfers between devices: 10.1 us -> 69 us
  Pallas kernels: 62.1 us -> 94 us
  matrix products: 13 us -> 0 us
    all_to_all x4 -> x0, blocking collectives: 393 us -> none  [shards(): lax.all_to_all(piece, FR, split_axis=0, concat_axis=0, tiled=True)]
    ppermute x4 -> x12, waiting for transfers between devices: 74.7 us -> 423 us  [the longest x3 175 us: collect_border(): below.append(lax.ppermute(below[-1], 'row', up))]
    all_to_all x1 -> x4, waiting for transfers between devices: 344 us -> 118 us  [shards(): lax.all_to_all(piece, FR, split_axis=0, concat_axis=0, tiled=True)]
    all_gather x1 -> x0, waiting for transfers between devices: 216 us -> none  [shards(): factor = lax.all_gather(leaves, ('row', 'col'), axis=0, tiled=True)]
    all_to_all x1 -> x4, starting transfers between devices: 5.49 us -> 40.7 us  [shards(): lax.all_to_all(piece, FR, split_axis=0, concat_axis=0, tiled=True)]
    pallas_call x0 -> x6, Pallas kernels: none -> 32.7 us  [the longest x5 28.8 us: eliminate(): pl.pallas_call(rows_kernel, out_shape=jax.ShapeDtypeStruct(rows.shape, jn...]
    ppermute x4 -> x12, starting transfers between devices: 4.05 us -> 26.8 us  [the longest x3 14.5 us: collect_border(): below.append(lax.ppermute(below[-1], 'row', up))]
    dot_general x11 -> x0, matrix products: 13 us -> none  [the longest x3 6.06 us: eliminate(): lax.dot_general(side, lower, (((1,), (1,)), ((), ())), preferred_element_...]
  transfers between devices with their start and end apart: 7 -> 17, of which waited for: 5 -> 15; matrix products, arithmetic and copies ran while one was open for 4% -> 5% of each run, Pallas kernels for 0% -> 7%
where the time goes in v2:
time: 791 us; the launch traced here: 789 us
  waiting for transfers between devices  555 us (70%)
  Pallas kernels  94 us (12%)
  starting transfers between devices  69 us (9%)
  local copies, waits for them, and re-layouts  30.8 us (4%)
  other arithmetic  25.8 us (3%)
  between operations  12.1 us (2%)
    ppermute x3, waiting for transfers between devices, collect_border(): below.append(lax.ppermute(below[-1], 'row', up))  175 us
    ppermute x4, waiting for transfers between devices, settle(): return (picked, lax.ppermute(picked, FR, neighbours))  148 us
    all_to_all x4, waiting for transfers between devices, shards(): lax.all_to_all(piece, FR, split_axis=0, concat_axis=0, tiled=True)  118 us
    ppermute x1, waiting for transfers between devices, others(): lax.ppermute(jnp.where(col_index == 0, high, low), 'col', [(0, 1), (1, 0)])  47.9 us
    ppermute x1, waiting for transfers between devices, collect_border(): lax.ppermute(near, ('row', 'col'), [(0, 1), (2, 3), (5, 4), (7, 6)])  44.3 us
    all_to_all x4, starting transfers between devices, shards(): lax.all_to_all(piece, FR, split_axis=0, concat_axis=0, tiled=True)  40.7 us
    pallas_call x4, Pallas kernels, update_chunk(): pl.pallas_call(lambda *refs: update_kernel(parts, *refs), out_shape=jax.S...  40.1 us
    pallas_call x5, Pallas kernels, eliminate(): pl.pallas_call(rows_kernel, out_shape=jax.ShapeDtypeStruct(rows.shape, jn...  28.8 us
  transfers between devices with their start and end apart: 17, of which 15 were waited for; matrix products, arithmetic and copies ran while one was open for 5% of the time, Pallas kernels for 7%

profile of v2, /device:TPU:0, one launch (start us, length us, event | category | flops | bytes accessed | tf_op | source)
XLA Modules:
  0.0 788.9 jit_solution(10569714410189122569)
XLA Ops:
  0.7 3.1 dynamic-slice_bitcast_fusion
  3.8 5.1 collective-permute-start.1
  10.3 1.9 gather_fusion.6
  12.2 41.7 %collective-permute-done.1 = bf16[1024,1024]{1,0:T(8,128)(2,1)S(1)} collective-permute-done((bf16[1024,1024]{1,0:T(8,128)(2,1)}, bf16[1024,1024]{1,0:T(8,128)(2,1)S(1)}, u32[]{:S(2)}, u32[]{:S(2)}) %collective-permute-start.1) | collective-permute-done | bytes 2097184 | tf_op jit(solution)/shard_map/ppermute | solution.py:96
  53.9 5.6 collective-permute-start.2
  61.1 3.9 pivot.1.lower
  65.0 7.9 %eliminate.5 = bf16[2048,1024]{1,0:T(8,128)(2,1)} custom-call(bf16[2048,1024]{1,0:T(8,128)(2,1)} %bitcast.148, bf16[4,256,256]{2,1,0:T(8,128)(2,1)} %bitcast.150, bf16[4,1024,256]{2,1,0:T(8,128)(2,1)} %pivot.1.lower), custom_call_target="tpu_custom_call" | custom-call | tf_op jit(solution)/shard_map/eliminate/pallas_call | solution.py:66
  76.2 26.1 %collective-permute-done.2 = bf16[1024,1024]{1,0:T(8,128)(2,1)} collective-permute-done((bf16[1024,1024]{1,0:T(8,128)(2,1)S(1)}, bf16[1024,1024]{1,0:T(8,128)(2,1)}, u32[]{:S(2)}, u32[]{:S(2)}) %collective-permute-start.2) | collective-permute-done | bytes 2097184 | tf_op jit(solution)/shard_map/ppermute | solution.py:96
  102.3 5.8 collective-permute-done.4
  108.1 6.9 broadcast_select_fusion.1
  114.9 5.2 eliminate.6.refs_5_
  120.1 10.0 %update.4 = bf16[16,128,1024]{2,1,0:T(8,128)(2,1)} custom-call(s32[20]{0:T(128)} %pad_add_fusion.refs_0_, bf16[16,128,1024]{2,1,0:T(8,128)(2,1)} %bitcast.132, bf16[16,128,1024]{2,1,0:T(8,128)(2,1)} %bitcast.133, bf16[16,128,1024]{2,1,0:T(8,128)(2,1)} %bitcast.134, bf16[16,128,1024]{2,1,0:T(8,128)(2,1)} %bitcast.135, bf16[1024,1024]{1,0:T(8,128)(2,1)} %eliminate.6.refs_5_, ...), custom_call_target="tpu_custom_call" | custom-call | tf_op jit(solution)/shard_map/update/pallas_call | solution.py:216
  130.2 4.5 all-to-all-start.5
  134.7 4.7 collective-permute-start.5
  139.5 44.3 %collective-permute-done.5 = bf16[1024,1024]{1,0:T(8,128)(2,1)} collective-permute-done((bf16[1024,1024]{1,0:T(8,128)(2,1)}, bf16[1024,1024]{1,0:T(8,128)(2,1)}, u32[]{:S(2)}, u32[]{:S(2)}) %collective-permute-start.5) | collective-permute-done | bytes 2097184 | tf_op jit(solution)/shard_map/ppermute | solution.py:100
  183.7 3.9 bitcast_select_fusion.2.rows
  187.6 5.2 eliminate.7.refs_5_
  192.8 10.0 %update.6 = bf16[16,128,1024]{2,1,0:T(8,128)(2,1)} custom-call(s32[20]{0:T(128)} %pad_add_fusion.refs_0_, bf16[16,128,1024]{2,1,0:T(8,128)(2,1)} %bitcast.136, bf16[16,128,1024]{2,1,0:T(8,128)(2,1)} %bitcast.137, bf16[16,128,1024]{2,1,0:T(8,128)(2,1)} %bitcast.138, bf16[16,128,1024]{2,1,0:T(8,128)(2,1)} %bitcast.139, bf16[1024,1024]{1,0:T(8,128)(2,1)} %eliminate.7.refs_5_, ...), custom_call_target="tpu_custom_call" | custom-call | tf_op jit(solution)/shard_map/update/pallas_call | solution.py:216
  202.9 26.2 %all-to-all-done.5.refs_0_ = bf16[16,128,1024]{2,1,0:T(8,128)(2,1)} async-done(((bf16[16,128,1024]{2,1,0:T(8,128)(2,1)}), bf16[16,128,1024]{2,1,0:T(8,128)(2,1)}, u32[]{:S(2)}, u32[]{:S(2)}) %all-to-all-start.5) | async-done | bytes 4194336 | tf_op jit(solution)/shard_map/all_to_all | solution.py:505
  229.0 4.5 all-to-all-start.3
  233.5 3.8 collective-permute-start.6
  239.9 107.2 %collective-permute-done.6 = bf16[1024,1024]{1,0:T(8,128)(2,1)S(1)} collective-permute-done((bf16[1024,1024]{1,0:T(8,128)(2,1)}, bf16[1024,1024]{1,0:T(8,128)(2,1)S(1)}, u32[]{:S(2)}, u32[]{:S(2)}) %collective-permute-start.6) | collective-permute-done | bytes 2097184 | tf_op jit(solution)/shard_map/ppermute | solution.py:96
  347.1 1.8 collective-permute-done.7
  348.8 4.3 broadcast_select_fusion.2
  353.2 5.3 eliminate.9.refs_5_
  358.4 10.0 %update.7 = bf16[16,128,1024]{2,1,0:T(8,128)(2,1)} custom-call(s32[20]{0:T(128)} %pad_add_fusion.refs_0_, bf16[16,128,1024]{2,1,0:T(8,128)(2,1)} %bitcast.140, bf16[16,128,1024]{2,1,0:T(8,128)(2,1)} %bitcast.141, bf16[16,128,1024]{2,1,0:T(8,128)(2,1)} %bitcast.142, bf16[16,128,1024]{2,1,0:T(8,128)(2,1)} %bitcast.143, bf16[1024,1024]{1,0:T(8,128)(2,1)} %eliminate.9.refs_5_, ...), custom_call_target="tpu_custom_call" | custom-call | tf_op jit(solution)/shard_map/update/pallas_call | solution.py:216
  368.4 4.2 gather_fusion.9
  372.6 26.9 %all-to-all-start.6 = ((bf16[16,128,1024]{2,1,0:T(8,128)(2,1)}), bf16[16,128,1024]{2,1,0:T(8,128)(2,1)}, u32[]{:S(2)}, u32[]{:S(2)}) async-start(bf16[16,128,1024]{2,1,0:T(8,128)(2,1)} %update.7), calls=%async_computation.6 | async-start | bytes 8388608 | tf_op jit(solution)/shard_map/all_to_all | solution.py:505
  399.5 1.9 broadcast_select_fusion.3
  401.5 47.9 %collective-permute-done.8.rows = bf16[1024,1024]{1,0:T(8,128)(2,1)S(1)} collective-permute-done((bf16[1024,1024]{1,0:T(8,128)(2,1)S(1)}, bf16[1024,1024]{1,0:T(8,128)(2,1)S(1)}, u32[]{:S(2)}, u32[]{:S(2)}) %collective-permute-start.8) | collective-permute-done | bytes 2097184 | tf_op jit(solution)/shard_map/ppermute | solution.py:111
  450.8 5.2 eliminate.8.refs_5_
  456.0 10.0 %update.5 = bf16[16,128,1024]{2,1,0:T(8,128)(2,1)} custom-call(s32[20]{0:T(128)} %pad_add_fusion.refs_0_, bf16[16,128,1024]{2,1,0:T(8,128)(2,1)} %bitcast.144, bf16[16,128,1024]{2,1,0:T(8,128)(2,1)} %bitcast.145, bf16[16,128,1024]{2,1,0:T(8,128)(2,1)} %bitcast.146, bf16[16,128,1024]{2,1,0:T(8,128)(2,1)} %bitcast.147, bf16[1024,1024]{1,0:T(8,128)(2,1)} %eliminate.8.refs_5_, ...), custom_call_target="tpu_custom_call" | custom-call | tf_op jit(solution)/shard_map/update/pallas_call | solution.py:216
  466.0 4.2 gather_fusion.8
  470.2 23.6 %all-to-all-done.6.refs_2_ = bf16[16,128,1024]{2,1,0:T(8,128)(2,1)} async-done(((bf16[16,128,1024]{2,1,0:T(8,128)(2,1)}), bf16[16,128,1024]{2,1,0:T(8,128)(2,1)}, u32[]{:S(2)}, u32[]{:S(2)}) %all-to-all-start.6) | async-done | bytes 4194336 | tf_op jit(solution)/shard_map/all_to_all | solution.py:505
  493.8 4.8 all-to-all-start.4
  498.7 1.9 gather_fusion.7
  503.2 1.6 collective-permute-start.9
  518.9 4.2 gather_fusion.10
  524.7 68.1 %all-to-all-done.4.refs_3_ = bf16[16,128,1024]{2,1,0:T(8,128)(2,1)} async-done(((bf16[16,128,1024]{2,1,0:T(8,128)(2,1)}), bf16[16,128,1024]{2,1,0:T(8,128)(2,1)}, u32[]{:S(2)}, u32[]{:S(2)}) %all-to-all-start.4) | async-done | bytes 4194336 | tf_op jit(solution)/shard_map/all_to_all | solution.py:505
  592.8 4.2 gather_fusion.11
  598.3 15.9 %collective-permute-done.9.refs_4_ = bf16[8,128,1024]{2,1,0:T(8,128)(2,1)S(1)} collective-permute-done((bf16[8,128,1024]{2,1,0:T(8,128)(2,1)}, bf16[8,128,1024]{2,1,0:T(8,128)(2,1)S(1)}, u32[]{:S(2)}, u32[]{:S(2)}) %collective-permute-start.9) | collective-permute-done | bytes 2097184 | tf_op jit(solution)/shard_map/ppermute | solution.py:484
  614.2 45.0 %collective-permute-done.10.refs_5_ = bf16[8,128,1024]{2,1,0:T(8,128)(2,1)} collective-permute-done((bf16[8,128,1024]{2,1,0:T(8,128)(2,1)}, bf16[8,128,1024]{2,1,0:T(8,128)(2,1)}, u32[]{:S(2)}, u32[]{:S(2)}) %collective-permute-start.10) | collective-permute-done | bytes 2097184 | tf_op jit(solution)/shard_map/ppermute | solution.py:484
  661.4 42.8 %collective-permute-done.11.refs_6_ = bf16[8,128,1024]{2,1,0:T(8,128)(2,1)} collective-permute-done((bf16[8,128,1024]{2,1,0:T(8,128)(2,1)}, bf16[8,128,1024]{2,1,0:T(8,128)(2,1)}, u32[]{:S(2)}, u32[]{:S(2)}) %collective-permute-start.11) | collective-permute-done | bytes 2097184 | tf_op jit(solution)/shard_map/ppermute | solution.py:484
  704.2 44.4 %collective-permute-done.12.refs_7_ = bf16[8,128,1024]{2,1,0:T(8,128)(2,1)} collective-permute-done((bf16[8,128,1024]{2,1,0:T(8,128)(2,1)}, bf16[8,128,1024]{2,1,0:T(8,128)(2,1)}, u32[]{:S(2)}, u32[]{:S(2)}) %collective-permute-start.12) | collective-permute-done | bytes 2097184 | tf_op jit(solution)/shard_map/ppermute | solution.py:484
  748.6 21.1 %assemble.1 = (f32[640,5120]{1,0:T(8,128)}, f32[640,512]{1,0:T(8,128)}) custom-call(s32[217]{0:T(256)} %concatenate.12.s, bf16[16,128,1024]{2,1,0:T(8,128)(2,1)} %all-to-all-done.5.refs_0_, bf16[16,128,1024]{2,1,0:T(8,128)(2,1)} %all-to-all-done.3.refs_1_, bf16[16,128,1024]{2,1,0:T(8,128)(2,1)} %all-to-all-done.6.refs_2_, ...), custom_call_target="tpu_custom_call" | custom-call | tf_op jit(solution)/shard_map/assemble/pallas_call | solution.py:342
  770.9 1.6 collective-permute-start.13
  772.4 14.4 %collective-permute-done.13 = f32[320,512]{1,0:T(8,128)S(1)} collective-permute-done((f32[320,512]{1,0:T(8,128)S(1)}, f32[320,512]{1,0:T(8,128)S(1)}, u32[]{:S(2)}, u32[]{:S(2)}) %collective-permute-start.13) | collective-permute-done | bytes 655392 | tf_op jit(solution)/shard_map/ppermute | solution.py:614
  786.9 2.1 dynamic-slice_add_fusion
  (124 shorter events, 22.0 us)
Async XLA Ops:
  0.6 9.7 %copy-start = (s32[80]{0:T(128)S(1)}, s32[80]{0:T(128)}, u32[]{:S(2)}) copy-start(s32[80]{0:T(128)} %param.21) | copy-start | bytes 964
  0.6 9.5 %copy-start.10 = (s32[4,64]{1,0:T(4,128)S(1)}, s32[4,64]{1,0:T(4,128)}, u32[]{:S(2)}) copy-start(s32[4,64]{1,0:T(4,128)} %param.19) | copy-start | bytes 3076
  0.7 9.5 %copy-start.9 = (s32[4,64]{1,0:T(4,128)S(1)}, s32[4,64]{1,0:T(4,128)}, u32[]{:S(2)}) copy-start(s32[4,64]{1,0:T(4,128)} %param.20) | copy-start | bytes 3076
  3.8 50.1 %collective-permute-start.1 = (bf16[1024,1024]{1,0:T(8,128)(2,1)}, bf16[1024,1024]{1,0:T(8,128)(2,1)S(1)}, u32[]{:S(2)}, u32[]{:S(2)}) collective-permute-start(bf16[1024,1024]{1,0:T(8,128)(2,1)} %dynamic-slice_bitcast_fusion), channel_id=1, source_target_pairs={{0,2},{2,4},{4,6},{1,3},{3,5},{5,7},{8,10},{10,12},{12,14},{9,11},... | collective-permute-start | bytes 6291464 | tf_op jit(solution)/shard_map/ppermute | solution.py:96
  8.8 50.7 %collective-permute-start.3 = (bf16[1024,1024]{1,0:T(8,128)(2,1)}, bf16[1024,1024]{1,0:T(8,128)(2,1)}, u32[]{:S(2)}, u32[]{:S(2)}) collective-permute-start(bf16[1024,1024]{1,0:T(8,128)(2,1)} %dynamic-slice_bitcast_fusion), channel_id=1, source_target_pairs={{2,0},{4,2},{6,4},{3,1},{5,3},{7,5},{10,8},{12,10},{14,12},{11,9},... | collective-permute-start | bytes 6291464 | tf_op jit(solution)/shard_map/ppermute | solution.py:97
  53.9 48.4 %collective-permute-start.2 = (bf16[1024,1024]{1,0:T(8,128)(2,1)S(1)}, bf16[1024,1024]{1,0:T(8,128)(2,1)}, u32[]{:S(2)}, u32[]{:S(2)}) collective-permute-start(bf16[1024,1024]{1,0:T(8,128)(2,1)S(1)} %collective-permute-done.1), channel_id=1, source_target_pairs={{0,2},{2,4},{4,6},{1,3},{3,5},{5,7},{8,10},{10,12},{12,14},{9,11},... | collective-permute-start | bytes 6291464 | tf_op jit(solution)/shard_map/ppermute | solution.py:96
  59.5 48.5 %collective-permute-start.4 = (bf16[1024,1024]{1,0:T(8,128)(2,1)}, bf16[1024,1024]{1,0:T(8,128)(2,1)}, u32[]{:S(2)}, u32[]{:S(2)}) collective-permute-start(bf16[1024,1024]{1,0:T(8,128)(2,1)} %collective-permute-done.3), channel_id=1, source_target_pairs={{2,0},{4,2},{6,4},{3,1},{5,3},{7,5},{10,8},{12,10},{14,12},{11,9},... | collective-permute-start | bytes 6291464 | tf_op jit(solution)/shard_map/ppermute | solution.py:97
  130.2 98.8 %all-to-all-start.5 = ((bf16[16,128,1024]{2,1,0:T(8,128)(2,1)}), bf16[16,128,1024]{2,1,0:T(8,128)(2,1)}, u32[]{:S(2)}, u32[]{:S(2)}) async-start(bf16[16,128,1024]{2,1,0:T(8,128)(2,1)} %update.4), calls=%async_computation.5 | async-start | bytes 8388608 | tf_op jit(solution)/shard_map/all_to_all | solution.py:505
  134.7 49.0 %collective-permute-start.5 = (bf16[1024,1024]{1,0:T(8,128)(2,1)}, bf16[1024,1024]{1,0:T(8,128)(2,1)}, u32[]{:S(2)}, u32[]{:S(2)}) collective-permute-start(bf16[1024,1024]{1,0:T(8,128)(2,1)} %get-tuple-element.800), channel_id=1, source_target_pairs={{0,1},{2,3},{5,4},{7,6},{8,9},{10,11},{13,12},{15,14},{16,17},{18,... | collective-permute-start | bytes 6291464 | tf_op jit(solution)/shard_map/ppermute | solution.py:100
  229.0 143.6 %all-to-all-start.3 = ((bf16[16,128,1024]{2,1,0:T(8,128)(2,1)}), bf16[16,128,1024]{2,1,0:T(8,128)(2,1)}, u32[]{:S(2)}, u32[]{:S(2)}) async-start(bf16[16,128,1024]{2,1,0:T(8,128)(2,1)} %update.6), calls=%async_computation.3 | async-start | bytes 8388608 | tf_op jit(solution)/shard_map/all_to_all | solution.py:505
  233.5 113.5 %collective-permute-start.6 = (bf16[1024,1024]{1,0:T(8,128)(2,1)}, bf16[1024,1024]{1,0:T(8,128)(2,1)S(1)}, u32[]{:S(2)}, u32[]{:S(2)}) collective-permute-start(bf16[1024,1024]{1,0:T(8,128)(2,1)} %collective-permute-done.2), channel_id=1, source_target_pairs={{0,2},{2,4},{4,6},{1,3},{3,5},{5,7},{8,10},{10,12},{12,14},{9,11},... | collective-permute-start | bytes 6291464 | tf_op jit(solution)/shard_map/ppermute | solution.py:96
  237.3 111.5 %collective-permute-start.7 = (bf16[1024,1024]{1,0:T(8,128)(2,1)}, bf16[1024,1024]{1,0:T(8,128)(2,1)S(1)}, u32[]{:S(2)}, u32[]{:S(2)}) collective-permute-start(bf16[1024,1024]{1,0:T(8,128)(2,1)} %collective-permute-done.4), channel_id=1, source_target_pairs={{2,0},{4,2},{6,4},{3,1},{5,3},{7,5},{10,8},{12,10},{14,12},{11,9},... | collective-permute-start | bytes 6291464 | tf_op jit(solution)/shard_map/ppermute | solution.py:97
  239.8 113.3 %copy-start.7 = (s32[8]{0:T(128)}, s32[8]{0:T(128)S(1)}, u32[]{:S(2)}) copy-start(s32[8]{0:T(128)S(1)} %select_reduce_fusion.11) | copy-start | bytes 100
  372.6 26.9 %copy-start.3 = (bf16[1024,1024]{1,0:T(8,128)(2,1)S(1)}, bf16[1024,1024]{1,0:T(8,128)(2,1)}, u32[]{:S(2)}) copy-start(bf16[1024,1024]{1,0:T(8,128)(2,1)} %get-tuple-element.797) | copy-start | bytes 6291460
  372.6 121.2 %all-to-all-start.6 = ((bf16[16,128,1024]{2,1,0:T(8,128)(2,1)}), bf16[16,128,1024]{2,1,0:T(8,128)(2,1)}, u32[]{:S(2)}, u32[]{:S(2)}) async-start(bf16[16,128,1024]{2,1,0:T(8,128)(2,1)} %update.7), calls=%async_computation.6 | async-start | bytes 8388608 | tf_op jit(solution)/shard_map/all_to_all | solution.py:505
  401.5 48.0 %collective-permute-start.8 = (bf16[1024,1024]{1,0:T(8,128)(2,1)S(1)}, bf16[1024,1024]{1,0:T(8,128)(2,1)S(1)}, u32[]{:S(2)}, u32[]{:S(2)}) collective-permute-start(bf16[1024,1024]{1,0:T(8,128)(2,1)S(1)} %broadcast_select_fusion.3), channel_id=1, source_target_pairs={{0,1},{1,0},{2,3},{3,2},{4,5},{5,4},{6,7},{7,6},{8,9},{9,8},{10,11... | collective-permute-start | bytes 6291464 | tf_op jit(solution)/shard_map/ppermute | solution.py:111
  449.4 1.4 copy-start.5
  493.8 98.9 %all-to-all-start.4 = ((bf16[16,128,1024]{2,1,0:T(8,128)(2,1)}), bf16[16,128,1024]{2,1,0:T(8,128)(2,1)}, u32[]{:S(2)}, u32[]{:S(2)}) async-start(bf16[16,128,1024]{2,1,0:T(8,128)(2,1)} %update.5), calls=%async_computation.4 | async-start | bytes 8388608 | tf_op jit(solution)/shard_map/all_to_all | solution.py:505
  503.2 111.0 %collective-permute-start.9 = (bf16[8,128,1024]{2,1,0:T(8,128)(2,1)}, bf16[8,128,1024]{2,1,0:T(8,128)(2,1)S(1)}, u32[]{:S(2)}, u32[]{:S(2)}) collective-permute-start(bf16[8,128,1024]{2,1,0:T(8,128)(2,1)} %gather_fusion.9), channel_id=1, source_target_pairs={{0,2},{2,0},{4,6},{6,4},{8,10},{10,8},{12,14},{14,12},{16,18},{18,... | collective-permute-start | bytes 6291464 | tf_op jit(solution)/shard_map/ppermute | solution.py:484
  504.8 154.5 %collective-permute-start.10 = (bf16[8,128,1024]{2,1,0:T(8,128)(2,1)}, bf16[8,128,1024]{2,1,0:T(8,128)(2,1)}, u32[]{:S(2)}, u32[]{:S(2)}) collective-permute-start(bf16[8,128,1024]{2,1,0:T(8,128)(2,1)} %gather_fusion.8), channel_id=1, source_target_pairs={{0,2},{2,0},{4,6},{6,4},{8,10},{10,8},{12,14},{14,12},{16,18},{18,... | collective-permute-start | bytes 6291464 | tf_op jit(solution)/shard_map/ppermute | solution.py:484
  523.2 181.0 %collective-permute-start.11 = (bf16[8,128,1024]{2,1,0:T(8,128)(2,1)}, bf16[8,128,1024]{2,1,0:T(8,128)(2,1)}, u32[]{:S(2)}, u32[]{:S(2)}) collective-permute-start(bf16[8,128,1024]{2,1,0:T(8,128)(2,1)} %gather_fusion.10), channel_id=1, source_target_pairs={{0,2},{2,0},{4,6},{6,4},{8,10},{10,8},{12,14},{14,12},{16,18},{18,... | collective-permute-start | bytes 6291464 | tf_op jit(solution)/shard_map/ppermute | solution.py:484
  597.0 151.6 %collective-permute-start.12 = (bf16[8,128,1024]{2,1,0:T(8,128)(2,1)}, bf16[8,128,1024]{2,1,0:T(8,128)(2,1)}, u32[]{:S(2)}, u32[]{:S(2)}) collective-permute-start(bf16[8,128,1024]{2,1,0:T(8,128)(2,1)} %gather_fusion.11), channel_id=1, source_target_pairs={{0,2},{2,0},{4,6},{6,4},{8,10},{10,8},{12,14},{14,12},{16,18},{18,... | collective-permute-start | bytes 6291464 | tf_op jit(solution)/shard_map/ppermute | solution.py:484
  614.2 45.1 %copy-start.4 = (bf16[8,128,1024]{2,1,0:T(8,128)(2,1)}, bf16[8,128,1024]{2,1,0:T(8,128)(2,1)S(1)}, u32[]{:S(2)}) copy-start(bf16[8,128,1024]{2,1,0:T(8,128)(2,1)S(1)} %collective-permute-done.9.refs_4_) | copy-start | bytes 6291460
  659.3 0.7 copy-start.8
  660.0 0.7 copy-start.6
  748.6 40.3 %copy-start.1 = (s32[80]{0:T(128)S(1)}, s32[80]{0:T(128)}, u32[]{:S(2)}) copy-start(s32[80]{0:T(128)} %param.21) | copy-start | bytes 964
  770.9 16.0 %collective-permute-start.13 = (f32[320,512]{1,0:T(8,128)S(1)}, f32[320,512]{1,0:T(8,128)S(1)}, u32[]{:S(2)}, u32[]{:S(2)}) collective-permute-start(f32[320,512]{1,0:T(8,128)S(1)} %constant_dynamic-slice_fusion), channel_id=1, source_target_pairs={{0,1},{1,0},{2,3},{3,2},{4,5},{5,4},{6,7},{7,6},{8,9},{9,8},{10,11... | collective-permute-start | bytes 1966088 | tf_op jit(solution)/shard_map/ppermute | solution.py:614

commit v3 on v2

--- a/solution.py
+++ b/solution.py
@@ -8,7 +8,8 @@
 
 TILE = 128
 CHUNKS = 4
-ADJACENT = 8
+ROW_CAP = 6
+FRONT_CAPS = (6, 4, 3)
 FR = ("front", "row")
 
 
@@ -80,11 +81,14 @@
 def collect_border(own, row_index, col_index):
     n_row = 4
     half = own.shape[0] // 2
+    part = half // 2
     up = [(z, z + 1) for z in range(n_row - 1)]
     down = [(z + 1, z) for z in range(n_row - 1)]
-    piece = lax.dynamic_slice_in_dim(own, col_index * half, half, 0)
-    rest = lax.dynamic_slice_in_dim(own, (1 - col_index) * half, half, 0)
-    below, above = [piece], [piece]
+    first_row = col_index * half
+    pieces = [lax.dynamic_slice_in_dim(own, first_row + p * part, part, 0) for p in range(2)]
+    rest = lax.dynamic_slice_in_dim(own, half - first_row, half, 0)
+    held = (row_index // 2) == col_index
+    left = col_index == 0
 
     def by_row(options):
         chosen = options[0]
@@ -92,24 +96,34 @@
             chosen = jnp.where(row_index == z, options[z], chosen)
         return chosen
 
-    for _ in range(n_row - 1):
-        below.append(lax.ppermute(below[-1], "row", up))
-        above.append(lax.ppermute(above[-1], "row", down))
-    held = (row_index // 2) == col_index
-    near = by_row([above[2], above[1], below[1], below[2]])
-    near_other = lax.ppermute(near, ("row", "col"), [(0, 1), (2, 3), (5, 4), (7, 6)])
-    first = jnp.where(held, piece, near)
+    below = [[piece] for piece in pieces]
+    above = [[piece] for piece in pieces]
+    for p in range(2):
+        for _ in range(n_row - 1):
+            below[p].append(lax.ppermute(below[p][-1], "row", up))
+            above[p].append(lax.ppermute(above[p][-1], "row", down))
+    swapped = [None, None]
+
+    def first(p, done):
+        options = [above[p][2], above[p][1], below[p][1], below[p][2]]
+        if done is not None:
+            _, options = lax.optimization_barrier((done, options))
+        near = by_row(options)
+        swapped[p] = lax.ppermute(near, ("row", "col"), [(0, 1), (2, 3), (5, 4), (7, 6)])
+        return jnp.where(held, pieces[p], near)
 
     def second(done):
-        _, arrived = lax.optimization_barrier((done, near_other))
-        return jnp.where(held, rest, arrived)
+        _, arrived = lax.optimization_barrier((done, swapped))
+        return jnp.where(held, rest, jnp.concatenate(arrived))
 
     def others(done):
-        _, up_moved, down_moved = lax.optimization_barrier((done, below, above))
-        low = by_row([down_moved[1], up_moved[1], up_moved[2], up_moved[3]])
-        high = by_row([down_moved[3], down_moved[2], down_moved[1], up_moved[1]])
-        other = lax.ppermute(jnp.where(col_index == 0, high, low), "col", [(0, 1), (1, 0)])
-        return jnp.where(col_index == 0, low, high), other
+        _, ups, downs = lax.optimization_barrier((done, below, above))
+        low = [by_row([d[1], u[1], u[2], u[3]]) for u, d in zip(ups, downs)]
+        high = [by_row([d[3], d[2], d[1], u[1]]) for u, d in zip(ups, downs)]
+        keep = jnp.concatenate([jnp.where(left, a, b) for a, b in zip(low, high)])
+        give = jnp.concatenate([jnp.where(left, b, a) for a, b in zip(low, high)])
+        other = lax.ppermute(give, "col", [(0, 1), (1, 0)])
+        return keep, other
 
     return first, second, others
 
@@ -122,26 +136,40 @@
     return jnp.arange(n)[None, :] < jnp.arange(n)[:, None]
 
 
-def row_plan(slot_rows, per_group, groups, adjacent):
+def row_plan(slot_rows, per_group, groups, kinds):
     sources, tile_rows = slot_rows.shape
+    places = jnp.arange(groups)
     target = slot_rows // per_group
     within = slot_rows % per_group
     same = target[:, :, None] == target[:, None, :]
-    rank = count(same & earlier(tile_rows)[None])
-    extra = rank > 0
-    key = target * tile_rows + rank
-    extra_order = count(extra[:, None, :] & (key[:, None, :] < key[:, :, None]))
-    empty = count(target[:, None, :] == jnp.arange(groups)[None, :, None]) == 0
+    extra = count(same & earlier(tile_rows)[None]) > 0
+    amount = count(target[:, None, :] == places[None, :, None])
+    double = amount > 1
+    empty = amount == 0
+    landing = jnp.zeros_like(amount)
+    for step, _ in kinds[1:]:
+        match = double & empty[:, places ^ step]
+        landing = jnp.where(match, places ^ step, landing)
+        double = double & ~match
+        empty = empty & ~match[:, places ^ step]
+    double_order = count(double[:, None, :] & earlier(groups)[None])
     empty_order = count(empty[:, None, :] & earlier(groups)[None])
-    lands = jnp.where(
-        extra[:, None, :],
-        empty[:, :, None] & (empty_order[:, :, None] == extra_order[:, None, :]),
-        target[:, None, :] == jnp.arange(groups)[None, :, None],
+    left = (
+        double[:, :, None]
+        & empty[:, None, :]
+        & (double_order[:, :, None] == empty_order[:, None, :])
+    )
+    landing = landing + jnp.sum(left.astype(jnp.int32) * places, axis=-1)
+    extra_place = jnp.sum(
+        (target[:, :, None] == places).astype(jnp.int32) * landing[:, None, :], axis=-1
+    )
+    lands = (
+        jnp.where(extra, extra_place, target)[:, None, :] == places[None, :, None]
     ).astype(jnp.int32)
     source_row = jnp.sum(lands * jnp.arange(tile_rows), axis=-1)
     to_group = jnp.sum(lands * target[:, None, :], axis=-1)
     to_within = jnp.sum(lands * within[:, None, :], axis=-1)
-    here = jnp.arange(groups)[None, :]
+    here = places[None, :]
     astray = to_group != here
     order = count(
         (to_group[:, None, :] == to_group[None, :, :])
@@ -149,10 +177,17 @@
         & earlier(sources)[:, :, None],
         axis=1,
     )
-    near = astray & (to_group == (here ^ 1)) & (order < adjacent)
-    far = astray & ~near
-    far_round = jnp.where(to_group == (here ^ 1), order - adjacent, order)
-    rounds = jnp.max(jnp.where(far, far_round + 1, 0))
+    steps = to_group ^ here
+    kind = jnp.zeros_like(order)
+    far_round = order
+    for index, (step, room) in enumerate(kinds):
+        kind = jnp.where(astray & (steps == step) & (order < room), index + 1, kind)
+        far_round = jnp.where(steps == step, order - room, far_round)
+    far = astray & (kind == 0)
+    kind = jnp.where(far, len(kinds) + 1, kind)
+    rounds = jnp.max(
+        jnp.where(far & (steps == places[:, None, None]), far_round + 1, 0), axis=(1, 2)
+    )
     flat_group = to_group.T.reshape(-1)
     flat_far = far.T.reshape(-1)
     total = flat_group.shape[0]
@@ -164,11 +199,10 @@
         to_group=to_group,
         to_within=to_within,
         order=order,
-        near=near,
+        kind=kind,
         far=far,
         far_round=far_round,
         far_place=far_place,
-        astray=astray,
         rounds=rounds,
     )
 
@@ -230,8 +264,12 @@
     fronts, per_rows = row_code.shape
     per_cols = col_code.shape[1]
     chunks = len(recv)
-    width = recv[0].shape[2]
-    span = chunks * width
+    moves_of = [recv] + near
+    cross_of = [cross_recv] + cross_near
+    sources = len(moves_of)
+    widths = [part.shape[2] for part in recv]
+    offsets = [sum(widths[:chunk]) for chunk in range(chunks)]
+    span = sum(widths)
     cross_span = cross_recv.shape[2]
     vectors = block.shape[1]
     cap = recv[0].shape[0]
@@ -250,13 +288,10 @@
     start_base = from_base + fronts * per_rows
 
     def kernel(s, *refs):
-        recv_refs = refs[:chunks]
-        near_refs = refs[chunks : 2 * chunks]
-        far_ref, cross_recv_ref, cross_near_ref, init_ref, block_ref = refs[
-            2 * chunks : 2 * chunks + 5
-        ]
-        schur_ref, product_ref = refs[2 * chunks + 5 : 2 * chunks + 7]
-        held, rounded, sems = refs[2 * chunks + 7 :]
+        main_refs = [refs[k * chunks : (k + 1) * chunks] for k in range(sources)]
+        refs = refs[sources * chunks :]
+        cross_refs, refs = refs[:sources], refs[sources:]
+        far_ref, init_ref, block_ref, schur_ref, product_ref, held, rounded, sems = refs
         step = pl.program_id(0)
 
         def moves(b, act):
@@ -281,28 +316,21 @@
                         )
                     )
 
-                @pl.when((code >= 0) & (code < cap))
+                for k in range(sources):
+
+                    @pl.when((code >= k * cap) & (code < (k + 1) * cap))
+                    def _(k=k):
+                        for chunk in range(chunks):
+                            go(main_refs[k][chunk], places[chunk], widths[chunk], chunk)
+
+                        @pl.when(s[flag] > 0)
+                        def _():
+                            go(cross_refs[k], span, cross_span, chunks)
+
+                @pl.when(code >= sources * cap)
                 def _():
                     for chunk in range(chunks):
-                        go(recv_refs[chunk], places[chunk], width, chunk)
-
-                    @pl.when(s[flag] > 0)
-                    def _():
-                        go(cross_recv_ref, span, cross_span, chunks)
-
-                @pl.when((code >= cap) & (code < 2 * cap))
-                def _():
-                    for chunk in range(chunks):
-                        go(near_refs[chunk], places[chunk], width, chunk)
-
-                    @pl.when(s[flag] > 0)
-                    def _():
-                        go(cross_near_ref, span, cross_span, chunks)
-
-                @pl.when(code >= 2 * cap)
-                def _():
-                    for chunk in range(chunks):
-                        go(far_ref, places[chunk], width, chunk, chunk * width)
+                        go(far_ref, places[chunk], widths[chunk], chunk, offsets[chunk])
 
                     @pl.when(s[flag] > 0)
                     def _():
@@ -348,7 +376,7 @@
         grid_spec=pltpu.PrefetchScalarGridSpec(
             num_scalar_prefetch=1,
             grid=(per_rows,),
-            in_specs=[anywhere] * (2 * chunks + 3)
+            in_specs=[anywhere] * (sources * (chunks + 1) + 1)
             + [
                 pl.BlockSpec((TILE, wide), lambda b, s: (b, 0)),
                 pl.BlockSpec((wide, vectors), lambda b, s: (0, 0)),
@@ -364,7 +392,7 @@
             ],
         ),
         name="assemble",
-    )(scalars, *recv, *near, far, cross_recv, cross_near, init, block)
+    )(scalars, *[part for parts in moves_of for part in parts], *cross_of, far, init, block)
 
 
 def shards(pivot_block, border, contrib, inverses, row_tiles, col_tiles, owner, schur_init, block):
@@ -382,23 +410,26 @@
     tile_cols = col_span // TILE
     rows_per_group = slots_all // groups
     cols_per_group = slots_all // n_col
-    chunks = CHUNKS if tile_cols % CHUNKS == 0 else 1
-    width = col_span // chunks
+    by_hops = takes_hops(n_row, n_col) and col_span == 2 * row_span
     me = front_index * n_row + row_index
 
     lower = pivot_panels(pivot_block[0], inverses[0])
     mine = eliminate(border[0], inverses[0], lower)
-    if n_row == 4 and n_col == 2 and col_span == 2 * row_span and chunks == 4:
+    if by_hops:
         first, second, others = collect_border(border[0], row_index, col_index)
-        theirs = [eliminate(first, inverses[0], lower)]
+        half = row_span // 2
+        widths = [half // 2, half // 2, half, half, half // 2, half // 2]
         lines = jnp.arange(n_row)
         turned = jnp.where(col_index == 0, lines > 0, lines == n_row - 1).astype(jnp.int32)
-        starts = width * jnp.stack(
+        mine_half = half * (2 * turned + col_index)
+        starts = jnp.stack(
             [
-                2 * turned + col_index,
-                2 * turned + 1 - col_index,
-                2 - 2 * turned + col_index,
-                3 - 2 * turned - col_index,
+                mine_half,
+                mine_half + half // 2,
+                half * (2 * turned + 1 - col_index),
+                half * (2 - 2 * turned + col_index),
+                half * (3 - 2 * turned - col_index),
+                half * (3 - 2 * turned - col_index) + half // 2,
             ],
             axis=1,
         )
@@ -406,28 +437,36 @@
         share = row_span // n_col
         own_rows = lax.dynamic_slice_in_dim(mine, col_index * share, share, 0)
         factor = lax.all_gather(own_rows, ("row", "col"), axis=0, tiled=True)
-        theirs = [lax.dynamic_slice_in_dim(factor, col_index * col_span, col_span, 0)]
-        second = None
-        starts = jnp.broadcast_to(jnp.arange(chunks) * width, (n_row, chunks))
+        whole = lax.dynamic_slice_in_dim(factor, col_index * col_span, col_span, 0)
+        widths = [col_span // CHUNKS] * CHUNKS
+        starts = jnp.broadcast_to(jnp.arange(CHUNKS) * widths[0], (n_row, CHUNKS))
+    chunks = len(widths)
     my_starts = lax.dynamic_index_in_dim(starts, row_index, 0, keepdims=False)
 
     slot_rows = owner[row_tiles].reshape(groups, tile_rows)
-    plan = row_plan(slot_rows, rows_per_group, groups, ADJACENT)
+    kinds = [(1, ROW_CAP)] + [
+        (n_row * other, FRONT_CAPS[(other - 1) % len(FRONT_CAPS)]) for other in range(1, n_front)
+    ]
+    plan = row_plan(slot_rows, rows_per_group, groups, kinds)
     held = lambda table: lax.dynamic_index_in_dim(table, me, 1, keepdims=False)
     my_group = held(plan["to_group"])
     my_order = held(plan["order"])
-    near_index = jnp.sum(
-        (held(plan["near"])[None, :] & (my_order[None, :] == jnp.arange(ADJACENT)[:, None])).astype(
-            jnp.int32
-        )
-        * jnp.arange(groups),
-        axis=-1,
-    )
+    my_kind = held(plan["kind"])
+    near_index = [
+        jnp.sum(
+            (
+                (my_kind == index + 1)[None, :] & (my_order[None, :] == jnp.arange(room)[:, None])
+            ).astype(jnp.int32)
+            * jnp.arange(groups),
+            axis=-1,
+        )
+        for index, (_, room) in enumerate(kinds)
+    ]
     for_me = plan["to_group"] == me
-    code = jnp.where(
-        ~plan["astray"],
+    code = groups * plan["kind"] + jnp.where(
+        plan["kind"] == 0,
         jnp.arange(groups)[:, None],
-        jnp.where(plan["near"], groups + plan["order"], 2 * groups + plan["far_place"]),
+        jnp.where(plan["far"], plan["far_place"], plan["order"]),
     )
     hit = for_me[:, :, None] & (plan["to_within"][:, :, None] == jnp.arange(rows_per_group))
     row_code = (
@@ -477,28 +516,33 @@
             my_starts,
         ]
     ).astype(jnp.int32)
-    neighbours = [(g, g ^ 1) for g in range(groups)]
+
+    def across(rows, step):
+        return lax.ppermute(rows, FR, [(g, g ^ step) for g in range(groups)])
 
     def settle(received):
-        picked = jnp.take(received, near_index, axis=0, mode="clip")
-        return picked, lax.ppermute(picked, FR, neighbours)
+        picked, moved = [], []
+        for index, (step, _) in enumerate(kinds):
+            picked.append(jnp.take(received, near_index[index], axis=0, mode="clip"))
+            moved.append(across(picked[-1], step))
+        return picked, moved
 
     sent, recv, near, picks = [], [], [], []
     for chunk in range(chunks):
-        per_part = chunks if second is None else 1
-        piece = update_chunk(
-            mine,
-            theirs[chunk // per_part],
-            (chunk % per_part) * width,
-            contrib[0],
-            scalars,
-            chunk,
-            width,
-            groups,
-        )
-        if chunk == 0 and second is not None:
-            theirs.append(eliminate(second(piece), inverses[0], lower))
-            theirs += [eliminate(part, inverses[0], lower) for part in others(theirs[1])]
+        offset = 0
+        if not by_hops:
+            theirs, offset = whole, chunk * widths[0]
+        elif chunk < 2:
+            theirs = eliminate(first(chunk, sent[-1] if sent else None), inverses[0], lower)
+        elif chunk == 2:
+            theirs = eliminate(second(sent[-1]), inverses[0], lower)
+            later = [eliminate(part, inverses[0], lower) for part in others(theirs)]
+        elif chunk == 3:
+            theirs = later[0]
+        else:
+            theirs, offset = later[1], (chunk - 4) * widths[chunk]
+        width = widths[chunk]
+        piece = update_chunk(mine, theirs, offset, contrib[0], scalars, chunk, width, groups)
         if chunk >= 2:
             piece, picks[chunk - 2] = lax.optimization_barrier((piece, picks[chunk - 2]))
         sent.append(piece)
@@ -506,6 +550,8 @@
         picked, moved = settle(recv[chunk])
         picks.append(picked)
         near.append(moved)
+
+    near = [[moved[index] for moved in near] for index in range(len(kinds))]
 
     cross_span = (tile_cols + 1) * TILE
 
@@ -518,9 +564,10 @@
             pick = None
             for chunk in range(chunks):
                 local = column - my_starts[chunk] // TILE
-                inside = (local >= 0) & (local < width // TILE)
+                most = widths[chunk] // TILE - 1
+                inside = (local >= 0) & (local <= most)
                 part = lax.dynamic_slice_in_dim(
-                    sent[chunk], jnp.clip(local, 0, width // TILE - 1) * TILE, TILE, 2
+                    sent[chunk], jnp.clip(local, 0, most) * TILE, TILE, 2
                 )
                 pick = part if pick is None else jnp.where(inside, part, pick)
             picks.append(pick)
@@ -538,7 +585,7 @@
         return (turn + 1, buffer)
 
     cross_rounds, _ = lax.optimization_barrier((cross_rounds, recv[-1]))
-    far_rounds, _ = lax.optimization_barrier((plan["rounds"], recv[-1]))
+    far_rounds, _ = lax.optimization_barrier((jnp.cumsum(plan["rounds"]), recv[-1]))
     crossed = unwritten((groups, TILE, cross_span), contrib.dtype)
     _, crossed = lax.while_loop(
         lambda state: state[0] < cross_rounds, cross_round, (jnp.int32(0), crossed)
@@ -557,7 +604,7 @@
             jnp.int32(0),
             crossed,
             unwritten((groups, TILE, cross_span), contrib.dtype),
-            unwritten((ADJACENT, TILE, cross_span), contrib.dtype),
+            [unwritten((room, TILE, cross_span), contrib.dtype) for _, room in kinds],
         ),
     )
 
@@ -566,31 +613,36 @@
 
     def far_exchange(state):
         turn, buffer = state
-        chosen = (
-            my_far[None, :]
-            & (my_far_round[None, :] == turn)
-            & (my_group[None, :] == jnp.arange(groups)[:, None])
-        )
-        index = jnp.sum(chosen.astype(jnp.int32) * jnp.arange(groups), axis=-1)
-        rows = jnp.concatenate(
-            [jnp.take(part, index, axis=0, mode="clip") for part in recv + [cross_recv]], axis=2
-        )
-        arrived = lax.all_to_all(rows, FR, split_axis=0, concat_axis=0, tiled=True)
-        coming = plan["far"] & for_me & (plan["far_round"] == turn)
+        step = count(far_rounds <= turn)
+        turn_of = turn - jnp.where(step > 0, far_rounds[jnp.maximum(step - 1, 0)], 0)
+        chosen = my_far & (my_far_round == turn_of) & (my_group == (me ^ step))
+        index = jnp.sum(chosen.astype(jnp.int32) * jnp.arange(groups))
+        row = jnp.concatenate(
+            [
+                lax.dynamic_slice_in_dim(part, index, 1, 0)
+                for part in recv + [cross_recv]
+            ],
+            axis=2,
+        )
+        arrived = lax.switch(
+            step - 1,
+            [lambda row, step=step: across(row, step) for step in range(1, groups)],
+            row,
+        )
+        coming = (
+            plan["far"]
+            & for_me
+            & (plan["far_round"] == turn_of)
+            & (jnp.arange(groups)[None, :] == (me ^ step))
+        )
         place = jnp.where(
-            jnp.any(coming, axis=0),
-            jnp.sum(jnp.where(coming, plan["far_place"], 0), axis=0),
-            groups,
-        )
-        for holder in range(groups):
-            buffer = lax.dynamic_update_slice_in_dim(
-                buffer, arrived[holder : holder + 1], place[holder], 0
-            )
-        return (turn + 1, buffer)
+            jnp.any(coming), jnp.sum(jnp.where(coming, plan["far_place"], 0)), groups
+        )
+        return (turn + 1, lax.dynamic_update_slice_in_dim(buffer, arrived, place, 0))
 
     far = unwritten((groups + 1, TILE, col_span + cross_span), contrib.dtype)
     _, far = lax.while_loop(
-        lambda state: state[0] < far_rounds, far_exchange, (jnp.int32(0), far)
+        lambda state: state[0] < far_rounds[-1], far_exchange, (jnp.int32(0), far)
     )
 
     schur, partial = assemble(
@@ -617,6 +669,10 @@
     return (schur, product)
 
 
+def takes_hops(n_row, n_col):
+    return n_row == 4 and n_col == 2
+
+
 def solution(mesh):
     in_specs = (
         P("front", None, None),

time: 791 us -> 834 us (1.054); the launches traced: 789 us -> 823 us
  waiting for transfers between devices: 555 us -> 400 us
  local copies, waits for them, and re-layouts: 30.8 us -> 112 us
  blocking collectives: 0 us -> 53.8 us
  starting transfers between devices: 69 us -> 95.1 us
  Pallas kernels: 94 us -> 107 us
  other arithmetic: 25.8 us -> 35 us
    ppermute x12 -> x39, waiting for transfers between devices: 423 us -> 252 us  [the longest x24 122 us: across(): return lax.ppermute(rows, FR, [(g, g ^ step) for g in range(groups)])]
    gather x4 -> x30, local copies, waits for them, and re-layouts: 16.8 us -> 83.3 us  [the longest x24 79.8 us: settle(): picked.append(jnp.take(received, near_index[index], axis=0, mode='clip'))]
    all_to_all x0 -> x1, blocking collectives: none -> 53.8 us  [shards(): lax.all_to_all(piece, FR, split_axis=0, concat_axis=0, tiled=True)]
    ppermute x12 -> x39, starting transfers between devices: 26.8 us -> 58.5 us  [the longest x6 27 us: collect_border(): below[p].append(lax.ppermute(below[p][-1], 'row', up))]
    all_to_all x4 -> x5, waiting for transfers between devices: 118 us -> 134 us  [shards(): lax.all_to_all(piece, FR, split_axis=0, concat_axis=0, tiled=True)]
    pallas_call x4 -> x6, Pallas kernels: 40.1 us -> 48.5 us  [update_chunk(): pl.pallas_call(lambda *refs: update_kernel(parts, *refs), out_shape=jax.S...]
    all_to_all x4 -> x5, starting transfers between devices: 40.7 us -> 34.7 us  [shards(): lax.all_to_all(piece, FR, split_axis=0, concat_axis=0, tiled=True)]
    pallas_call x5 -> x6, Pallas kernels: 28.8 us -> 31.8 us  [eliminate(): pl.pallas_call(rows_kernel, out_shape=jax.ShapeDtypeStruct(rows.shape, jn...]
  transfers between devices with their start and end apart: 17 -> 45, of which waited for: 15 -> 24; matrix products, arithmetic and copies ran while one was open for 5% -> 16% of each run, Pallas kernels for 7% -> 9%
where the time goes in v3:
time: 834 us; the launch traced here: 823 us
  waiting for transfers between devices  400 us (48%)
  local copies, waits for them, and re-layouts  112 us (13%)
  Pallas kernels  107 us (13%)
  starting transfers between devices  95.1 us (11%)
  blocking collectives  53.8 us (6%)
  other arithmetic  35 us (4%)
  between operations  17.8 us (2%)
    all_to_all x5, waiting for transfers between devices, shards(): lax.all_to_all(piece, FR, split_axis=0, concat_axis=0, tiled=True)  134 us
    ppermute x24, waiting for transfers between devices, across(): return lax.ppermute(rows, FR, [(g, g ^ step) for g in range(groups)])  122 us
    gather x24, local copies, waits for them, and re-layouts, settle(): picked.append(jnp.take(received, near_index[index], axis=0, mode='clip'))  79.8 us
    all_to_all x1, blocking collectives, shards(): lax.all_to_all(piece, FR, split_axis=0, concat_axis=0, tiled=True)  53.8 us
    pallas_call x6, Pallas kernels, update_chunk(): pl.pallas_call(lambda *refs: update_kernel(parts, *refs), out_shape=jax.S...  48.5 us
    ppermute x1, waiting for transfers between devices, others(): other = lax.ppermute(give, 'col', [(0, 1), (1, 0)])  46.4 us
    ppermute x6, waiting for transfers between devices, collect_border(): below[p].append(lax.ppermute(below[p][-1], 'row', up))  36.2 us
    all_to_all x5, starting transfers between devices, shards(): lax.all_to_all(piece, FR, split_axis=0, concat_axis=0, tiled=True)  34.7 us
  transfers between devices with their start and end apart: 45, of which 24 were waited for; matrix products, arithmetic and copies ran while one was open for 16% of the time, Pallas kernels for 9%

profile of v3, /device:TPU:0, one launch (start us, length us, event | category | flops | bytes accessed | tf_op | source)
XLA Modules:
  0.0 822.8 jit_solution(2278742234729619643)
XLA Ops:
  3.8 5.0 collective-permute-start.19
  11.4 5.2 collective-permute-start.25
  25.7 6.9 collective-permute-done.19
  32.6 5.3 collective-permute-start.20
  43.8 7.9 eliminate.6
  51.7 7.6 collective-permute-done.23
  60.7 5.5 collective-permute-start.26
  68.2 9.2 %collective-permute-done.20 = bf16[512,1024]{1,0:T(8,128)(2,1)} collective-permute-done((bf16[512,1024]{1,0:T(8,128)(2,1)S(1)}, bf16[512,1024]{1,0:T(8,128)(2,1)}, u32[]{:S(2)}, u32[]{:S(2)}) %collective-permute-start.20) | collective-permute-done | bytes 1048608 | tf_op jit(solution)/shard_map/ppermute | solution.py:103
  77.4 4.6 collective-permute-done.22
  85.2 4.1 eliminate.7.refs_5_
  89.3 7.4 update.6
  96.7 6.3 collective-permute-done.24
  106.4 4.2 eliminate.8.refs_5_
  110.5 6.4 update.7
  117.0 53.8 %all_to_all.45.refs_1_ = bf16[16,128,512]{2,1,0:T(8,128)(2,1)} all-to-all(bf16[16,128,512]{2,1,0:T(8,128)(2,1)S(1)} %update.7), channel_id=1, replica_groups=mesh['front'=4,'row'=4,'col'=2] {'front','row'}, dimensions={0} | all-to-all | bytes 4194304 | tf_op jit(solution)/shard_map/all_to_all | solution.py:549
  170.7 4.4 all-to-all-start.5
  175.7 4.7 collective-permute-start.28
  185.1 4.6 collective-permute-start.29
  192.4 10.8 %collective-permute-done.28 = bf16[512,1024]{1,0:T(8,128)(2,1)} collective-permute-done((bf16[512,1024]{1,0:T(8,128)(2,1)}, bf16[512,1024]{1,0:T(8,128)(2,1)}, u32[]{:S(2)}, u32[]{:S(2)}) %collective-permute-start.28) | collective-permute-done | bytes 1048608 | tf_op jit(solution)/shard_map/ppermute | solution.py:112
  207.3 17.7 %collective-permute-done.27 = bf16[512,1024]{1,0:T(8,128)(2,1)} collective-permute-done((bf16[512,1024]{1,0:T(8,128)(2,1)}, bf16[512,1024]{1,0:T(8,128)(2,1)}, u32[]{:S(2)}, u32[]{:S(2)}) %collective-permute-start.27) | collective-permute-done | bytes 1048608 | tf_op jit(solution)/shard_map/ppermute | solution.py:112
  225.0 4.7 maximum_select_fusion.rows
  229.6 5.2 eliminate.9.refs_5_
  234.9 20.1 %collective-permute-done.30 = bf16[512,1024]{1,0:T(8,128)(2,1)S(1)} collective-permute-done((bf16[512,1024]{1,0:T(8,128)(2,1)}, bf16[512,1024]{1,0:T(8,128)(2,1)S(1)}, u32[]{:S(2)}, u32[]{:S(2)}) %collective-permute-start.30) | collective-permute-done | bytes 1048608 | tf_op jit(solution)/shard_map/ppermute | solution.py:103
  264.5 5.2 eliminate.11.refs_5_
  269.7 10.0 %update.9 = bf16[16,128,1024]{2,1,0:T(8,128)(2,1)} custom-call(s32[22]{0:T(128)} %pad_add_fusion.refs_0_, bf16[16,128,1024]{2,1,0:T(8,128)(2,1)} %bitcast.153, bf16[16,128,1024]{2,1,0:T(8,128)(2,1)} %bitcast.151, bf16[16,128,1024]{2,1,0:T(8,128)(2,1)} %bitcast.152, bf16[16,128,1024]{2,1,0:T(8,128)(2,1)} %bitcast.150, bf16[1024,1024]{1,0:T(8,128)(2,1)} %eliminate.11.refs_5_, ...), custom_call_target="tpu_custom_call" | custom-call | tf_op jit(solution)/shard_map/update/pallas_call | solution.py:250
  291.8 16.7 %all-to-all-start.3 = ((bf16[16,128,1024]{2,1,0:T(8,128)(2,1)}), bf16[16,128,1024]{2,1,0:T(8,128)(2,1)}, u32[]{:S(2)}, u32[]{:S(2)}) async-start(bf16[16,128,1024]{2,1,0:T(8,128)(2,1)} %update.9), calls=%async_computation.3 | async-start | bytes 8388608 | tf_op jit(solution)/shard_map/all_to_all | solution.py:549
  308.5 10.0 %update.10 = bf16[16,128,1024]{2,1,0:T(8,128)(2,1)} custom-call(s32[22]{0:T(128)} %pad_add_fusion.refs_0_, bf16[16,128,1024]{2,1,0:T(8,128)(2,1)} %bitcast.154, bf16[16,128,1024]{2,1,0:T(8,128)(2,1)} %bitcast.155, bf16[16,128,1024]{2,1,0:T(8,128)(2,1)} %bitcast.156, bf16[16,128,1024]{2,1,0:T(8,128)(2,1)} %bitcast.157, bf16[1024,1024]{1,0:T(8,128)(2,1)} %eliminate.9.refs_5_, ...), custom_call_target="tpu_custom_call" | custom-call | tf_op jit(solution)/shard_map/update/pallas_call | solution.py:250
  330.6 72.2 %all-to-all-done.3.refs_3_ = bf16[16,128,1024]{2,1,0:T(8,128)(2,1)} async-done(((bf16[16,128,1024]{2,1,0:T(8,128)(2,1)}), bf16[16,128,1024]{2,1,0:T(8,128)(2,1)}, u32[]{:S(2)}, u32[]{:S(2)}) %all-to-all-start.3) | async-done | bytes 4194336 | tf_op jit(solution)/shard_map/all_to_all | solution.py:549
  402.8 4.5 all-to-all-start.6
  411.0 46.4 %collective-permute-done.33.rows = bf16[1024,1024]{1,0:T(8,128)(2,1)} collective-permute-done((bf16[1024,1024]{1,0:T(8,128)(2,1)S(1)}, bf16[1024,1024]{1,0:T(8,128)(2,1)}, u32[]{:S(2)}, u32[]{:S(2)}) %collective-permute-start.33) | collective-permute-done | bytes 2097184 | tf_op jit(solution)/shard_map/ppermute | solution.py:125
  457.4 5.2 eliminate.10.refs_5_
  462.6 7.4 update.8
  485.6 16.0 %all-to-all-done.6.refs_2_ = bf16[16,128,1024]{2,1,0:T(8,128)(2,1)} async-done(((bf16[16,128,1024]{2,1,0:T(8,128)(2,1)}), bf16[16,128,1024]{2,1,0:T(8,128)(2,1)}, u32[]{:S(2)}, u32[]{:S(2)}) %all-to-all-start.6) | async-done | bytes 4194336 | tf_op jit(solution)/shard_map/all_to_all | solution.py:549
  501.6 4.6 all-to-all-start.4
  528.0 7.4 update.11
  551.0 4.6 all-to-all-done.4.refs_5_
  556.9 4.4 all-to-all-start.7
  569.7 41.2 %all-to-all-done.7.refs_4_ = bf16[16,128,512]{2,1,0:T(8,128)(2,1)} async-done(((bf16[16,128,512]{2,1,0:T(8,128)(2,1)}), bf16[16,128,512]{2,1,0:T(8,128)(2,1)}, u32[]{:S(2)}, u32[]{:S(2)}) %all-to-all-start.7) | async-done | bytes 2097184 | tf_op jit(solution)/shard_map/all_to_all | solution.py:549
  614.3 10.4 %collective-permute-done.52.refs_24_ = bf16[3,128,512]{2,1,0:T(8,128)(2,1)} collective-permute-done((bf16[3,128,512]{2,1,0:T(8,128)(2,1)}, bf16[3,128,512]{2,1,0:T(8,128)(2,1)}, u32[]{:S(2)}, u32[]{:S(2)}) %collective-permute-start.52) | collective-permute-done | bytes 393248 | tf_op jit(solution)/shard_map/ppermute | solution.py:521
  625.5 10.0 %collective-permute-done.46.refs_18_ = bf16[4,128,512]{2,1,0:T(8,128)(2,1)S(1)} collective-permute-done((bf16[4,128,512]{2,1,0:T(8,128)(2,1)}, bf16[4,128,512]{2,1,0:T(8,128)(2,1)S(1)}, u32[]{:S(2)}, u32[]{:S(2)}) %collective-permute-start.46) | collective-permute-done | bytes 524320 | tf_op jit(solution)/shard_map/ppermute | solution.py:521
  638.1 6.0 collective-permute-done.34.refs_6_
  644.4 32.8 %collective-permute-done.54.refs_26_ = bf16[3,128,1024]{2,1,0:T(8,128)(2,1)S(1)} collective-permute-done((bf16[3,128,1024]{2,1,0:T(8,128)(2,1)}, bf16[3,128,1024]{2,1,0:T(8,128)(2,1)S(1)}, u32[]{:S(2)}, u32[]{:S(2)}) %collective-permute-start.54) | collective-permute-done | bytes 786464 | tf_op jit(solution)/shard_map/ppermute | solution.py:521
  678.8 15.3 %collective-permute-done.55.refs_27_ = bf16[3,128,1024]{2,1,0:T(8,128)(2,1)S(1)} collective-permute-done((bf16[3,128,1024]{2,1,0:T(8,128)(2,1)}, bf16[3,128,1024]{2,1,0:T(8,128)(2,1)S(1)}, u32[]{:S(2)}, u32[]{:S(2)}) %collective-permute-start.55) | collective-permute-done | bytes 786464 | tf_op jit(solution)/shard_map/ppermute | solution.py:521
  700.7 20.2 %collective-permute-done.49.refs_21_ = bf16[4,128,1024]{2,1,0:T(8,128)(2,1)} collective-permute-done((bf16[4,128,1024]{2,1,0:T(8,128)(2,1)}, bf16[4,128,1024]{2,1,0:T(8,128)(2,1)}, u32[]{:S(2)}, u32[]{:S(2)}) %collective-permute-start.49) | collective-permute-done | bytes 1048608 | tf_op jit(solution)/shard_map/ppermute | solution.py:521
  755.4 10.7 %collective-permute-done.51.refs_23_ = bf16[4,128,512]{2,1,0:T(8,128)(2,1)S(1)} collective-permute-done((bf16[4,128,512]{2,1,0:T(8,128)(2,1)}, bf16[4,128,512]{2,1,0:T(8,128)(2,1)S(1)}, u32[]{:S(2)}, u32[]{:S(2)}) %collective-permute-start.51) | collective-permute-done | bytes 524320 | tf_op jit(solution)/shard_map/ppermute | solution.py:521
  766.1 15.0 %collective-permute-done.39.refs_11_ = bf16[6,128,512]{2,1,0:T(8,128)(2,1)} collective-permute-done((bf16[6,128,512]{2,1,0:T(8,128)(2,1)}, bf16[6,128,512]{2,1,0:T(8,128)(2,1)}, u32[]{:S(2)}, u32[]{:S(2)}) %collective-permute-start.39) | collective-permute-done | bytes 786464 | tf_op jit(solution)/shard_map/ppermute | solution.py:521
  781.2 22.7 %assemble.1 = (f32[640,5120]{1,0:T(8,128)}, f32[640,512]{1,0:T(8,128)}) custom-call(s32[225]{0:T(256)} %concatenate.70.s, bf16[16,128,512]{2,1,0:T(8,128)(2,1)} %all-to-all-done.5.refs_0_, bf16[16,128,512]{2,1,0:T(8,128)(2,1)S(1)} %get-tuple-element.1794, bf16[16,128,1024]{2,1,0:T(8,128)(2,1)} %all-to-all-done.6.refs_2_, ...), custom_call_target="tpu_custom_call" | custom-call | tf_op jit(solution)/shard_map/assemble/pallas_call | solution.py:370
  806.9 13.7 %collective-permute-done.58 = f32[320,512]{1,0:T(8,128)S(1)} collective-permute-done((f32[320,512]{1,0:T(8,128)S(1)}, f32[320,512]{1,0:T(8,128)S(1)}, u32[]{:S(2)}, u32[]{:S(2)}) %collective-permute-start.58) | collective-permute-done | bytes 655392 | tf_op jit(solution)/shard_map/ppermute | solution.py:666
  (367 shorter events, 182.0 us)
Async XLA Ops:
  3.8 28.8 %collective-permute-start.19 = (bf16[512,1024]{1,0:T(8,128)(2,1)}, bf16[512,1024]{1,0:T(8,128)(2,1)S(1)}, u32[]{:S(2)}, u32[]{:S(2)}) collective-permute-start(bf16[512,1024]{1,0:T(8,128)(2,1)} %get-tuple-element.1201), channel_id=1, source_target_pairs={{0,2},{2,4},{4,6},{1,3},{3,5},{5,7},{8,10},{10,12},{12,14},{9,11},... | collective-permute-start | bytes 3145736 | tf_op jit(solution)/shard_map/ppermute | solution.py:103
  8.8 29.1 %collective-permute-start.21 = (bf16[512,1024]{1,0:T(8,128)(2,1)}, bf16[512,1024]{1,0:T(8,128)(2,1)}, u32[]{:S(2)}, u32[]{:S(2)}) collective-permute-start(bf16[512,1024]{1,0:T(8,128)(2,1)} %get-tuple-element.1201), channel_id=1, source_target_pairs={{2,0},{4,2},{6,4},{3,1},{5,3},{7,5},{10,8},{12,10},{14,12},{11,9},... | collective-permute-start | bytes 3145736 | tf_op jit(solution)/shard_map/ppermute | solution.py:104
  10.1 49.3 %collective-permute-start.23 = (bf16[512,1024]{1,0:T(8,128)(2,1)}, bf16[512,1024]{1,0:T(8,128)(2,1)S(1)}, u32[]{:S(2)}, u32[]{:S(2)}) collective-permute-start(bf16[512,1024]{1,0:T(8,128)(2,1)} %get-tuple-element.1202), channel_id=1, source_target_pairs={{2,0},{4,2},{6,4},{3,1},{5,3},{7,5},{10,8},{12,10},{14,12},{11,9},... | collective-permute-start | bytes 3145736 | tf_op jit(solution)/shard_map/ppermute | solution.py:104
  11.4 49.3 %collective-permute-start.25 = (bf16[512,1024]{1,0:T(8,128)(2,1)}, bf16[512,1024]{1,0:T(8,128)(2,1)S(1)}, u32[]{:S(2)}, u32[]{:S(2)}) collective-permute-start(bf16[512,1024]{1,0:T(8,128)(2,1)} %get-tuple-element.1202), channel_id=1, source_target_pairs={{0,2},{2,4},{4,6},{1,3},{3,5},{5,7},{8,10},{10,12},{12,14},{9,11},... | collective-permute-start | bytes 3145736 | tf_op jit(solution)/shard_map/ppermute | solution.py:103
  32.6 44.8 %collective-permute-start.20 = (bf16[512,1024]{1,0:T(8,128)(2,1)S(1)}, bf16[512,1024]{1,0:T(8,128)(2,1)}, u32[]{:S(2)}, u32[]{:S(2)}) collective-permute-start(bf16[512,1024]{1,0:T(8,128)(2,1)S(1)} %collective-permute-done.19), channel_id=1, source_target_pairs={{0,2},{2,4},{4,6},{1,3},{3,5},{5,7},{8,10},{10,12},{12,14},{9,11},... | collective-permute-start | bytes 3145736 | tf_op jit(solution)/shard_map/ppermute | solution.py:103
  37.8 44.1 %collective-permute-start.22 = (bf16[512,1024]{1,0:T(8,128)(2,1)}, bf16[512,1024]{1,0:T(8,128)(2,1)}, u32[]{:S(2)}, u32[]{:S(2)}) collective-permute-start(bf16[512,1024]{1,0:T(8,128)(2,1)} %collective-permute-done.21), channel_id=1, source_target_pairs={{2,0},{4,2},{6,4},{3,1},{5,3},{7,5},{10,8},{12,10},{14,12},{11,9},... | collective-permute-start | bytes 3145736 | tf_op jit(solution)/shard_map/ppermute | solution.py:104
  59.4 43.6 %collective-permute-start.24 = (bf16[512,1024]{1,0:T(8,128)(2,1)S(1)}, bf16[512,1024]{1,0:T(8,128)(2,1)}, u32[]{:S(2)}, u32[]{:S(2)}) collective-permute-start(bf16[512,1024]{1,0:T(8,128)(2,1)S(1)} %collective-permute-done.23), channel_id=1, source_target_pairs={{2,0},{4,2},{6,4},{3,1},{5,3},{7,5},{10,8},{12,10},{14,12},{11,9},... | collective-permute-start | bytes 3145736 | tf_op jit(solution)/shard_map/ppermute | solution.py:104
  60.7 42.3 %collective-permute-start.26 = (bf16[512,1024]{1,0:T(8,128)(2,1)S(1)}, bf16[512,1024]{1,0:T(8,128)(2,1)}, u32[]{:S(2)}, u32[]{:S(2)}) collective-permute-start(bf16[512,1024]{1,0:T(8,128)(2,1)S(1)} %collective-permute-done.25), channel_id=1, source_target_pairs={{0,2},{2,4},{4,6},{1,3},{3,5},{5,7},{8,10},{10,12},{12,14},{9,11},... | collective-permute-start | bytes 3145736 | tf_op jit(solution)/shard_map/ppermute | solution.py:103
  170.7 121.0 %all-to-all-start.5 = ((bf16[16,128,512]{2,1,0:T(8,128)(2,1)}), bf16[16,128,512]{2,1,0:T(8,128)(2,1)}, u32[]{:S(2)}, u32[]{:S(2)}) async-start(bf16[16,128,512]{2,1,0:T(8,128)(2,1)} %update.6), calls=%async_computation.5 | async-start | bytes 4194304 | tf_op jit(solution)/shard_map/all_to_all | solution.py:549
  175.7 27.6 %collective-permute-start.28 = (bf16[512,1024]{1,0:T(8,128)(2,1)}, bf16[512,1024]{1,0:T(8,128)(2,1)}, u32[]{:S(2)}, u32[]{:S(2)}) collective-permute-start(bf16[512,1024]{1,0:T(8,128)(2,1)} %get-tuple-element.1176), channel_id=1, source_target_pairs={{0,1},{2,3},{5,4},{7,6},{8,9},{10,11},{13,12},{15,14},{16,17},{18,... | collective-permute-start | bytes 3145736 | tf_op jit(solution)/shard_map/ppermute | solution.py:112
  182.8 42.2 %collective-permute-start.27 = (bf16[512,1024]{1,0:T(8,128)(2,1)}, bf16[512,1024]{1,0:T(8,128)(2,1)}, u32[]{:S(2)}, u32[]{:S(2)}) collective-permute-start(bf16[512,1024]{1,0:T(8,128)(2,1)} %get-tuple-element.1178), channel_id=1, source_target_pairs={{0,1},{2,3},{5,4},{7,6},{8,9},{10,11},{13,12},{15,14},{16,17},{18,... | collective-permute-start | bytes 3145736 | tf_op jit(solution)/shard_map/ppermute | solution.py:112
  185.1 49.8 %collective-permute-start.29 = (bf16[512,1024]{1,0:T(8,128)(2,1)}, bf16[512,1024]{1,0:T(8,128)(2,1)}, u32[]{:S(2)}, u32[]{:S(2)}) collective-permute-start(bf16[512,1024]{1,0:T(8,128)(2,1)} %collective-permute-done.20), channel_id=1, source_target_pairs={{0,2},{2,4},{4,6},{1,3},{3,5},{5,7},{8,10},{10,12},{12,14},{9,11},... | collective-permute-start | bytes 3145736 | tf_op jit(solution)/shard_map/ppermute | solution.py:103
  189.8 65.2 %collective-permute-start.30 = (bf16[512,1024]{1,0:T(8,128)(2,1)}, bf16[512,1024]{1,0:T(8,128)(2,1)S(1)}, u32[]{:S(2)}, u32[]{:S(2)}) collective-permute-start(bf16[512,1024]{1,0:T(8,128)(2,1)} %collective-permute-done.26), channel_id=1, source_target_pairs={{0,2},{2,4},{4,6},{1,3},{3,5},{5,7},{8,10},{10,12},{12,14},{9,11},... | collective-permute-start | bytes 3145736 | tf_op jit(solution)/shard_map/ppermute | solution.py:103
  191.1 63.9 %collective-permute-start.31 = (bf16[512,1024]{1,0:T(8,128)(2,1)}, bf16[512,1024]{1,0:T(8,128)(2,1)}, u32[]{:S(2)}, u32[]{:S(2)}) collective-permute-start(bf16[512,1024]{1,0:T(8,128)(2,1)} %collective-permute-done.22), channel_id=1, source_target_pairs={{2,0},{4,2},{6,4},{3,1},{5,3},{7,5},{10,8},{12,10},{14,12},{11,9},... | collective-permute-start | bytes 3145736 | tf_op jit(solution)/shard_map/ppermute | solution.py:104
  203.2 53.6 %collective-permute-start.32 = (bf16[512,1024]{1,0:T(8,128)(2,1)}, bf16[512,1024]{1,0:T(8,128)(2,1)}, u32[]{:S(2)}, u32[]{:S(2)}) collective-permute-start(bf16[512,1024]{1,0:T(8,128)(2,1)} %collective-permute-done.24), channel_id=1, source_target_pairs={{2,0},{4,2},{6,4},{3,1},{5,3},{7,5},{10,8},{12,10},{14,12},{11,9},... | collective-permute-start | bytes 3145736 | tf_op jit(solution)/shard_map/ppermute | solution.py:104
  205.9 333.5 %copy-start.48 = (s32[1024]{0:T(1024)}, s32[1024]{0:T(1024)S(1)}, u32[]{:S(2)}) copy-start(s32[1024]{0:T(1024)S(1)} %pad_clamp_fusion.6) | copy-start | bytes 12292
  206.6 336.9 %copy-start.45 = (s32[1024]{0:T(1024)}, s32[1024]{0:T(1024)S(1)}, u32[]{:S(2)}) copy-start(s32[1024]{0:T(1024)S(1)} %pad_clamp_fusion.5) | copy-start | bytes 12292
  207.3 340.0 %copy-start.46 = (s32[1024]{0:T(1024)}, s32[1024]{0:T(1024)S(1)}, u32[]{:S(2)}) copy-start(s32[1024]{0:T(1024)S(1)} %pad_clamp_fusion.4) | copy-start | bytes 12292
  291.8 111.0 %all-to-all-start.3 = ((bf16[16,128,1024]{2,1,0:T(8,128)(2,1)}), bf16[16,128,1024]{2,1,0:T(8,128)(2,1)}, u32[]{:S(2)}, u32[]{:S(2)}) async-start(bf16[16,128,1024]{2,1,0:T(8,128)(2,1)} %update.9), calls=%async_computation.3 | async-start | bytes 8388608 | tf_op jit(solution)/shard_map/all_to_all | solution.py:549
  402.8 98.8 %all-to-all-start.6 = ((bf16[16,128,1024]{2,1,0:T(8,128)(2,1)}), bf16[16,128,1024]{2,1,0:T(8,128)(2,1)}, u32[]{:S(2)}, u32[]{:S(2)}) async-start(bf16[16,128,1024]{2,1,0:T(8,128)(2,1)} %update.10), calls=%async_computation.6 | async-start | bytes 8388608 | tf_op jit(solution)/shard_map/all_to_all | solution.py:549
  409.5 48.0 %collective-permute-start.33 = (bf16[1024,1024]{1,0:T(8,128)(2,1)S(1)}, bf16[1024,1024]{1,0:T(8,128)(2,1)}, u32[]{:S(2)}, u32[]{:S(2)}) collective-permute-start(bf16[1024,1024]{1,0:T(8,128)(2,1)S(1)} %pad_maximum_fusion.1), channel_id=1, source_target_pairs={{0,1},{1,0},{2,3},{3,2},{4,5},{5,4},{6,7},{7,6},{8,9},{9,8},{10,11... | collective-permute-start | bytes 6291464 | tf_op jit(solution)/shard_map/ppermute | solution.py:125
  501.6 54.0 %all-to-all-start.4 = ((bf16[16,128,512]{2,1,0:T(8,128)(2,1)}), bf16[16,128,512]{2,1,0:T(8,128)(2,1)}, u32[]{:S(2)}, u32[]{:S(2)}) async-start(bf16[16,128,512]{2,1,0:T(8,128)(2,1)} %update.8), calls=%async_computation.4 | async-start | bytes 4194304 | tf_op jit(solution)/shard_map/all_to_all | solution.py:549
  556.9 53.9 %all-to-all-start.7 = ((bf16[16,128,512]{2,1,0:T(8,128)(2,1)}), bf16[16,128,512]{2,1,0:T(8,128)(2,1)}, u32[]{:S(2)}, u32[]{:S(2)}) async-start(bf16[16,128,512]{2,1,0:T(8,128)(2,1)} %get-tuple-element.1791), calls=%async_computation.7 | async-start | bytes 4194304 | tf_op jit(solution)/shard_map/all_to_all | solution.py:549
  566.1 70.3 %collective-permute-start.35 = (bf16[6,128,512]{2,1,0:T(8,128)(2,1)}, bf16[6,128,512]{2,1,0:T(8,128)(2,1)}, u32[]{:S(2)}, u32[]{:S(2)}) collective-permute-start(bf16[6,128,512]{2,1,0:T(8,128)(2,1)} %gather_fusion.12), channel_id=1, source_target_pairs={{0,2},{2,0},{4,6},{6,4},{8,10},{10,8},{12,14},{14,12},{16,18},{18,... | collective-permute-start | bytes 2359304 | tf_op jit(solution)/shard_map/ppermute | solution.py:521
  567.8 69.3 %collective-permute-start.41 = (bf16[6,128,512]{2,1,0:T(8,128)(2,1)}, bf16[6,128,512]{2,1,0:T(8,128)(2,1)}, u32[]{:S(2)}, u32[]{:S(2)}) collective-permute-start(bf16[6,128,512]{2,1,0:T(8,128)(2,1)} %gather_fusion.13), channel_id=1, source_target_pairs={{0,8},{2,10},{4,12},{6,14},{8,0},{10,2},{12,4},{14,6},{16,24},{18,... | collective-permute-start | bytes 2359304 | tf_op jit(solution)/shard_map/ppermute | solution.py:521
  567.8 56.9 %collective-permute-start.47 = (bf16[4,128,512]{2,1,0:T(8,128)(2,1)S(1)}, bf16[4,128,512]{2,1,0:T(8,128)(2,1)S(1)}, u32[]{:S(2)}, u32[]{:S(2)}) collective-permute-start(bf16[4,128,512]{2,1,0:T(8,128)(2,1)S(1)} %copy-done.23), channel_id=1, source_target_pairs={{0,16},{2,18},{4,20},{6,22},{8,24},{10,26},{12,28},{14,30},{16,0},... | collective-permute-start | bytes 1572872 | tf_op jit(solution)/shard_map/ppermute | solution.py:521
  569.3 44.2 %collective-permute-start.53 = (bf16[3,128,512]{2,1,0:T(8,128)(2,1)S(1)}, bf16[3,128,512]{2,1,0:T(8,128)(2,1)}, u32[]{:S(2)}, u32[]{:S(2)}) collective-permute-start(bf16[3,128,512]{2,1,0:T(8,128)(2,1)S(1)} %copy-done.24), channel_id=1, source_target_pairs={{0,24},{2,26},{4,28},{6,30},{8,16},{10,18},{12,20},{14,22},{16,8},... | collective-permute-start | bytes 1179656 | tf_op jit(solution)/shard_map/ppermute | solution.py:521
  612.9 11.8 %collective-permute-start.52 = (bf16[3,128,512]{2,1,0:T(8,128)(2,1)}, bf16[3,128,512]{2,1,0:T(8,128)(2,1)}, u32[]{:S(2)}, u32[]{:S(2)}) collective-permute-start(bf16[3,128,512]{2,1,0:T(8,128)(2,1)} %gather_fusion.23), channel_id=1, source_target_pairs={{0,24},{2,26},{4,28},{6,30},{8,16},{10,18},{12,20},{14,22},{16,8},... | collective-permute-start | bytes 1179656 | tf_op jit(solution)/shard_map/ppermute | solution.py:521
  613.5 22.0 %collective-permute-start.46 = (bf16[4,128,512]{2,1,0:T(8,128)(2,1)}, bf16[4,128,512]{2,1,0:T(8,128)(2,1)S(1)}, u32[]{:S(2)}, u32[]{:S(2)}) collective-permute-start(bf16[4,128,512]{2,1,0:T(8,128)(2,1)} %gather_fusion.22), channel_id=1, source_target_pairs={{0,16},{2,18},{4,20},{6,22},{8,24},{10,26},{12,28},{14,30},{16,0},... | collective-permute-start | bytes 1572872 | tf_op jit(solution)/shard_map/ppermute | solution.py:521
  624.7 19.4 %collective-permute-start.34 = (bf16[6,128,512]{2,1,0:T(8,128)(2,1)}, bf16[6,128,512]{2,1,0:T(8,128)(2,1)S(1)}, u32[]{:S(2)}, u32[]{:S(2)}) collective-permute-start(bf16[6,128,512]{2,1,0:T(8,128)(2,1)} %gather_fusion.20), channel_id=1, source_target_pairs={{0,2},{2,0},{4,6},{6,4},{8,10},{10,8},{12,14},{14,12},{16,18},{18,... | collective-permute-start | bytes 2359304 | tf_op jit(solution)/shard_map/ppermute | solution.py:521
  624.7 19.7 %collective-permute-start.40 = (bf16[6,128,512]{2,1,0:T(8,128)(2,1)}, bf16[6,128,512]{2,1,0:T(8,128)(2,1)S(1)}, u32[]{:S(2)}, u32[]{:S(2)}) collective-permute-start(bf16[6,128,512]{2,1,0:T(8,128)(2,1)} %gather_fusion.21), channel_id=1, source_target_pairs={{0,8},{2,10},{4,12},{6,14},{8,0},{10,2},{12,4},{14,6},{16,24},{18,... | collective-permute-start | bytes 2359304 | tf_op jit(solution)/shard_map/ppermute | solution.py:521
  635.5 58.6 %collective-permute-start.48 = (bf16[4,128,1024]{2,1,0:T(8,128)(2,1)}, bf16[4,128,1024]{2,1,0:T(8,128)(2,1)S(1)}, u32[]{:S(2)}, u32[]{:S(2)}) collective-permute-start(bf16[4,128,1024]{2,1,0:T(8,128)(2,1)} %gather_fusion.26), channel_id=1, source_target_pairs={{0,16},{2,18},{4,20},{6,22},{8,24},{10,26},{12,28},{14,30},{16,0},... | collective-permute-start | bytes 3145736 | tf_op jit(solution)/shard_map/ppermute | solution.py:521
  636.4 40.9 %collective-permute-start.54 = (bf16[3,128,1024]{2,1,0:T(8,128)(2,1)}, bf16[3,128,1024]{2,1,0:T(8,128)(2,1)S(1)}, u32[]{:S(2)}, u32[]{:S(2)}) collective-permute-start(bf16[3,128,1024]{2,1,0:T(8,128)(2,1)} %gather_fusion.27), channel_id=1, source_target_pairs={{0,24},{2,26},{4,28},{6,30},{8,16},{10,18},{12,20},{14,22},{16,8},... | collective-permute-start | bytes 2359304 | tf_op jit(solution)/shard_map/ppermute | solution.py:521
  637.2 56.9 %collective-permute-start.55 = (bf16[3,128,1024]{2,1,0:T(8,128)(2,1)}, bf16[3,128,1024]{2,1,0:T(8,128)(2,1)S(1)}, u32[]{:S(2)}, u32[]{:S(2)}) collective-permute-start(bf16[3,128,1024]{2,1,0:T(8,128)(2,1)} %gather_fusion.19), channel_id=1, source_target_pairs={{0,24},{2,26},{4,28},{6,30},{8,16},{10,18},{12,20},{14,22},{16,8},... | collective-permute-start | bytes 2359304 | tf_op jit(solution)/shard_map/ppermute | solution.py:521
  644.1 76.7 %collective-permute-start.36 = (bf16[6,128,1024]{2,1,0:T(8,128)(2,1)}, bf16[6,128,1024]{2,1,0:T(8,128)(2,1)}, u32[]{:S(2)}, u32[]{:S(2)}) collective-permute-start(bf16[6,128,1024]{2,1,0:T(8,128)(2,1)} %gather_fusion.24), channel_id=1, source_target_pairs={{0,2},{2,0},{4,6},{6,4},{8,10},{10,8},{12,14},{14,12},{16,18},{18,... | collective-permute-start | bytes 4718600 | tf_op jit(solution)/shard_map/ppermute | solution.py:521
  644.4 81.3 %collective-permute-start.42 = (bf16[6,128,1024]{2,1,0:T(8,128)(2,1)}, bf16[6,128,1024]{2,1,0:T(8,128)(2,1)}, u32[]{:S(2)}, u32[]{:S(2)}) collective-permute-start(bf16[6,128,1024]{2,1,0:T(8,128)(2,1)} %gather_fusion.25), channel_id=1, source_target_pairs={{0,8},{2,10},{4,12},{6,14},{8,0},{10,2},{12,4},{14,6},{16,24},{18,... | collective-permute-start | bytes 4718600 | tf_op jit(solution)/shard_map/ppermute | solution.py:521
  677.2 67.5 %collective-permute-start.43 = (bf16[6,128,1024]{2,1,0:T(8,128)(2,1)}, bf16[6,128,1024]{2,1,0:T(8,128)(2,1)}, u32[]{:S(2)}, u32[]{:S(2)}) collective-permute-start(bf16[6,128,1024]{2,1,0:T(8,128)(2,1)} %gather_fusion.17), channel_id=1, source_target_pairs={{0,8},{2,10},{4,12},{6,14},{8,0},{10,2},{12,4},{14,6},{16,24},{18,... | collective-permute-start | bytes 4718600 | tf_op jit(solution)/shard_map/ppermute | solution.py:521
  694.1 51.6 %collective-permute-start.37 = (bf16[6,128,1024]{2,1,0:T(8,128)(2,1)}, bf16[6,128,1024]{2,1,0:T(8,128)(2,1)}, u32[]{:S(2)}, u32[]{:S(2)}) collective-permute-start(bf16[6,128,1024]{2,1,0:T(8,128)(2,1)} %gather_fusion.16), channel_id=1, source_target_pairs={{0,2},{2,0},{4,6},{6,4},{8,10},{10,8},{12,14},{14,12},{16,18},{18,... | collective-permute-start | bytes 4718600 | tf_op jit(solution)/shard_map/ppermute | solution.py:521
  695.0 25.9 %collective-permute-start.49 = (bf16[4,128,1024]{2,1,0:T(8,128)(2,1)}, bf16[4,128,1024]{2,1,0:T(8,128)(2,1)}, u32[]{:S(2)}, u32[]{:S(2)}) collective-permute-start(bf16[4,128,1024]{2,1,0:T(8,128)(2,1)} %gather_fusion.18), channel_id=1, source_target_pairs={{0,16},{2,18},{4,20},{6,22},{8,24},{10,26},{12,28},{14,30},{16,0},... | collective-permute-start | bytes 3145736 | tf_op jit(solution)/shard_map/ppermute | solution.py:521
  720.8 24.9 %collective-permute-start.56 = (bf16[3,128,512]{2,1,0:T(8,128)(2,1)}, bf16[3,128,512]{2,1,0:T(8,128)(2,1)}, u32[]{:S(2)}, u32[]{:S(2)}) collective-permute-start(bf16[3,128,512]{2,1,0:T(8,128)(2,1)} %gather_fusion.34), channel_id=1, source_target_pairs={{0,24},{2,26},{4,28},{6,30},{8,16},{10,18},{12,20},{14,22},{16,8},... | collective-permute-start | bytes 1179656 | tf_op jit(solution)/shard_map/ppermute | solution.py:521
  720.9 26.0 %collective-permute-start.57 = (bf16[3,128,512]{2,1,0:T(8,128)(2,1)S(1)}, bf16[3,128,512]{2,1,0:T(8,128)(2,1)}, u32[]{:S(2)}, u32[]{:S(2)}) collective-permute-start(bf16[3,128,512]{2,1,0:T(8,128)(2,1)S(1)} %gather_fusion.35), channel_id=1, source_target_pairs={{0,24},{2,26},{4,28},{6,30},{8,16},{10,18},{12,20},{14,22},{16,8},... | collective-permute-start | bytes 1179656 | tf_op jit(solution)/shard_map/ppermute | solution.py:521
  725.7 26.2 %collective-permute-start.50 = (bf16[4,128,512]{2,1,0:T(8,128)(2,1)}, bf16[4,128,512]{2,1,0:T(8,128)(2,1)}, u32[]{:S(2)}, u32[]{:S(2)}) collective-permute-start(bf16[4,128,512]{2,1,0:T(8,128)(2,1)} %gather_fusion.32), channel_id=1, source_target_pairs={{0,16},{2,18},{4,20},{6,22},{8,24},{10,26},{12,28},{14,30},{16,0},... | collective-permute-start | bytes 1572872 | tf_op jit(solution)/shard_map/ppermute | solution.py:521
  744.7 21.4 %collective-permute-start.38 = (bf16[6,128,512]{2,1,0:T(8,128)(2,1)}, bf16[6,128,512]{2,1,0:T(8,128)(2,1)S(1)}, u32[]{:S(2)}, u32[]{:S(2)}) collective-permute-start(bf16[6,128,512]{2,1,0:T(8,128)(2,1)} %gather_fusion.28), channel_id=1, source_target_pairs={{0,2},{2,0},{4,6},{6,4},{8,10},{10,8},{12,14},{14,12},{16,18},{18,... | collective-permute-start | bytes 2359304 | tf_op jit(solution)/shard_map/ppermute | solution.py:521
  745.7 20.4 %collective-permute-start.44 = (bf16[6,128,512]{2,1,0:T(8,128)(2,1)}, bf16[6,128,512]{2,1,0:T(8,128)(2,1)}, u32[]{:S(2)}, u32[]{:S(2)}) collective-permute-start(bf16[6,128,512]{2,1,0:T(8,128)(2,1)} %gather_fusion.30), channel_id=1, source_target_pairs={{0,8},{2,10},{4,12},{6,14},{8,0},{10,2},{12,4},{14,6},{16,24},{18,... | collective-permute-start | bytes 2359304 | tf_op jit(solution)/shard_map/ppermute | solution.py:521
  745.7 35.5 %collective-permute-start.39 = (bf16[6,128,512]{2,1,0:T(8,128)(2,1)}, bf16[6,128,512]{2,1,0:T(8,128)(2,1)}, u32[]{:S(2)}, u32[]{:S(2)}) collective-permute-start(bf16[6,128,512]{2,1,0:T(8,128)(2,1)} %gather_fusion.29), channel_id=1, source_target_pairs={{0,2},{2,0},{4,6},{6,4},{8,10},{10,8},{12,14},{14,12},{16,18},{18,... | collective-permute-start | bytes 2359304 | tf_op jit(solution)/shard_map/ppermute | solution.py:521
  746.8 34.4 %collective-permute-start.45 = (bf16[6,128,512]{2,1,0:T(8,128)(2,1)}, bf16[6,128,512]{2,1,0:T(8,128)(2,1)}, u32[]{:S(2)}, u32[]{:S(2)}) collective-permute-start(bf16[6,128,512]{2,1,0:T(8,128)(2,1)} %gather_fusion.31), channel_id=1, source_target_pairs={{0,8},{2,10},{4,12},{6,14},{8,0},{10,2},{12,4},{14,6},{16,24},{18,... | collective-permute-start | bytes 2359304 | tf_op jit(solution)/shard_map/ppermute | solution.py:521
  751.9 14.2 %collective-permute-start.51 = (bf16[4,128,512]{2,1,0:T(8,128)(2,1)}, bf16[4,128,512]{2,1,0:T(8,128)(2,1)S(1)}, u32[]{:S(2)}, u32[]{:S(2)}) collective-permute-start(bf16[4,128,512]{2,1,0:T(8,128)(2,1)} %gather_fusion.33), channel_id=1, source_target_pairs={{0,16},{2,18},{4,20},{6,22},{8,24},{10,26},{12,28},{14,30},{16,0},... | collective-permute-start | bytes 1572872 | tf_op jit(solution)/shard_map/ppermute | solution.py:521
  805.0 15.5 %collective-permute-start.58 = (f32[320,512]{1,0:T(8,128)S(1)}, f32[320,512]{1,0:T(8,128)S(1)}, u32[]{:S(2)}, u32[]{:S(2)}) collective-permute-start(f32[320,512]{1,0:T(8,128)S(1)} %constant_dynamic-slice_fusion), channel_id=1, source_target_pairs={{0,1},{1,0},{2,3},{3,2},{4,5},{5,4},{6,7},{7,6},{8,9},{9,8},{10,11... | collective-permute-start | bytes 1966088 | tf_op jit(solution)/shard_map/ppermute | solution.py:666
  (53 other events, 1432.0 us)

commit v4 on v3

--- a/solution.py
+++ b/solution.py
@@ -63,7 +63,7 @@
 
 def eliminate(rows, inverse_set, lower):
     size, depth = rows.shape
-    step = min(size, 512)
+    step = min(size, 256)
     return pl.pallas_call(
         rows_kernel,
         out_shape=jax.ShapeDtypeStruct(rows.shape, jnp.bfloat16),
@@ -230,9 +230,9 @@
 
 
 def update_chunk(mine, theirs, first, contrib, scalars, chunk, width, groups):
-    parts = 4 if groups % 4 == 0 else 1
+    parts = 2
     depth = mine.shape[1]
-    block = min(width, 1024)
+    block = min(width, 512)
     steps = width // block
     tiles = mine.reshape(-1, TILE, depth)
     left_specs = [
@@ -296,7 +296,9 @@
 
         def moves(b, act):
             slot = b % 2
-            for f in range(fronts):
+
+            @pl.loop(0, fronts)
+            def _(f):
                 code = s[f * per_rows + b]
                 index = code % cap
                 source_row = s[from_base + f * per_rows + b]

time: 834 us -> 837 us (level)
  Pallas kernels: 107 us -> 137 us
  waiting for transfers between devices: 400 us -> 382 us
    pallas_call x6, Pallas kernels: 48.5 us -> 68.7 us  [update_chunk(): pl.pallas_call(lambda *refs: update_kernel(parts, *refs), out_shape=jax.S...]
    all_to_all x5, waiting for transfers between devices: 134 us -> 123 us  [shards(): lax.all_to_all(piece, FR, split_axis=0, concat_axis=0, tiled=True)]
    pallas_call x6, Pallas kernels: 31.8 us -> 41.6 us  [eliminate(): pl.pallas_call(rows_kernel, out_shape=jax.ShapeDtypeStruct(rows.shape, jn...]
  transfers between devices with their start and end apart: 45 -> 45, of which waited for: 24 -> 24; matrix products, arithmetic and copies ran while one was open for 16% -> 16% of each run, Pallas kernels for 9% -> 12%
where the time goes in v4:
time: 837 us; the launch traced here: 833 us
  waiting for transfers between devices  382 us (46%)
  Pallas kernels  137 us (16%)
  local copies, waits for them, and re-layouts  111 us (13%)
  starting transfers between devices  94.6 us (11%)
  blocking collectives  53.8 us (6%)
  other arithmetic  34.5 us (4%)
  between operations  17.4 us (2%)
    all_to_all x5, waiting for transfers between devices, shards(): lax.all_to_all(piece, FR, split_axis=0, concat_axis=0, tiled=True)  123 us
    ppermute x24, waiting for transfers between devices, across(): return lax.ppermute(rows, FR, [(g, g ^ step) for g in range(groups)])  122 us
    gather x24, local copies, waits for them, and re-layouts, settle(): picked.append(jnp.take(received, near_index[index], axis=0, mode='clip'))  79.8 us
    pallas_call x6, Pallas kernels, update_chunk(): pl.pallas_call(lambda *refs: update_kernel(parts, *refs), out_shape=jax.S...  68.7 us
    all_to_all x1, blocking collectives, shards(): lax.all_to_all(piece, FR, split_axis=0, concat_axis=0, tiled=True)  53.8 us
    ppermute x1, waiting for transfers between devices, others(): other = lax.ppermute(give, 'col', [(0, 1), (1, 0)])  46.4 us
    pallas_call x6, Pallas kernels, eliminate(): pl.pallas_call(rows_kernel, out_shape=jax.ShapeDtypeStruct(rows.shape, jn...  41.6 us
    ppermute x6, waiting for transfers between devices, collect_border(): below[p].append(lax.ppermute(below[p][-1], 'row', up))  35.1 us
  transfers between devices with their start and end apart: 45, of which 24 were waited for; matrix products, arithmetic and copies ran while one was open for 16% of the time, Pallas kernels for 12%

profile of v4, /device:TPU:0, one launch (start us, length us, event | category | flops | bytes accessed | tf_op | source)
XLA Modules:
  0.0 833.1 jit_solution(543506261372291447)
XLA Ops:
  3.8 5.0 collective-permute-start.19
  11.4 5.2 collective-permute-start.25
  25.1 7.4 collective-permute-done.19
  32.6 5.2 collective-permute-start.20
  43.7 11.4 %eliminate.6 = bf16[2048,1024]{1,0:T(8,128)(2,1)} custom-call(bf16[2048,1024]{1,0:T(8,128)(2,1)} %bitcast.149, bf16[4,256,256]{2,1,0:T(8,128)(2,1)} %bitcast.143, bf16[4,1024,256]{2,1,0:T(8,128)(2,1)} %pivot.1.lower), custom_call_target="tpu_custom_call" | custom-call | tf_op jit(solution)/shard_map/eliminate/pallas_call | solution.py:67
  55.2 4.2 collective-permute-done.23
  60.7 5.6 collective-permute-start.26
  68.3 9.1 %collective-permute-done.20 = bf16[512,1024]{1,0:T(8,128)(2,1)} collective-permute-done((bf16[512,1024]{1,0:T(8,128)(2,1)S(1)}, bf16[512,1024]{1,0:T(8,128)(2,1)}, u32[]{:S(2)}, u32[]{:S(2)}) %collective-permute-start.20) | collective-permute-done | bytes 1048608 | tf_op jit(solution)/shard_map/ppermute | solution.py:103
  77.4 4.6 collective-permute-done.22
  85.2 4.7 eliminate.7.refs_3_
  89.9 9.3 %update.6 = bf16[16,128,512]{2,1,0:T(8,128)(2,1)} custom-call(s32[22]{0:T(128)} %pad_add_fusion.refs_0_, bf16[16,128,1024]{2,1,0:T(8,128)(2,1)} %bitcast.130, bf16[16,128,1024]{2,1,0:T(8,128)(2,1)} %bitcast.131, bf16[512,1024]{1,0:T(8,128)(2,1)} %eliminate.7.refs_3_, bf16[2048,4096]{1,0:T(8,128)(2,1)} %bitcast.118, bf16[2048,4096]{1,0:T(8,128)(2,1)} %bitcast.119), custom_call_target="tpu_custom_call" | custom-call | tf_op jit(solution)/shard_map/update/pallas_call | solution.py:250
  106.4 4.7 eliminate.8.refs_3_
  111.1 8.3 update.7
  119.4 53.8 %all_to_all.45.refs_1_ = bf16[16,128,512]{2,1,0:T(8,128)(2,1)} all-to-all(bf16[16,128,512]{2,1,0:T(8,128)(2,1)S(1)} %update.7), channel_id=1, replica_groups=mesh['front'=4,'row'=4,'col'=2] {'front','row'}, dimensions={0} | all-to-all | bytes 4194304 | tf_op jit(solution)/shard_map/all_to_all | solution.py:551
  173.1 4.4 all-to-all-start.5
  178.1 4.7 collective-permute-start.28
  187.5 4.6 collective-permute-start.29
  194.8 10.8 %collective-permute-done.28 = bf16[512,1024]{1,0:T(8,128)(2,1)} collective-permute-done((bf16[512,1024]{1,0:T(8,128)(2,1)}, bf16[512,1024]{1,0:T(8,128)(2,1)}, u32[]{:S(2)}, u32[]{:S(2)}) %collective-permute-start.28) | collective-permute-done | bytes 1048608 | tf_op jit(solution)/shard_map/ppermute | solution.py:112
  209.4 18.0 %collective-permute-done.27 = bf16[512,1024]{1,0:T(8,128)(2,1)} collective-permute-done((bf16[512,1024]{1,0:T(8,128)(2,1)}, bf16[512,1024]{1,0:T(8,128)(2,1)}, u32[]{:S(2)}, u32[]{:S(2)}) %collective-permute-start.27) | collective-permute-done | bytes 1048608 | tf_op jit(solution)/shard_map/ppermute | solution.py:112
  227.4 4.6 maximum_select_fusion.rows
  231.9 7.0 eliminate.9.refs_3_
  238.9 18.5 %collective-permute-done.30 = bf16[512,1024]{1,0:T(8,128)(2,1)S(1)} collective-permute-done((bf16[512,1024]{1,0:T(8,128)(2,1)}, bf16[512,1024]{1,0:T(8,128)(2,1)S(1)}, u32[]{:S(2)}, u32[]{:S(2)}) %collective-permute-start.30) | collective-permute-done | bytes 1048608 | tf_op jit(solution)/shard_map/ppermute | solution.py:103
  267.0 6.9 eliminate.11.refs_3_
  273.9 16.4 %update.9 = bf16[16,128,1024]{2,1,0:T(8,128)(2,1)} custom-call(s32[22]{0:T(128)} %pad_add_fusion.refs_0_, bf16[16,128,1024]{2,1,0:T(8,128)(2,1)} %bitcast.134, bf16[16,128,1024]{2,1,0:T(8,128)(2,1)} %bitcast.135, bf16[1024,1024]{1,0:T(8,128)(2,1)} %eliminate.11.refs_3_, bf16[2048,4096]{1,0:T(8,128)(2,1)} %bitcast.122, bf16[2048,4096]{1,0:T(8,128)(2,1)} %bitcast.123), custom_call_target="tpu_custom_call" | custom-call | tf_op jit(solution)/shard_map/update/pallas_call | solution.py:250
  302.3 16.7 %all-to-all-start.3 = ((bf16[16,128,1024]{2,1,0:T(8,128)(2,1)}), bf16[16,128,1024]{2,1,0:T(8,128)(2,1)}, u32[]{:S(2)}, u32[]{:S(2)}) async-start(bf16[16,128,1024]{2,1,0:T(8,128)(2,1)} %update.9), calls=%async_computation.3 | async-start | bytes 8388608 | tf_op jit(solution)/shard_map/all_to_all | solution.py:551
  319.0 16.4 %update.10 = bf16[16,128,1024]{2,1,0:T(8,128)(2,1)} custom-call(s32[22]{0:T(128)} %pad_add_fusion.refs_0_, bf16[16,128,1024]{2,1,0:T(8,128)(2,1)} %bitcast.136, bf16[16,128,1024]{2,1,0:T(8,128)(2,1)} %bitcast.137, bf16[1024,1024]{1,0:T(8,128)(2,1)} %eliminate.9.refs_3_, bf16[2048,4096]{1,0:T(8,128)(2,1)} %bitcast.124, bf16[2048,4096]{1,0:T(8,128)(2,1)} %bitcast.125), custom_call_target="tpu_custom_call" | custom-call | tf_op jit(solution)/shard_map/update/pallas_call | solution.py:250
  347.5 65.8 %all-to-all-done.3.refs_3_ = bf16[16,128,1024]{2,1,0:T(8,128)(2,1)} async-done(((bf16[16,128,1024]{2,1,0:T(8,128)(2,1)}), bf16[16,128,1024]{2,1,0:T(8,128)(2,1)}, u32[]{:S(2)}, u32[]{:S(2)}) %all-to-all-start.3) | async-done | bytes 4194336 | tf_op jit(solution)/shard_map/all_to_all | solution.py:551
  413.4 4.5 all-to-all-start.6
  421.6 46.4 %collective-permute-done.33.rows = bf16[1024,1024]{1,0:T(8,128)(2,1)} collective-permute-done((bf16[1024,1024]{1,0:T(8,128)(2,1)S(1)}, bf16[1024,1024]{1,0:T(8,128)(2,1)}, u32[]{:S(2)}, u32[]{:S(2)}) %collective-permute-start.33) | collective-permute-done | bytes 2097184 | tf_op jit(solution)/shard_map/ppermute | solution.py:125
  468.0 6.9 eliminate.10.refs_3_
  474.9 9.2 %update.8 = bf16[16,128,512]{2,1,0:T(8,128)(2,1)} custom-call(s32[22]{0:T(128)} %pad_add_fusion.refs_0_, bf16[16,128,1024]{2,1,0:T(8,128)(2,1)} %bitcast.138, bf16[16,128,1024]{2,1,0:T(8,128)(2,1)} %bitcast.139, bf16[1024,1024]{1,0:T(8,128)(2,1)} %eliminate.10.refs_3_, bf16[2048,4096]{1,0:T(8,128)(2,1)} %bitcast.126, bf16[2048,4096]{1,0:T(8,128)(2,1)} %bitcast.127), custom_call_target="tpu_custom_call" | custom-call | tf_op jit(solution)/shard_map/update/pallas_call | solution.py:250
  492.0 4.1 gather_fusion.16
  499.7 12.4 %all-to-all-done.6.refs_2_ = bf16[16,128,1024]{2,1,0:T(8,128)(2,1)} async-done(((bf16[16,128,1024]{2,1,0:T(8,128)(2,1)}), bf16[16,128,1024]{2,1,0:T(8,128)(2,1)}, u32[]{:S(2)}, u32[]{:S(2)}) %all-to-all-start.6) | async-done | bytes 4194336 | tf_op jit(solution)/shard_map/all_to_all | solution.py:551
  512.2 4.4 all-to-all-start.4
  537.6 9.3 %update.11 = bf16[16,128,512]{2,1,0:T(8,128)(2,1)} custom-call(s32[22]{0:T(128)} %pad_add_fusion.refs_0_, bf16[16,128,1024]{2,1,0:T(8,128)(2,1)} %bitcast.140, bf16[16,128,1024]{2,1,0:T(8,128)(2,1)} %bitcast.141, bf16[1024,1024]{1,0:T(8,128)(2,1)} %eliminate.10.refs_3_, bf16[2048,4096]{1,0:T(8,128)(2,1)} %bitcast.128, bf16[2048,4096]{1,0:T(8,128)(2,1)} %bitcast.129), custom_call_target="tpu_custom_call" | custom-call | tf_op jit(solution)/shard_map/update/pallas_call | solution.py:250
  550.9 4.1 gather_fusion.25
  567.6 4.4 all-to-all-start.7
  580.4 41.2 %all-to-all-done.7.refs_4_ = bf16[16,128,512]{2,1,0:T(8,128)(2,1)} async-done(((bf16[16,128,512]{2,1,0:T(8,128)(2,1)}), bf16[16,128,512]{2,1,0:T(8,128)(2,1)}, u32[]{:S(2)}, u32[]{:S(2)}) %all-to-all-start.7) | async-done | bytes 2097184 | tf_op jit(solution)/shard_map/all_to_all | solution.py:551
  624.8 10.4 %collective-permute-done.52.refs_24_ = bf16[3,128,512]{2,1,0:T(8,128)(2,1)} collective-permute-done((bf16[3,128,512]{2,1,0:T(8,128)(2,1)}, bf16[3,128,512]{2,1,0:T(8,128)(2,1)}, u32[]{:S(2)}, u32[]{:S(2)}) %collective-permute-start.52) | collective-permute-done | bytes 393248 | tf_op jit(solution)/shard_map/ppermute | solution.py:523
  636.1 10.0 %collective-permute-done.46.refs_18_ = bf16[4,128,512]{2,1,0:T(8,128)(2,1)S(1)} collective-permute-done((bf16[4,128,512]{2,1,0:T(8,128)(2,1)}, bf16[4,128,512]{2,1,0:T(8,128)(2,1)S(1)}, u32[]{:S(2)}, u32[]{:S(2)}) %collective-permute-start.46) | collective-permute-done | bytes 524320 | tf_op jit(solution)/shard_map/ppermute | solution.py:523
  648.7 6.0 collective-permute-done.34.refs_6_
  655.0 32.8 %collective-permute-done.54.refs_26_ = bf16[3,128,1024]{2,1,0:T(8,128)(2,1)S(1)} collective-permute-done((bf16[3,128,1024]{2,1,0:T(8,128)(2,1)}, bf16[3,128,1024]{2,1,0:T(8,128)(2,1)S(1)}, u32[]{:S(2)}, u32[]{:S(2)}) %collective-permute-start.54) | collective-permute-done | bytes 786464 | tf_op jit(solution)/shard_map/ppermute | solution.py:523
  689.4 15.3 %collective-permute-done.55.refs_27_ = bf16[3,128,1024]{2,1,0:T(8,128)(2,1)S(1)} collective-permute-done((bf16[3,128,1024]{2,1,0:T(8,128)(2,1)}, bf16[3,128,1024]{2,1,0:T(8,128)(2,1)S(1)}, u32[]{:S(2)}, u32[]{:S(2)}) %collective-permute-start.55) | collective-permute-done | bytes 786464 | tf_op jit(solution)/shard_map/ppermute | solution.py:523
  711.2 20.2 %collective-permute-done.49.refs_21_ = bf16[4,128,1024]{2,1,0:T(8,128)(2,1)} collective-permute-done((bf16[4,128,1024]{2,1,0:T(8,128)(2,1)}, bf16[4,128,1024]{2,1,0:T(8,128)(2,1)}, u32[]{:S(2)}, u32[]{:S(2)}) %collective-permute-start.49) | collective-permute-done | bytes 1048608 | tf_op jit(solution)/shard_map/ppermute | solution.py:523
  766.0 10.7 %collective-permute-done.51.refs_23_ = bf16[4,128,512]{2,1,0:T(8,128)(2,1)S(1)} collective-permute-done((bf16[4,128,512]{2,1,0:T(8,128)(2,1)}, bf16[4,128,512]{2,1,0:T(8,128)(2,1)S(1)}, u32[]{:S(2)}, u32[]{:S(2)}) %collective-permute-start.51) | collective-permute-done | bytes 524320 | tf_op jit(solution)/shard_map/ppermute | solution.py:523
  776.7 15.0 %collective-permute-done.39.refs_11_ = bf16[6,128,512]{2,1,0:T(8,128)(2,1)} collective-permute-done((bf16[6,128,512]{2,1,0:T(8,128)(2,1)}, bf16[6,128,512]{2,1,0:T(8,128)(2,1)}, u32[]{:S(2)}, u32[]{:S(2)}) %collective-permute-start.39) | collective-permute-done | bytes 786464 | tf_op jit(solution)/shard_map/ppermute | solution.py:523
  791.7 22.6 %assemble.1 = (f32[640,5120]{1,0:T(8,128)}, f32[640,512]{1,0:T(8,128)}) custom-call(s32[225]{0:T(256)} %concatenate.70.s, bf16[16,128,512]{2,1,0:T(8,128)(2,1)} %all-to-all-done.5.refs_0_, bf16[16,128,512]{2,1,0:T(8,128)(2,1)S(1)} %get-tuple-element.1794, bf16[16,128,1024]{2,1,0:T(8,128)(2,1)} %all-to-all-done.6.refs_2_, ...), custom_call_target="tpu_custom_call" | custom-call | tf_op jit(solution)/shard_map/assemble/pallas_call | solution.py:372
  817.4 13.7 %collective-permute-done.58 = f32[320,512]{1,0:T(8,128)S(1)} collective-permute-done((f32[320,512]{1,0:T(8,128)S(1)}, f32[320,512]{1,0:T(8,128)S(1)}, u32[]{:S(2)}, u32[]{:S(2)}) %collective-permute-start.58) | collective-permute-done | bytes 655392 | tf_op jit(solution)/shard_map/ppermute | solution.py:668
  (365 shorter events, 180.0 us)
Async XLA Ops:
  3.8 28.8 %collective-permute-start.19 = (bf16[512,1024]{1,0:T(8,128)(2,1)}, bf16[512,1024]{1,0:T(8,128)(2,1)S(1)}, u32[]{:S(2)}, u32[]{:S(2)}) collective-permute-start(bf16[512,1024]{1,0:T(8,128)(2,1)} %get-tuple-element.1201), channel_id=1, source_target_pairs={{0,2},{2,4},{4,6},{1,3},{3,5},{5,7},{8,10},{10,12},{12,14},{9,11},... | collective-permute-start | bytes 3145736 | tf_op jit(solution)/shard_map/ppermute | solution.py:103
  8.8 29.0 %collective-permute-start.21 = (bf16[512,1024]{1,0:T(8,128)(2,1)}, bf16[512,1024]{1,0:T(8,128)(2,1)}, u32[]{:S(2)}, u32[]{:S(2)}) collective-permute-start(bf16[512,1024]{1,0:T(8,128)(2,1)} %get-tuple-element.1201), channel_id=1, source_target_pairs={{2,0},{4,2},{6,4},{3,1},{5,3},{7,5},{10,8},{12,10},{14,12},{11,9},... | collective-permute-start | bytes 3145736 | tf_op jit(solution)/shard_map/ppermute | solution.py:104
  10.1 49.3 %collective-permute-start.23 = (bf16[512,1024]{1,0:T(8,128)(2,1)}, bf16[512,1024]{1,0:T(8,128)(2,1)S(1)}, u32[]{:S(2)}, u32[]{:S(2)}) collective-permute-start(bf16[512,1024]{1,0:T(8,128)(2,1)} %get-tuple-element.1202), channel_id=1, source_target_pairs={{2,0},{4,2},{6,4},{3,1},{5,3},{7,5},{10,8},{12,10},{14,12},{11,9},... | collective-permute-start | bytes 3145736 | tf_op jit(solution)/shard_map/ppermute | solution.py:104
  11.4 49.3 %collective-permute-start.25 = (bf16[512,1024]{1,0:T(8,128)(2,1)}, bf16[512,1024]{1,0:T(8,128)(2,1)S(1)}, u32[]{:S(2)}, u32[]{:S(2)}) collective-permute-start(bf16[512,1024]{1,0:T(8,128)(2,1)} %get-tuple-element.1202), channel_id=1, source_target_pairs={{0,2},{2,4},{4,6},{1,3},{3,5},{5,7},{8,10},{10,12},{12,14},{9,11},... | collective-permute-start | bytes 3145736 | tf_op jit(solution)/shard_map/ppermute | solution.py:103
  32.6 44.8 %collective-permute-start.20 = (bf16[512,1024]{1,0:T(8,128)(2,1)S(1)}, bf16[512,1024]{1,0:T(8,128)(2,1)}, u32[]{:S(2)}, u32[]{:S(2)}) collective-permute-start(bf16[512,1024]{1,0:T(8,128)(2,1)S(1)} %collective-permute-done.19), channel_id=1, source_target_pairs={{0,2},{2,4},{4,6},{1,3},{3,5},{5,7},{8,10},{10,12},{12,14},{9,11},... | collective-permute-start | bytes 3145736 | tf_op jit(solution)/shard_map/ppermute | solution.py:103
  37.8 44.2 %collective-permute-start.22 = (bf16[512,1024]{1,0:T(8,128)(2,1)}, bf16[512,1024]{1,0:T(8,128)(2,1)}, u32[]{:S(2)}, u32[]{:S(2)}) collective-permute-start(bf16[512,1024]{1,0:T(8,128)(2,1)} %collective-permute-done.21), channel_id=1, source_target_pairs={{2,0},{4,2},{6,4},{3,1},{5,3},{7,5},{10,8},{12,10},{14,12},{11,9},... | collective-permute-start | bytes 3145736 | tf_op jit(solution)/shard_map/ppermute | solution.py:104
  59.4 43.6 %collective-permute-start.24 = (bf16[512,1024]{1,0:T(8,128)(2,1)S(1)}, bf16[512,1024]{1,0:T(8,128)(2,1)}, u32[]{:S(2)}, u32[]{:S(2)}) collective-permute-start(bf16[512,1024]{1,0:T(8,128)(2,1)S(1)} %collective-permute-done.23), channel_id=1, source_target_pairs={{2,0},{4,2},{6,4},{3,1},{5,3},{7,5},{10,8},{12,10},{14,12},{11,9},... | collective-permute-start | bytes 3145736 | tf_op jit(solution)/shard_map/ppermute | solution.py:104
  60.7 42.3 %collective-permute-start.26 = (bf16[512,1024]{1,0:T(8,128)(2,1)S(1)}, bf16[512,1024]{1,0:T(8,128)(2,1)}, u32[]{:S(2)}, u32[]{:S(2)}) collective-permute-start(bf16[512,1024]{1,0:T(8,128)(2,1)S(1)} %collective-permute-done.25), channel_id=1, source_target_pairs={{0,2},{2,4},{4,6},{1,3},{3,5},{5,7},{8,10},{10,12},{12,14},{9,11},... | collective-permute-start | bytes 3145736 | tf_op jit(solution)/shard_map/ppermute | solution.py:103
  66.4 452.4 %copy-start.49 = (s32[4,6]{1,0:T(4,128)}, s32[4,6]{1,0:T(4,128)S(1)}, u32[]{:S(2)}) copy-start(s32[4,6]{1,0:T(4,128)S(1)} %stack.27) | copy-start | bytes 292
  173.1 129.2 %all-to-all-start.5 = ((bf16[16,128,512]{2,1,0:T(8,128)(2,1)}), bf16[16,128,512]{2,1,0:T(8,128)(2,1)}, u32[]{:S(2)}, u32[]{:S(2)}) async-start(bf16[16,128,512]{2,1,0:T(8,128)(2,1)} %update.6), calls=%async_computation.5 | async-start | bytes 4194304 | tf_op jit(solution)/shard_map/all_to_all | solution.py:551
  178.1 27.6 %collective-permute-start.28 = (bf16[512,1024]{1,0:T(8,128)(2,1)}, bf16[512,1024]{1,0:T(8,128)(2,1)}, u32[]{:S(2)}, u32[]{:S(2)}) collective-permute-start(bf16[512,1024]{1,0:T(8,128)(2,1)} %get-tuple-element.1176), channel_id=1, source_target_pairs={{0,1},{2,3},{5,4},{7,6},{8,9},{10,11},{13,12},{15,14},{16,17},{18,... | collective-permute-start | bytes 3145736 | tf_op jit(solution)/shard_map/ppermute | solution.py:112
  185.2 42.2 %collective-permute-start.27 = (bf16[512,1024]{1,0:T(8,128)(2,1)}, bf16[512,1024]{1,0:T(8,128)(2,1)}, u32[]{:S(2)}, u32[]{:S(2)}) collective-permute-start(bf16[512,1024]{1,0:T(8,128)(2,1)} %get-tuple-element.1178), channel_id=1, source_target_pairs={{0,1},{2,3},{5,4},{7,6},{8,9},{10,11},{13,12},{15,14},{16,17},{18,... | collective-permute-start | bytes 3145736 | tf_op jit(solution)/shard_map/ppermute | solution.py:112
  187.5 51.4 %collective-permute-start.29 = (bf16[512,1024]{1,0:T(8,128)(2,1)}, bf16[512,1024]{1,0:T(8,128)(2,1)}, u32[]{:S(2)}, u32[]{:S(2)}) collective-permute-start(bf16[512,1024]{1,0:T(8,128)(2,1)} %collective-permute-done.20), channel_id=1, source_target_pairs={{0,2},{2,4},{4,6},{1,3},{3,5},{5,7},{8,10},{10,12},{12,14},{9,11},... | collective-permute-start | bytes 3145736 | tf_op jit(solution)/shard_map/ppermute | solution.py:103
  192.1 65.2 %collective-permute-start.30 = (bf16[512,1024]{1,0:T(8,128)(2,1)}, bf16[512,1024]{1,0:T(8,128)(2,1)S(1)}, u32[]{:S(2)}, u32[]{:S(2)}) collective-permute-start(bf16[512,1024]{1,0:T(8,128)(2,1)} %collective-permute-done.26), channel_id=1, source_target_pairs={{0,2},{2,4},{4,6},{1,3},{3,5},{5,7},{8,10},{10,12},{12,14},{9,11},... | collective-permute-start | bytes 3145736 | tf_op jit(solution)/shard_map/ppermute | solution.py:103
  193.5 63.9 %collective-permute-start.31 = (bf16[512,1024]{1,0:T(8,128)(2,1)}, bf16[512,1024]{1,0:T(8,128)(2,1)}, u32[]{:S(2)}, u32[]{:S(2)}) collective-permute-start(bf16[512,1024]{1,0:T(8,128)(2,1)} %collective-permute-done.22), channel_id=1, source_target_pairs={{2,0},{4,2},{6,4},{3,1},{5,3},{7,5},{10,8},{12,10},{14,12},{11,9},... | collective-permute-start | bytes 3145736 | tf_op jit(solution)/shard_map/ppermute | solution.py:104
  205.6 53.6 %collective-permute-start.32 = (bf16[512,1024]{1,0:T(8,128)(2,1)}, bf16[512,1024]{1,0:T(8,128)(2,1)}, u32[]{:S(2)}, u32[]{:S(2)}) collective-permute-start(bf16[512,1024]{1,0:T(8,128)(2,1)} %collective-permute-done.24), channel_id=1, source_target_pairs={{2,0},{4,2},{6,4},{3,1},{5,3},{7,5},{10,8},{12,10},{14,12},{11,9},... | collective-permute-start | bytes 3145736 | tf_op jit(solution)/shard_map/ppermute | solution.py:104
  208.7 346.3 %copy-start.45 = (s32[1024]{0:T(1024)}, s32[1024]{0:T(1024)S(1)}, u32[]{:S(2)}) copy-start(s32[1024]{0:T(1024)S(1)} %pad_clamp_fusion.5) | copy-start | bytes 12292
  209.4 349.4 %copy-start.46 = (s32[1024]{0:T(1024)}, s32[1024]{0:T(1024)S(1)}, u32[]{:S(2)}) copy-start(s32[1024]{0:T(1024)S(1)} %pad_clamp_fusion.4) | copy-start | bytes 12292
  302.3 111.0 %all-to-all-start.3 = ((bf16[16,128,1024]{2,1,0:T(8,128)(2,1)}), bf16[16,128,1024]{2,1,0:T(8,128)(2,1)}, u32[]{:S(2)}, u32[]{:S(2)}) async-start(bf16[16,128,1024]{2,1,0:T(8,128)(2,1)} %update.9), calls=%async_computation.3 | async-start | bytes 8388608 | tf_op jit(solution)/shard_map/all_to_all | solution.py:551
  413.4 98.8 %all-to-all-start.6 = ((bf16[16,128,1024]{2,1,0:T(8,128)(2,1)}), bf16[16,128,1024]{2,1,0:T(8,128)(2,1)}, u32[]{:S(2)}, u32[]{:S(2)}) async-start(bf16[16,128,1024]{2,1,0:T(8,128)(2,1)} %update.10), calls=%async_computation.6 | async-start | bytes 8388608 | tf_op jit(solution)/shard_map/all_to_all | solution.py:551
  420.1 48.0 %collective-permute-start.33 = (bf16[1024,1024]{1,0:T(8,128)(2,1)S(1)}, bf16[1024,1024]{1,0:T(8,128)(2,1)}, u32[]{:S(2)}, u32[]{:S(2)}) collective-permute-start(bf16[1024,1024]{1,0:T(8,128)(2,1)S(1)} %pad_maximum_fusion.1), channel_id=1, source_target_pairs={{0,1},{1,0},{2,3},{3,2},{4,5},{5,4},{6,7},{7,6},{8,9},{9,8},{10,11... | collective-permute-start | bytes 6291464 | tf_op jit(solution)/shard_map/ppermute | solution.py:125
  512.2 53.8 %all-to-all-start.4 = ((bf16[16,128,512]{2,1,0:T(8,128)(2,1)}), bf16[16,128,512]{2,1,0:T(8,128)(2,1)}, u32[]{:S(2)}, u32[]{:S(2)}) async-start(bf16[16,128,512]{2,1,0:T(8,128)(2,1)} %update.8), calls=%async_computation.4 | async-start | bytes 4194304 | tf_op jit(solution)/shard_map/all_to_all | solution.py:551
  567.6 53.9 %all-to-all-start.7 = ((bf16[16,128,512]{2,1,0:T(8,128)(2,1)}), bf16[16,128,512]{2,1,0:T(8,128)(2,1)}, u32[]{:S(2)}, u32[]{:S(2)}) async-start(bf16[16,128,512]{2,1,0:T(8,128)(2,1)} %get-tuple-element.1791), calls=%async_computation.7 | async-start | bytes 4194304 | tf_op jit(solution)/shard_map/all_to_all | solution.py:551
  576.8 70.1 %collective-permute-start.35 = (bf16[6,128,512]{2,1,0:T(8,128)(2,1)}, bf16[6,128,512]{2,1,0:T(8,128)(2,1)}, u32[]{:S(2)}, u32[]{:S(2)}) collective-permute-start(bf16[6,128,512]{2,1,0:T(8,128)(2,1)} %gather_fusion.12), channel_id=1, source_target_pairs={{0,2},{2,0},{4,6},{6,4},{8,10},{10,8},{12,14},{14,12},{16,18},{18,... | collective-permute-start | bytes 2359304 | tf_op jit(solution)/shard_map/ppermute | solution.py:523
  578.5 69.2 %collective-permute-start.41 = (bf16[6,128,512]{2,1,0:T(8,128)(2,1)}, bf16[6,128,512]{2,1,0:T(8,128)(2,1)}, u32[]{:S(2)}, u32[]{:S(2)}) collective-permute-start(bf16[6,128,512]{2,1,0:T(8,128)(2,1)} %gather_fusion.13), channel_id=1, source_target_pairs={{0,8},{2,10},{4,12},{6,14},{8,0},{10,2},{12,4},{14,6},{16,24},{18,... | collective-permute-start | bytes 2359304 | tf_op jit(solution)/shard_map/ppermute | solution.py:523
  578.5 56.8 %collective-permute-start.47 = (bf16[4,128,512]{2,1,0:T(8,128)(2,1)S(1)}, bf16[4,128,512]{2,1,0:T(8,128)(2,1)S(1)}, u32[]{:S(2)}, u32[]{:S(2)}) collective-permute-start(bf16[4,128,512]{2,1,0:T(8,128)(2,1)S(1)} %copy-done.23), channel_id=1, source_target_pairs={{0,16},{2,18},{4,20},{6,22},{8,24},{10,26},{12,28},{14,30},{16,0},... | collective-permute-start | bytes 1572872 | tf_op jit(solution)/shard_map/ppermute | solution.py:523
  580.1 44.0 %collective-permute-start.53 = (bf16[3,128,512]{2,1,0:T(8,128)(2,1)S(1)}, bf16[3,128,512]{2,1,0:T(8,128)(2,1)}, u32[]{:S(2)}, u32[]{:S(2)}) collective-permute-start(bf16[3,128,512]{2,1,0:T(8,128)(2,1)S(1)} %copy-done.24), channel_id=1, source_target_pairs={{0,24},{2,26},{4,28},{6,30},{8,16},{10,18},{12,20},{14,22},{16,8},... | collective-permute-start | bytes 1179656 | tf_op jit(solution)/shard_map/ppermute | solution.py:523
  623.5 11.8 %collective-permute-start.52 = (bf16[3,128,512]{2,1,0:T(8,128)(2,1)}, bf16[3,128,512]{2,1,0:T(8,128)(2,1)}, u32[]{:S(2)}, u32[]{:S(2)}) collective-permute-start(bf16[3,128,512]{2,1,0:T(8,128)(2,1)} %gather_fusion.23), channel_id=1, source_target_pairs={{0,24},{2,26},{4,28},{6,30},{8,16},{10,18},{12,20},{14,22},{16,8},... | collective-permute-start | bytes 1179656 | tf_op jit(solution)/shard_map/ppermute | solution.py:523
  624.1 22.0 %collective-permute-start.46 = (bf16[4,128,512]{2,1,0:T(8,128)(2,1)}, bf16[4,128,512]{2,1,0:T(8,128)(2,1)S(1)}, u32[]{:S(2)}, u32[]{:S(2)}) collective-permute-start(bf16[4,128,512]{2,1,0:T(8,128)(2,1)} %gather_fusion.22), channel_id=1, source_target_pairs={{0,16},{2,18},{4,20},{6,22},{8,24},{10,26},{12,28},{14,30},{16,0},... | collective-permute-start | bytes 1572872 | tf_op jit(solution)/shard_map/ppermute | solution.py:523
  635.3 19.4 %collective-permute-start.34 = (bf16[6,128,512]{2,1,0:T(8,128)(2,1)}, bf16[6,128,512]{2,1,0:T(8,128)(2,1)S(1)}, u32[]{:S(2)}, u32[]{:S(2)}) collective-permute-start(bf16[6,128,512]{2,1,0:T(8,128)(2,1)} %gather_fusion.20), channel_id=1, source_target_pairs={{0,2},{2,0},{4,6},{6,4},{8,10},{10,8},{12,14},{14,12},{16,18},{18,... | collective-permute-start | bytes 2359304 | tf_op jit(solution)/shard_map/ppermute | solution.py:523
  635.3 19.7 %collective-permute-start.40 = (bf16[6,128,512]{2,1,0:T(8,128)(2,1)}, bf16[6,128,512]{2,1,0:T(8,128)(2,1)S(1)}, u32[]{:S(2)}, u32[]{:S(2)}) collective-permute-start(bf16[6,128,512]{2,1,0:T(8,128)(2,1)} %gather_fusion.21), channel_id=1, source_target_pairs={{0,8},{2,10},{4,12},{6,14},{8,0},{10,2},{12,4},{14,6},{16,24},{18,... | collective-permute-start | bytes 2359304 | tf_op jit(solution)/shard_map/ppermute | solution.py:523
  646.1 58.6 %collective-permute-start.48 = (bf16[4,128,1024]{2,1,0:T(8,128)(2,1)}, bf16[4,128,1024]{2,1,0:T(8,128)(2,1)S(1)}, u32[]{:S(2)}, u32[]{:S(2)}) collective-permute-start(bf16[4,128,1024]{2,1,0:T(8,128)(2,1)} %gather_fusion.26), channel_id=1, source_target_pairs={{0,16},{2,18},{4,20},{6,22},{8,24},{10,26},{12,28},{14,30},{16,0},... | collective-permute-start | bytes 3145736 | tf_op jit(solution)/shard_map/ppermute | solution.py:523
  646.9 40.9 %collective-permute-start.54 = (bf16[3,128,1024]{2,1,0:T(8,128)(2,1)}, bf16[3,128,1024]{2,1,0:T(8,128)(2,1)S(1)}, u32[]{:S(2)}, u32[]{:S(2)}) collective-permute-start(bf16[3,128,1024]{2,1,0:T(8,128)(2,1)} %gather_fusion.27), channel_id=1, source_target_pairs={{0,24},{2,26},{4,28},{6,30},{8,16},{10,18},{12,20},{14,22},{16,8},... | collective-permute-start | bytes 2359304 | tf_op jit(solution)/shard_map/ppermute | solution.py:523
  647.7 56.9 %collective-permute-start.55 = (bf16[3,128,1024]{2,1,0:T(8,128)(2,1)}, bf16[3,128,1024]{2,1,0:T(8,128)(2,1)S(1)}, u32[]{:S(2)}, u32[]{:S(2)}) collective-permute-start(bf16[3,128,1024]{2,1,0:T(8,128)(2,1)} %gather_fusion.19), channel_id=1, source_target_pairs={{0,24},{2,26},{4,28},{6,30},{8,16},{10,18},{12,20},{14,22},{16,8},... | collective-permute-start | bytes 2359304 | tf_op jit(solution)/shard_map/ppermute | solution.py:523
  654.7 76.7 %collective-permute-start.36 = (bf16[6,128,1024]{2,1,0:T(8,128)(2,1)}, bf16[6,128,1024]{2,1,0:T(8,128)(2,1)}, u32[]{:S(2)}, u32[]{:S(2)}) collective-permute-start(bf16[6,128,1024]{2,1,0:T(8,128)(2,1)} %gather_fusion.24), channel_id=1, source_target_pairs={{0,2},{2,0},{4,6},{6,4},{8,10},{10,8},{12,14},{14,12},{16,18},{18,... | collective-permute-start | bytes 4718600 | tf_op jit(solution)/shard_map/ppermute | solution.py:523
  655.0 81.2 %collective-permute-start.42 = (bf16[6,128,1024]{2,1,0:T(8,128)(2,1)}, bf16[6,128,1024]{2,1,0:T(8,128)(2,1)}, u32[]{:S(2)}, u32[]{:S(2)}) collective-permute-start(bf16[6,128,1024]{2,1,0:T(8,128)(2,1)} %gather_fusion.25), channel_id=1, source_target_pairs={{0,8},{2,10},{4,12},{6,14},{8,0},{10,2},{12,4},{14,6},{16,24},{18,... | collective-permute-start | bytes 4718600 | tf_op jit(solution)/shard_map/ppermute | solution.py:523
  687.8 67.4 %collective-permute-start.43 = (bf16[6,128,1024]{2,1,0:T(8,128)(2,1)}, bf16[6,128,1024]{2,1,0:T(8,128)(2,1)}, u32[]{:S(2)}, u32[]{:S(2)}) collective-permute-start(bf16[6,128,1024]{2,1,0:T(8,128)(2,1)} %gather_fusion.17), channel_id=1, source_target_pairs={{0,8},{2,10},{4,12},{6,14},{8,0},{10,2},{12,4},{14,6},{16,24},{18,... | collective-permute-start | bytes 4718600 | tf_op jit(solution)/shard_map/ppermute | solution.py:523
  704.7 51.6 %collective-permute-start.37 = (bf16[6,128,1024]{2,1,0:T(8,128)(2,1)}, bf16[6,128,1024]{2,1,0:T(8,128)(2,1)}, u32[]{:S(2)}, u32[]{:S(2)}) collective-permute-start(bf16[6,128,1024]{2,1,0:T(8,128)(2,1)} %gather_fusion.16), channel_id=1, source_target_pairs={{0,2},{2,0},{4,6},{6,4},{8,10},{10,8},{12,14},{14,12},{16,18},{18,... | collective-permute-start | bytes 4718600 | tf_op jit(solution)/shard_map/ppermute | solution.py:523
  705.5 25.9 %collective-permute-start.49 = (bf16[4,128,1024]{2,1,0:T(8,128)(2,1)}, bf16[4,128,1024]{2,1,0:T(8,128)(2,1)}, u32[]{:S(2)}, u32[]{:S(2)}) collective-permute-start(bf16[4,128,1024]{2,1,0:T(8,128)(2,1)} %gather_fusion.18), channel_id=1, source_target_pairs={{0,16},{2,18},{4,20},{6,22},{8,24},{10,26},{12,28},{14,30},{16,0},... | collective-permute-start | bytes 3145736 | tf_op jit(solution)/shard_map/ppermute | solution.py:523
  731.4 24.8 %collective-permute-start.56 = (bf16[3,128,512]{2,1,0:T(8,128)(2,1)}, bf16[3,128,512]{2,1,0:T(8,128)(2,1)}, u32[]{:S(2)}, u32[]{:S(2)}) collective-permute-start(bf16[3,128,512]{2,1,0:T(8,128)(2,1)} %gather_fusion.34), channel_id=1, source_target_pairs={{0,24},{2,26},{4,28},{6,30},{8,16},{10,18},{12,20},{14,22},{16,8},... | collective-permute-start | bytes 1179656 | tf_op jit(solution)/shard_map/ppermute | solution.py:523
  731.4 25.9 %collective-permute-start.57 = (bf16[3,128,512]{2,1,0:T(8,128)(2,1)S(1)}, bf16[3,128,512]{2,1,0:T(8,128)(2,1)}, u32[]{:S(2)}, u32[]{:S(2)}) collective-permute-start(bf16[3,128,512]{2,1,0:T(8,128)(2,1)S(1)} %gather_fusion.35), channel_id=1, source_target_pairs={{0,24},{2,26},{4,28},{6,30},{8,16},{10,18},{12,20},{14,22},{16,8},... | collective-permute-start | bytes 1179656 | tf_op jit(solution)/shard_map/ppermute | solution.py:523
  736.3 26.2 %collective-permute-start.50 = (bf16[4,128,512]{2,1,0:T(8,128)(2,1)}, bf16[4,128,512]{2,1,0:T(8,128)(2,1)}, u32[]{:S(2)}, u32[]{:S(2)}) collective-permute-start(bf16[4,128,512]{2,1,0:T(8,128)(2,1)} %gather_fusion.32), channel_id=1, source_target_pairs={{0,16},{2,18},{4,20},{6,22},{8,24},{10,26},{12,28},{14,30},{16,0},... | collective-permute-start | bytes 1572872 | tf_op jit(solution)/shard_map/ppermute | solution.py:523
  755.2 21.4 %collective-permute-start.38 = (bf16[6,128,512]{2,1,0:T(8,128)(2,1)}, bf16[6,128,512]{2,1,0:T(8,128)(2,1)S(1)}, u32[]{:S(2)}, u32[]{:S(2)}) collective-permute-start(bf16[6,128,512]{2,1,0:T(8,128)(2,1)} %gather_fusion.28), channel_id=1, source_target_pairs={{0,2},{2,0},{4,6},{6,4},{8,10},{10,8},{12,14},{14,12},{16,18},{18,... | collective-permute-start | bytes 2359304 | tf_op jit(solution)/shard_map/ppermute | solution.py:523
  756.2 20.5 %collective-permute-start.44 = (bf16[6,128,512]{2,1,0:T(8,128)(2,1)}, bf16[6,128,512]{2,1,0:T(8,128)(2,1)}, u32[]{:S(2)}, u32[]{:S(2)}) collective-permute-start(bf16[6,128,512]{2,1,0:T(8,128)(2,1)} %gather_fusion.30), channel_id=1, source_target_pairs={{0,8},{2,10},{4,12},{6,14},{8,0},{10,2},{12,4},{14,6},{16,24},{18,... | collective-permute-start | bytes 2359304 | tf_op jit(solution)/shard_map/ppermute | solution.py:523
  756.2 35.5 %collective-permute-start.39 = (bf16[6,128,512]{2,1,0:T(8,128)(2,1)}, bf16[6,128,512]{2,1,0:T(8,128)(2,1)}, u32[]{:S(2)}, u32[]{:S(2)}) collective-permute-start(bf16[6,128,512]{2,1,0:T(8,128)(2,1)} %gather_fusion.29), channel_id=1, source_target_pairs={{0,2},{2,0},{4,6},{6,4},{8,10},{10,8},{12,14},{14,12},{16,18},{18,... | collective-permute-start | bytes 2359304 | tf_op jit(solution)/shard_map/ppermute | solution.py:523
  757.4 34.4 %collective-permute-start.45 = (bf16[6,128,512]{2,1,0:T(8,128)(2,1)}, bf16[6,128,512]{2,1,0:T(8,128)(2,1)}, u32[]{:S(2)}, u32[]{:S(2)}) collective-permute-start(bf16[6,128,512]{2,1,0:T(8,128)(2,1)} %gather_fusion.31), channel_id=1, source_target_pairs={{0,8},{2,10},{4,12},{6,14},{8,0},{10,2},{12,4},{14,6},{16,24},{18,... | collective-permute-start | bytes 2359304 | tf_op jit(solution)/shard_map/ppermute | solution.py:523
  762.5 14.2 %collective-permute-start.51 = (bf16[4,128,512]{2,1,0:T(8,128)(2,1)}, bf16[4,128,512]{2,1,0:T(8,128)(2,1)S(1)}, u32[]{:S(2)}, u32[]{:S(2)}) collective-permute-start(bf16[4,128,512]{2,1,0:T(8,128)(2,1)} %gather_fusion.33), channel_id=1, source_target_pairs={{0,16},{2,18},{4,20},{6,22},{8,24},{10,26},{12,28},{14,30},{16,0},... | collective-permute-start | bytes 1572872 | tf_op jit(solution)/shard_map/ppermute | solution.py:523
  815.5 15.5 %collective-permute-start.58 = (f32[320,512]{1,0:T(8,128)S(1)}, f32[320,512]{1,0:T(8,128)S(1)}, u32[]{:S(2)}, u32[]{:S(2)}) collective-permute-start(f32[320,512]{1,0:T(8,128)S(1)} %constant_dynamic-slice_fusion), channel_id=1, source_target_pairs={{0,1},{1,0},{2,3},{3,2},{4,5},{5,4},{6,7},{7,6},{8,9},{9,8},{10,11... | collective-permute-start | bytes 1966088 | tf_op jit(solution)/shard_map/ppermute | solution.py:668
  (52 other events, 1745.5 us)
